TPU v7x, 32 devices: a whole 2x2x4 slice. The times are simulated.
32 devices in a mesh: section: 4 (over z), space: 8 (over y, x, core).
Axes of the slice: x: 2, y: 2, z: 4, core: 2. Of those that a mesh axis runs over, the one named last changes fastest.
Arguments:
- features: bfloat16 [1, 32, 128, 320], P(None, 'space'), may hold values from -30 to 30
- section_packs: bfloat16 [4, 11520, 640], P('section', None, 'space'), may hold values from -6 to 6
Outputs:
- output: bfloat16 [1, 32, 128, 320], P(None, 'space', 'section')
All inputs are finite; a program needn't handle non-finite values.
Results may differ from a plain program's by a relative error of at most 0.009.
Values may be sent and summed in bfloat16 or wider, within the bound.
No kernel may reach another device: no remote copies, remote signals or barrier semaphores. Data moves between devices by JAX's collectives and lax.ppermute only.
A program may use at most 128 MiB of HBM per device.

v0:
```python
import math

import jax
import jax.numpy as jnp
from jax import lax
from jax.experimental import pallas as pl
from jax.experimental.pallas import tpu as pltpu
from jax.sharding import PartitionSpec as P


GROUPS = 32
EPSILON = 1e-05
TAIL = 16
BF16 = jnp.bfloat16
F32 = jnp.float32


def row_stack(rows, count, width):
    ids = lax.broadcasted_iota(jnp.int32, (count, width), 0)
    total = jnp.zeros((count, width), F32)
    for place, row in enumerate(rows):
        total = jnp.where(ids == place, row, total)
    return total


def bf16_terms(row):
    high = row.astype(BF16).astype(F32)
    rest = row - high
    mid = rest.astype(BF16).astype(F32)
    return [high, mid, (rest - mid).astype(BF16).astype(F32)]


def moments_of(value):
    return [
        jnp.sum(value, axis=0, keepdims=True),
        jnp.sum(value * value, axis=0, keepdims=True),
    ]


def group_terms(sums, count):
    width = sums.shape[1]
    size = width // GROUPS
    terms = row_stack(bf16_terms(sums[0:1]) + bf16_terms(sums[1:2]), 16, width).astype(BF16)
    left = lax.broadcasted_iota(jnp.int32, (width, width), 0) // size
    right = lax.broadcasted_iota(jnp.int32, (width, width), 1) // size
    together = jnp.where(left == right, 1.0, 0.0).astype(BF16)
    summed = jnp.dot(terms, together, preferred_element_type=F32) * (1.0 / (count * size))
    mean = summed[0:1] + summed[1:2] + summed[2:3]
    square = summed[3:4] + summed[4:5] + summed[5:6]
    variance = jnp.maximum(square - mean * mean, 0.0)
    return mean, lax.rsqrt(variance + EPSILON)


def silu(z):
    half = 0.5 * z
    return half + half * jnp.tanh(half)


def parity_matrix(width):
    source = lax.broadcasted_iota(jnp.int32, (width, width), 0)
    target = lax.broadcasted_iota(jnp.int32, (width, width), 1)
    half = width // 2
    wanted = jnp.where(target < half, 2 * target, 2 * (target - half) + 1)
    return jnp.where(source == wanted, 1.0, 0.0).astype(BF16)


def shifted(value, step):
    rows = value.shape[0]
    ids = lax.broadcasted_iota(jnp.int32, value.shape, 0)
    if step == 1:
        return jnp.where(ids == 0, 0.0, pltpu.roll(value, 1, 0))
    return jnp.where(ids == rows - 1, 0.0, pltpu.roll(value, rows - 1, 0))


class Shape:
    def __init__(self, features, n):
        self.rows = features.shape[1]
        self.cols = features.shape[2]
        self.half = self.cols // 2
        self.narrow = features.shape[3]
        self.wide = 2 * self.narrow
        self.m = min(n, 8)
        self.cols_of = self.wide // self.m
        self.blk = 3 * self.narrow // 2
        self.lanes = -(-self.blk // 128) * 128
        self.fine_count = self.rows * n * self.cols
        self.coarse_count = self.fine_count // 4


def emit(flags, out_ref, outer_ref, inner_ref, stats_ref, keep, rows, width, sums):
    channels = out_ref.shape[1]
    core0 = flags[0] == 0
    tail = row_stack([term for row in sums for term in bf16_terms(row)], TAIL, channels).astype(BF16)
    out_ref[rows * width :, :] = tail
    stats_ref[...] = row_stack(sums, 8, channels)
    size = keep * width
    first = out_ref[0:size, :].astype(F32)
    last = out_ref[(rows - keep) * width : rows * width, :].astype(F32)
    outer_ref[0:size, :] = jnp.where(core0, first, last).astype(BF16)
    outer_ref[size:, :] = tail
    inner_ref[...] = jnp.where(core0, last, first).astype(BF16)


def ext_row(index, block_ref, outer_ref, inner_ref, flags, rows, halo, width):
    if index < halo:
        span = slice(index * width, (index + 1) * width)
        pick = jnp.where(flags[0] == 0, outer_ref[span, :].astype(F32), inner_ref[span, :].astype(F32))
        return pick, flags[1] != 0
    index -= halo
    if index < rows:
        return block_ref[index * width : (index + 1) * width, :].astype(F32), None
    index -= rows
    span = slice(index * width, (index + 1) * width)
    pick = jnp.where(flags[0] == 0, inner_ref[span, :].astype(F32), outer_ref[span, :].astype(F32))
    return pick, flags[2] != 0


def masked(value, outside):
    if outside is None:
        return value
    return jnp.where(outside, 0.0, value)


class Weights:
    def __init__(self, shape, bounds, start, c_in, c_out):
        self.shape = shape
        self.c_in = c_in
        self.c_out = c_out
        self.split = c_out != shape.wide
        self.blocks = 3 * c_in * c_out // shape.wide // shape.blk
        self.start = start // shape.blk
        self.bounds = bounds
        self.depth = self.blocks * shape.lanes
        self.width = (2 if self.split else 1) * self.depth

    def stacks(self, refs):
        refs = list(refs)
        return {low: [refs.pop(0) for _ in owners] for low, _, owners in self.bounds}

    def copies(self, flags, stack_refs, buffer, sems):
        made = []
        lanes = self.shape.lanes
        for dy in range(3):
            mine = []
            begin = self.start + dy * self.blocks
            for low, high, owners in self.bounds:
                a, b = max(begin, low), min(begin + self.blocks, high)
                if a >= b:
                    continue
                for ref, owner in zip(stack_refs[low], owners, strict=True):
                    mine.append(
                        pltpu.make_async_copy(
                            ref.at[:, (a - low) * lanes : (b - low) * lanes],
                            self.slot(buffer.at[dy], owner(flags), a - begin, b - begin),
                            sems.at[dy],
                        )
                    )
            made.append(mine)
        return made

    def slot(self, target, owner, first, last):
        lanes = self.shape.lanes
        if not self.split:
            return target.at[owner, :, first * lanes : last * lanes]
        half = self.shape.m // 2
        shift = pl.multiple_of(owner // half * self.depth, lanes)
        return target.at[owner % half, :, pl.ds(first * lanes + shift, (last - first) * lanes)]

    def product(self, left, buffer, dy):
        right = buffer[dy].reshape(self.c_out, self.width)
        return lax.dot_general(left, right, (((1,), (1,)), ((), ())), preferred_element_type=F32)

    def put(self, image, row, place, tap, value, first=0, channels=None):
        shape = self.shape
        size = value.shape[0]
        half = self.c_in // 2
        runs = []
        if self.split:
            c = value.shape[1] // 2
            runs = [(odd, tap * half + first // 2, odd * c, c) for odd in range(2)]
        else:
            runs = [(0, tap * self.c_in + first, 0, value.shape[1])]
        for odd, index, at, left in runs:
            while left > 0:
                step = min(left, shape.blk - index % shape.blk)
                lane = odd * self.depth + index // shape.blk * shape.lanes + index % shape.blk
                image[row, place : place + size, lane : lane + step] = value[:, at : at + step]
                index, at, left = index + step, at + step, left - step

    def clear(self, image):
        shape = self.shape
        for block in range(self.width // shape.lanes):
            begin = block * shape.lanes + shape.blk
            end = (block + 1) * shape.lanes
            image[:, :, begin:end] = jnp.zeros((image.shape[0], image.shape[1], end - begin), BF16)


def fine_columns(store, row, even, odd):
    half = even.shape[0]
    store(row, 0, half, 0, shifted(odd, 1))
    store(row, 0, half, 1, even)
    store(row, 0, half, 2, odd)
    store(row, half, half, 0, even)
    store(row, half, half, 1, odd)
    store(row, half, half, 2, shifted(even, -1))


def run_conv(weights, buffer, image, acc, sems, rows, width, begin=lambda dy: dy):
    acc[...] = jnp.zeros(acc.shape, F32)

    def step(dy, carry):
        pltpu.make_async_copy(buffer.at[dy], buffer.at[dy], sems.at[dy]).wait()
        left = image[pl.ds(begin(dy), rows)].reshape(rows * width, weights.width)
        acc[...] += weights.product(left, buffer, dy)
        return carry

    lax.fori_loop(0, 3, step, 0)


def scratch_of(weights, image_rows, out_rows, width, extra=()):
    return [
        pltpu.VMEM((3, weights.c_out // weights.shape.cols_of, weights.shape.cols_of, weights.width), BF16),
        pltpu.VMEM((image_rows, width, weights.width), BF16),
        pltpu.VMEM((out_rows * width, weights.c_out), F32),
        pltpu.SemaphoreType.DMA((3,)),
    ] + list(extra)


def call(body, n_smem, n_vmem, n_any, outs, scratch, flops, limit=60 * 1024 * 1024):
    specs = (
        [pl.BlockSpec(memory_space=pltpu.SMEM)] * n_smem
        + [pl.BlockSpec(memory_space=pltpu.VMEM)] * n_vmem
        + [pl.BlockSpec(memory_space=pltpu.HBM)] * n_any
    )
    return pl.pallas_call(
        body,
        out_shape=[jax.ShapeDtypeStruct(s, d) for s, d in outs],
        in_specs=specs,
        out_specs=[pl.BlockSpec(memory_space=pltpu.VMEM)] * len(outs),
        scratch_shapes=scratch,
        compiler_params=pltpu.CompilerParams(vmem_limit_bytes=limit),
        cost_estimate=pl.CostEstimate(flops=flops, bytes_accessed=4_000_000, transcendentals=0),
    )


def message_outs(rows, width, channels, keep):
    return [
        ((rows * width + TAIL, channels), BF16),
        ((keep * width + TAIL, channels), BF16),
        ((keep * width, channels), BF16),
        ((8, channels), F32),
    ]


def prepare(shape, flags, x, keep):
    rows, width, c = shape.rows, shape.cols, shape.narrow

    def body(flags, x_ref, out_ref, outer_ref, inner_ref, stats_ref):
        out_ref[0 : rows * width, :] = x_ref[...]
        sums = moments_of(x_ref[...].astype(F32))
        emit(flags, out_ref, outer_ref, inner_ref, stats_ref, keep, rows, width, sums)

    return call(body, 1, 1, 0, message_outs(rows, width, c, keep), [], 1000)(flags, x)


def fine_conv(shape, flags, weights, pieces, got, halo, out_halo, keep, residual=None):
    rows, width, half, c = shape.rows, shape.cols, shape.half, shape.narrow
    out_rows = rows + 2 * out_halo
    image_rows = out_rows + 2
    n_pieces = len(pieces)
    extra = 0 if residual is None else 3

    def body(flags, block, outer, inner, sa, sb, *rest):
        res = rest[:extra]
        piece_refs = rest[extra : extra + n_pieces]
        rest = rest[extra + n_pieces :]
        outs = rest[:-4]
        buffer, image, acc, sems = rest[-4:]
        copies = weights.copies(flags, weights.stacks(piece_refs), buffer, sems)
        for mine in copies:
            for copy in mine:
                copy.start()
        weights.clear(image)
        mean, inv = group_terms(sa[...] + sb[...], shape.fine_count)
        mix = parity_matrix(c)

        def store(row, place, size, tap, value):
            weights.put(image, row, place, tap, value.astype(BF16))

        for row in range(image_rows):
            value, outside = ext_row(row + halo - out_halo - 1, block, outer, inner, flags, rows, halo, width)
            value = masked(silu((value - mean) * inv), outside).astype(BF16)
            value = jnp.dot(value, mix, preferred_element_type=F32)
            fine_columns(store, row, value[:half], value[half:])
        run_conv(weights, buffer, image, acc, sems, out_rows, width)
        scale = 1.0 / math.sqrt(9 * c)
        if residual is None:
            out_ref, outer_ref, inner_ref, stats_ref = outs
            value = (acc[...] * scale).astype(BF16)
            out_ref[0 : rows * width, :] = value
            emit(flags, out_ref, outer_ref, inner_ref, stats_ref, keep, rows, width, moments_of(value.astype(F32)))
        else:
            (out_ref,) = outs
            for row in range(out_rows):
                own, _ = ext_row(row, res[0], res[1], res[2], flags, rows, out_halo, width)
                span = slice(row * width, (row + 1) * width)
                out_ref[span, :] = (own + acc[span, :] * scale).astype(BF16)

    outs = message_outs(rows, width, c, keep) if residual is None else [((out_rows * width, c), BF16)]
    args = (flags,) + tuple(got) + (() if residual is None else tuple(residual)) + tuple(pieces)
    flops = 2 * out_rows * width * 9 * c * c
    return call(body, 1, 5 + extra, n_pieces, outs, scratch_of(weights, image_rows, out_rows, width), flops)(*args)


def down_conv(shape, flags, weights, pieces, skip, keep):
    rows, width, half, c = shape.rows, shape.cols, shape.half, shape.narrow
    out_rows = rows // 2

    def body(flags, skip_ref, *rest):
        piece_refs = rest[: len(pieces)]
        outs = rest[len(pieces) : -4]
        buffer, image, acc, sems = rest[-4:]
        copies = weights.copies(flags, weights.stacks(piece_refs), buffer, sems)
        for mine in copies:
            for copy in mine:
                copy.start()
        weights.clear(image)
        for row in range(rows + 1):
            value = skip_ref[row * width : (row + 1) * width, :].astype(F32)
            if row == 0:
                value = masked(value, flags[1] != 0)
            even, odd = value[:half], value[half:]
            place = (row % 2) * (out_rows + 1) + row // 2
            weights.put(image, place, 0, 0, shifted(odd, 1).astype(BF16))
            weights.put(image, place, 0, 1, even.astype(BF16))
            weights.put(image, place, 0, 2, odd.astype(BF16))

        def begin(dy):
            return jnp.where(dy == 1, out_rows + 1, dy // 2)

        run_conv(weights, buffer, image, acc, sems, out_rows, half, begin)
        out_ref, outer_ref, inner_ref, stats_ref = outs
        value = (acc[...] * (1.0 / math.sqrt(9 * c))).astype(BF16)
        out_ref[0 : out_rows * half, :] = value
        emit(flags, out_ref, outer_ref, inner_ref, stats_ref, keep, out_rows, half, moments_of(value.astype(F32)))

    scratch = scratch_of(weights, 2 * (out_rows + 1), out_rows, half)
    outs = message_outs(out_rows, half, shape.wide, keep)
    return call(body, 1, 1, len(pieces), outs, scratch, 2 * out_rows * half * 9 * c * shape.wide)(flags, skip, *pieces)


def coarse_conv(shape, flags, weights, pieces, got, keep, residual=None):
    rows, width, c = shape.rows // 2, shape.half, shape.wide
    extra = 0 if residual is None else 1

    def body(flags, block, outer, inner, sa, sb, *rest):
        res = rest[:extra]
        piece_refs = rest[extra : extra + len(pieces)]
        outs = rest[extra + len(pieces) : -4]
        buffer, image, acc, sems = rest[-4:]
        copies = weights.copies(flags, weights.stacks(piece_refs), buffer, sems)
        for mine in copies:
            for copy in mine:
                copy.start()
        weights.clear(image)
        mean, inv = group_terms(sa[...] + sb[...], shape.coarse_count)
        for row in range(rows + 2):
            value, outside = ext_row(row, block, outer, inner, flags, rows, 1, width)
            value = masked(silu((value - mean) * inv), outside)
            weights.put(image, row, 0, 0, shifted(value, 1).astype(BF16))
            weights.put(image, row, 0, 1, value.astype(BF16))
            weights.put(image, row, 0, 2, shifted(value, -1).astype(BF16))
        run_conv(weights, buffer, image, acc, sems, rows, width)
        out_ref, outer_ref, inner_ref, stats_ref = outs
        value = acc[...] * (1.0 / math.sqrt(9 * c))
        if residual is not None:
            value = res[0][0 : rows * width, :].astype(F32) + value
        value = value.astype(BF16)
        out_ref[0 : rows * width, :] = value
        emit(flags, out_ref, outer_ref, inner_ref, stats_ref, keep, rows, width, moments_of(value.astype(F32)))

    args = (flags,) + tuple(got) + (() if residual is None else (residual,)) + tuple(pieces)
    outs = message_outs(rows, width, c, keep)
    flops = 2 * rows * width * 9 * c * c
    return call(body, 1, 5 + extra, len(pieces), outs, scratch_of(weights, rows + 2, rows, width), flops)(*args)


def up_conv(shape, flags, weights, pieces, got, skip, keep):
    rows, width, half = shape.rows, shape.cols, shape.half
    c, c_out = shape.wide, shape.narrow

    def body(flags, block, outer, inner, skip_ref, *rest):
        piece_refs = rest[: len(pieces)]
        outs = rest[len(pieces) : -4]
        buffer, image, acc, sems = rest[-4:]
        copies = weights.copies(flags, weights.stacks(piece_refs), buffer, sems)
        for mine in copies:
            for copy in mine:
                copy.start()
        weights.clear(image)
        mix = parity_matrix(c)
        for row in range(rows // 2 + 2):
            value, outside = ext_row(row, block, outer, inner, flags, rows // 2, 1, half)
            value = masked(value, outside).astype(BF16)
            value = jnp.dot(value, mix, preferred_element_type=F32)
            before, after = shifted(value, 1).astype(BF16), shifted(value, -1).astype(BF16)
            value = value.astype(BF16)
            for fine in (2 * row - 1, 2 * row):
                if 0 <= fine < rows + 2:
                    for tap, (even, odd) in enumerate(((before, value), (value, value), (value, after))):
                        weights.put(image, fine, 0, tap, even)
                        weights.put(image, fine, half, tap, odd)
        run_conv(weights, buffer, image, acc, sems, rows, width)
        out_ref, outer_ref, inner_ref, stats_ref = outs
        value = (acc[...] * (1.0 / math.sqrt(9 * c))).astype(BF16)
        out_ref[0 : rows * width, :] = value
        own = skip_ref[width : (rows + 1) * width, :].astype(F32)
        sums = moments_of(value.astype(F32)) + moments_of(own)
        emit(flags, out_ref, outer_ref, inner_ref, stats_ref, keep, rows, width, sums)

    outs = message_outs(rows, width, c_out, keep)
    flops = 2 * rows * width * 9 * c * c_out
    scratch = scratch_of(weights, rows + 2, rows, width)
    return call(body, 1, 4, len(pieces), outs, scratch, flops)(flags, *got, skip, *pieces)


def join_conv(shape, flags, weights, pieces, got, skip, keep):
    rows, width, half, c = shape.rows, shape.cols, shape.half, shape.narrow

    def body(flags, block, outer, inner, sa, sb, skip_ref, *rest):
        piece_refs = rest[: len(pieces)]
        outs = rest[len(pieces) : -4]
        buffer, image, acc, sems = rest[-4:]
        copies = weights.copies(flags, weights.stacks(piece_refs), buffer, sems)
        for mine in copies:
            for copy in mine:
                copy.start()
        weights.clear(image)
        mix = parity_matrix(c)
        for part in range(2):
            sums = sa[...] + sb[...]
            mean, inv = pair_terms(sums[2 * part : 2 * part + 2], shape.fine_count)

            def store(row, place, size, tap, value, part=part):
                weights.put(image, row, place, tap, value.astype(BF16), first=part * c)

            for row in range(rows + 2):
                if part == 0:
                    value, outside = ext_row(row, block, outer, inner, flags, rows, 1, width)
                else:
                    value = skip_ref[row * width : (row + 1) * width, :].astype(F32)
                    outside = flags[1] != 0 if row == 0 else flags[2] != 0 if row == rows + 1 else None
                value = masked(silu((value - mean) * inv), outside).astype(BF16)
                value = jnp.dot(value, mix, preferred_element_type=F32)
                fine_columns(store, row, value[:half], value[half:])
        run_conv(weights, buffer, image, acc, sems, rows, width)
        out_ref, outer_ref, inner_ref, stats_ref = outs
        value = (acc[...] * (1.0 / math.sqrt(18 * c))).astype(BF16)
        out_ref[0 : rows * width, :] = value
        emit(flags, out_ref, outer_ref, inner_ref, stats_ref, keep, rows, width, moments_of(value.astype(F32)))

    outs = message_outs(rows, width, c, keep)
    flops = 2 * rows * width * 18 * c * c
    scratch = scratch_of(weights, rows + 2, rows, width)
    return call(body, 1, 6, len(pieces), outs, scratch, flops)(flags, *got, skip, *pieces)


def pair_terms(sums, count):
    width = sums.shape[1]
    size = 2 * width // GROUPS
    terms = row_stack(bf16_terms(sums[0:1]) + bf16_terms(sums[1:2]), 16, width).astype(BF16)
    left = lax.broadcasted_iota(jnp.int32, (width, width), 0) // size
    right = lax.broadcasted_iota(jnp.int32, (width, width), 1) // size
    together = jnp.where(left == right, 1.0, 0.0).astype(BF16)
    summed = jnp.dot(terms, together, preferred_element_type=F32) * (1.0 / (count * size))
    mean = summed[0:1] + summed[1:2] + summed[2:3]
    square = summed[3:4] + summed[4:5] + summed[5:6]
    variance = jnp.maximum(square - mean * mean, 0.0)
    return mean, lax.rsqrt(variance + EPSILON)


def last_conv(shape, flags, weights, pieces, got, u, skip, j_start, n_quarters):
    rows, width, half, c = shape.rows, shape.cols, shape.half, shape.narrow
    quarter = half // n_quarters
    j_block = j_start // shape.blk

    def body(flags, block, outer, inner, sa, sb, u_ref, skip_ref, *rest):
        piece_refs = rest[: len(pieces)]
        outs = rest[len(pieces) : -6]
        buffer, image, acc, sems, jbuf, jsem = rest[-6:]
        copies = weights.copies(flags, weights.stacks(piece_refs), buffer, sems)
        for mine in copies:
            for copy in mine:
                copy.start()
        weights.clear(image)
        for low, high, owners in weights.bounds:
            if low <= j_block < high:
                for ref, owner in zip(weights.stacks(piece_refs)[low], owners, strict=True):
                    pltpu.make_async_copy(
                        ref.at[:, (j_block - low) * shape.lanes : (j_block - low + 1) * shape.lanes],
                        jbuf.at[owner(flags)],
                        jsem,
                    ).start()
        mean, inv = group_terms(sa[...] + sb[...], shape.fine_count)
        mix = parity_matrix(c)

        def store(row, place, size, tap, value):
            weights.put(image, row, place, tap, value.astype(BF16))

        for row in range(rows + 2):
            value, outside = ext_row(row, block, outer, inner, flags, rows, 1, width)
            value = masked(silu((value - mean) * inv), outside).astype(BF16)
            value = jnp.dot(value, mix, preferred_element_type=F32)
            fine_columns(store, row, value[:half], value[half:])
        run_conv(weights, buffer, image, acc, sems, rows, width)
        pltpu.make_async_copy(jbuf, jbuf, jsem).wait()
        right = jbuf[...].reshape(2 * c, shape.lanes)
        left = [u_ref[0 : rows * width, :], skip_ref[width : (rows + 1) * width, :]]
        left = [jnp.dot(part, mix, preferred_element_type=F32).astype(BF16) for part in left]
        made = jnp.zeros((rows * width, c), F32)
        for odd in range(2):
            mine = jnp.concatenate(
                [part[:, odd * (c // 2) : (odd + 1) * (c // 2)] for part in left]
                + [jnp.zeros((rows * width, shape.lanes - c), BF16)],
                axis=1,
            )
            made += lax.dot_general(
                mine, right[odd * c : (odd + 1) * c], (((1,), (1,)), ((), ())), preferred_element_type=F32
            )
        value = made * (1.0 / math.sqrt(2 * c)) + acc[...] * (1.0 / math.sqrt(9 * c))
        value = value.reshape(2 * rows, half, c).astype(BF16)
        for q, out in enumerate(outs):
            out[...] = value[:, q * quarter : (q + 1) * quarter, :]

    outs = [((2 * rows, quarter, c), BF16)] * n_quarters
    flops = 2 * rows * width * 11 * c * c
    extra = [pltpu.VMEM((shape.m, shape.cols_of, shape.lanes), BF16), pltpu.SemaphoreType.DMA(())]
    scratch = scratch_of(weights, rows + 2, rows, width, extra)
    return call(body, 1, 7, len(pieces), outs, scratch, flops)(flags, *got, u, skip, *pieces)


def pack_blocks(shape, pack, bounds):
    columns = pack.shape[0]
    first = bounds[0][0] * shape.blk // 128 * 128
    last = min(-(-bounds[-1][1] * shape.blk // 128) * 128, pack.shape[1])

    def body(pack_ref, *rest):
        outs, (rows, sem) = rest[:-2], rest[-2:]
        copy = pltpu.make_async_copy(pack_ref.at[:, first:last], rows, sem)
        copy.start()
        copy.wait()
        for (low, high), out_ref in zip(bounds, outs, strict=True):
            for block in range(high - low):
                begin, end = block * shape.lanes, (block + 1) * shape.lanes
                at = (low + block) * shape.blk - first
                out_ref[:, begin : begin + shape.blk] = rows[:, at : at + shape.blk]
                out_ref[:, begin + shape.blk : end] = jnp.zeros((columns, shape.lanes - shape.blk), BF16)

    scratch = [pltpu.VMEM((columns, last - first), BF16), pltpu.SemaphoreType.DMA(())]
    outs = [((columns, (high - low) * shape.lanes), BF16) for low, high in bounds]
    return call(body, 0, 0, 1, outs, scratch, 1000)(pack)


def shards(n, n_section, features, section_packs):
    section_id = lax.axis_index("section")
    w = lax.axis_index("space")
    shape = Shape(features, n)
    q_rows = shape.narrow * shape.narrow // shape.wide
    pack = section_packs[0]
    flags = jnp.stack([w % 2, (w == 0).astype(jnp.int32), (w == n - 1).astype(jnp.int32), section_id, w]).astype(jnp.int32)

    total = pack.shape[0] // shape.blk
    cuts = [0, 9 * q_rows // shape.blk, 18 * q_rows // shape.blk, 36 * q_rows // shape.blk, total]
    bounds = list(zip(cuts[:-1], cuts[1:], strict=True))

    def permute(value, source, target, move):
        other = {source: target, target: source}
        pairs = [
            (s * n + i, other[s] * n + move(i) if s in other else s * n + i) for s in range(n_section) for i in range(n)
        ]
        return lax.ppermute(value, ("section", "space"), pairs)

    def within(value, move):
        pairs = [(s * n + i, s * n + move(i)) for s in range(n_section) for i in range(n)]
        return lax.ppermute(value, ("section", "space"), pairs)

    def to_outer(i):
        return (i + 1) % n if i % 2 else (i - 1) % n

    def ahead(i):
        return (i - 2) % n if i % 2 else (i + 2) % n

    def across(i):
        return (i + 4) % n

    def partner(i):
        return i ^ 1

    def sums_of(tail):
        tail = tail[: TAIL // 4 * 3].astype(F32).reshape(-1, 3, tail.shape[1]).sum(1)
        return jnp.concatenate([tail, jnp.zeros((8 - tail.shape[0], tail.shape[1]), F32)], 0)

    def exchange(made, source, target, with_stats=True):
        block, outer, inner, own = made
        if source != target:
            block = permute(block, source, target, lambda i: i)
            rows, size = block.shape[0] - TAIL, inner.shape[0]
            top, bottom, tail = block[:size], block[rows - size : rows], block[rows:]
            outer = jnp.concatenate([jnp.where(flags[0] == 0, top, bottom), tail], 0)
            inner = jnp.where(flags[0] == 0, bottom, top)
            own = sums_of(tail)
        stats = own
        outer = permute(outer, target, target, to_outer)
        inner = permute(inner, target, target, partner)
        if not with_stats:
            return block, outer, inner
        if n == 8:
            b = permute(stats, target, target, ahead)
            c = permute(stats, target, target, across)
            mine = own + sums_of(outer[-TAIL:]) + b + c
            other = permute(mine, target, target, partner)
        else:
            mine = lax.psum(own, "space")
            other = jnp.zeros_like(mine)
        return block, outer, inner, mine, other

    def after(value, *deps):
        return lax.optimization_barrier((value,) + deps)[0]

    pieces = {}
    packed = []
    if n == 8:
        packed = pack_blocks(shape, pack.T, bounds[:1])

    def send(number, *deps):
        low, high = bounds[number]
        if n == 8:
            got = [after(packed[number], *deps)]
            for k in range(1, 4):
                got.append(within(got[0], lambda i, k=k: i ^ (2 * k)))
            return got
        got = lax.all_gather(pack[low * shape.blk : high * shape.blk], "space")
        got = got.reshape(shape.m, n // shape.m, high - low, shape.blk, -1).transpose(0, 1, 4, 2, 3)
        got = got.reshape(shape.m, shape.cols_of, high - low, shape.blk)
        got = jnp.pad(got, ((0, 0), (0, 0), (0, 0), (0, shape.lanes - shape.blk)))
        return list(got.reshape(shape.m, shape.cols_of, -1))

    def finish(number, got, *deps):
        if n == 8:
            got = after(got, *deps)
            shared = [within(part, partner) for part in got]
            near = [lambda flags, j=j: ((flags[4] // 2) ^ j) * 2 + flags[0] for j in range(4)]
            far = [lambda flags, j=j: ((flags[4] // 2) ^ j) * 2 + 1 - flags[0] for j in range(4)]
            pieces[number] = (list(got) + shared, near + far)
        else:
            pieces[number] = (got, [lambda flags, j=j: j for j in range(shape.m)])

    def weights(start, c_in, c_out):
        first = start // shape.blk
        end = (start + 9 * c_in * c_out // shape.wide) // shape.blk
        used = [i for i, (a, b) in enumerate(bounds) if a < end and b > first]
        made = Weights(shape, [bounds[i] + (pieces[i][1],) for i in used], start, c_in, c_out)
        return made, [stack for i in used for stack in pieces[i][0]]

    narrow, wide = shape.narrow, shape.wide
    x = features[0].reshape(shape.rows, shape.half, 2, narrow).transpose(0, 2, 1, 3).reshape(-1, narrow)
    ready = prepare(shape, flags, x, 1)
    sent = send(0, ready[3])
    if n == 8:
        packed += pack_blocks(shape, after(pack.T, sent[0]), bounds[1:])
    first = exchange(ready, 0, 0)
    finish(0, sent, first[3])
    sent = send(1, sent)
    first = (after(first[0], sent[0]),) + first[1:]
    hidden = fine_conv(shape, flags, *weights(0, narrow, narrow), first, 1, 0, 2)
    second = exchange(hidden, 0, 0)
    finish(1, sent, second[3])
    sent = send(2, sent, second[3])
    second = (after(second[0], sent[0]),) + second[1:]
    (skip,) = fine_conv(shape, flags, *weights(9 * q_rows, narrow, narrow), second, 2, 1, 0, residual=first[:3])
    finish(2, sent, skip)
    sent = send(3, sent)
    skip = after(skip, sent[0])
    coarse = down_conv(shape, flags, *weights(18 * q_rows, narrow, wide), skip, 1)
    for section in (1, 2):
        got = exchange(coarse, section - 1, section)
        if section == 1:
            skip, got = lax.optimization_barrier((skip, got))
            skip = permute(skip, 0, n_section - 1, lambda i: i)
        hidden = coarse_conv(shape, flags, *weights(0, wide, wide), got, 1)
        if section == 1:
            finish(3, sent, hidden[3])
            hidden, skip = lax.optimization_barrier((hidden, skip))
        then = exchange(hidden, section, section)
        coarse = coarse_conv(shape, flags, *weights(36 * q_rows, wide, wide), then, 1, residual=got[0])
    got = exchange(coarse, 2, 3, with_stats=False)
    up = up_conv(shape, flags, *weights(0, wide, narrow), got, skip, 1)
    got = exchange(up, 3, 3)
    hidden = join_conv(shape, flags, *weights(18 * q_rows, wide, narrow), got, skip, 1)
    then = exchange(hidden, 3, 3)
    outs = last_conv(shape, flags, *weights(36 * q_rows, narrow, narrow), then, got[0], skip, 45 * q_rows, n_section)
    result = outs[3]
    for target in range(3):
        result = jnp.where(section_id == target, permute(outs[target], 3, target, lambda i: i), result)
    quarter = shape.half // n_section
    result = result.reshape(shape.rows, 2, quarter, narrow).transpose(0, 2, 1, 3)
    return result.reshape(1, shape.rows, 2 * quarter, narrow)


def solution(mesh):
    n, n_section = mesh.shape["space"], mesh.shape["section"]

    def body(features, section_packs):
        return shards(n, n_section, features, section_packs)

    return jax.shard_map(
        body,
        mesh=mesh,
        in_specs=(P(None, "space", None, None), P("section", None, "space")),
        out_specs=P(None, "space", "section", None),
        check_vma=False,
    )
```

profile of v0, /device:TPU:0, one launch (start us, length us, event | category | flops | bytes accessed | tf_op | source)
XLA Modules:
  0.0 355.2 jit_solution(11953273552610305268)
XLA Ops:
  2.7 2.1 shard_map.28
  4.8 5.4 %collective-permute-start.3 = (bf16[144,320]{1,0:T(8,128)(2,1)}, bf16[144,320]{1,0:T(8,128)(2,1)S(1)}, u32[]{:S(2)}, u32[]{:S(2)}) collective-permute-start(bf16[144,320]{1,0:T(8,128)(2,1)} %get-tuple-element.81), channel_id=1, source_target_pairs={{0,7},{1,2},{2,1},{3,4},{4,3},{5,6},{6,5},{7,0},{8,8},{9,9},{10,10... | collective-permute-start | bytes 276488 | tf_op jit(solution)/shard_map/ppermute | solution.py:581
  10.2 1.8 shard_map.29.rest_0_
  13.2 2.4 collective-permute-start.2
  15.5 2.4 collective-permute-start.6
  18.0 2.5 collective-permute-start.5
  20.6 6.1 %collective-permute-done.6 = f32[8,320]{1,0:T(8,128)S(1)} collective-permute-done((f32[8,320]{1,0:T(8,128)S(1)}, f32[8,320]{1,0:T(8,128)S(1)}, u32[]{:S(2)}, u32[]{:S(2)}) %collective-permute-start.6) | collective-permute-done | bytes 10272 | tf_op jit(solution)/shard_map/ppermute | solution.py:581
  27.9 2.0 collective-permute-start.4
  31.1 2.0 collective-permute-start.7
  33.1 3.0 shard_map.30
  37.8 7.0 %shard_map.31 = (bf16[528,320]{1,0:T(8,128)(2,1)}, bf16[272,320]{1,0:T(8,128)(2,1)}, bf16[256,320]{1,0:T(8,128)(2,1)}, f32[8,320]{1,0:T(8,128)}) custom-call(s32[5]{0:T(128)} %stack.31.flags, bf16[528,320]{1,0:T(8,128)(2,1)} %get-tuple-element.80.block.rest_0_, bf16[144,320]{1,0:T(8,128)(2,1)} %copy-done.49, bf16[128,320]{1,0:T(8,128)(2,1)} %copy-done.54, ...), custom_call_target="tpu_custom_call" | custom-call | flops 943718400 | bytes 4000000 | tf_op jit(solution)/shard_map/pallas_call | solution.py:312
  44.8 3.4 collective-permute-start.15
  49.2 2.6 collective-permute-start.14
  51.8 2.4 collective-permute-start.17
  55.3 1.9 collective-permute-start.16
  57.3 1.5 collective-permute-done.17
  58.7 2.0 collective-permute-start.18
  60.8 4.3 %collective-permute-done.16 = f32[8,320]{1,0:T(8,128)S(1)} collective-permute-done((f32[8,320]{1,0:T(8,128)}, f32[8,320]{1,0:T(8,128)S(1)}, u32[]{:S(2)}, u32[]{:S(2)}) %collective-permute-start.16) | collective-permute-done | bytes 10272 | tf_op jit(solution)/shard_map/ppermute | solution.py:581
  66.4 2.0 collective-permute-start.19
  74.8 8.1 %shard_map.32.skip_ref = bf16[768,320]{1,0:T(8,128)(2,1)} custom-call(s32[5]{0:T(128)} %stack.31.flags, bf16[528,320]{1,0:T(8,128)(2,1)} %get-tuple-element.92.block, bf16[272,320]{1,0:T(8,128)(2,1)} %copy-done.51, bf16[256,320]{1,0:T(8,128)(2,1)} %copy-done.52, f32[8,320]{1,0:T(8,128)} %copy-done.45, f32[8,320]{1,0:T(8,128)} %copy-done.58, ...), custom_call_target="tpu_custom_call" | custom-call | flops 1415577600 | bytes 4000000 | tf_op jit(solution)/shard_map/pallas_call | solution.py:312
  83.0 9.1 %collective-permute-done.25.rest_2_.rest_18_ = bf16[80,3072]{1,0:T(8,128)(2,1)S(1)} collective-permute-done((bf16[80,3072]{1,0:T(8,128)(2,1)S(1)}, bf16[80,3072]{1,0:T(8,128)(2,1)S(1)}, u32[]{:S(2)}, u32[]{:S(2)}) %collective-permute-start.25) | collective-permute-done | bytes 491552 | tf_op jit(solution)/shard_map/ppermute | solution.py:585
  92.0 1.4 collective-permute-done.26.rest_3_.rest_19_
  97.6 5.2 %shard_map.33 = (bf16[144,640]{1,0:T(8,128)(2,1)}, bf16[80,640]{1,0:T(8,128)(2,1)}, bf16[64,640]{1,0:T(8,128)(2,1)}, f32[8,640]{1,0:T(8,128)}) custom-call(s32[5]{0:T(128)} %stack.31.flags, bf16[768,320]{1,0:T(8,128)(2,1)} %shard_map.32.skip_ref, bf16[80,3072]{1,0:T(8,128)(2,1)} %get-tuple-element.101.rest_0_.rest_16_, bf16[80,3072]{1,0:T(8,128)(2,1)} %copy-done.4, ...), custom_call_target="tpu_custom_call" | custom-call | flops 471859200 | bytes 4000000 | tf_op jit(solution)/shard_map/pallas_call | solution.py:349
  102.7 1.9 collective-permute-start.31
  105.6 1.5 collective-permute-start.44
  108.2 3.4 collective-permute-done.31.block.rest_0_
  111.6 1.6 broadcast_select_fusion.4
  114.6 2.1 collective-permute-start.32
  118.1 1.4 reshape.99
  120.9 2.0 collective-permute-start.35
  122.9 2.0 collective-permute-start.34
  126.2 1.4 reshape.101
  127.6 1.4 reduce_sum.93
  129.0 2.1 collective-permute-start.33
  134.8 2.1 collective-permute-start.37
  136.9 7.1 %shard_map.34 = (bf16[144,640]{1,0:T(8,128)(2,1)}, bf16[80,640]{1,0:T(8,128)(2,1)}, bf16[64,640]{1,0:T(8,128)(2,1)}, f32[8,640]{1,0:T(8,128)}) custom-call(s32[5]{0:T(128)} %stack.31.flags, bf16[144,640]{1,0:T(8,128)(2,1)} %collective-permute-done.31.block.rest_0_, bf16[80,640]{1,0:T(8,128)(2,1)} %collective-permute-done.32.outer, ...), custom_call_target="tpu_custom_call" | custom-call | flops 943718400 | bytes 4000000 | tf_op jit(solution)/shard_map/pallas_call | solution.py:385
  144.0 5.2 %collective-permute-done.44.rest_3_.rest_2_ = bf16[80,6144]{1,0:T(8,128)(2,1)S(1)} collective-permute-done((bf16[80,6144]{1,0:T(8,128)(2,1)S(1)}, bf16[80,6144]{1,0:T(8,128)(2,1)S(1)}, u32[]{:S(2)}, u32[]{:S(2)}) %collective-permute-start.44) | collective-permute-done | bytes 983072 | tf_op jit(solution)/shard_map/ppermute | solution.py:585
  151.3 1.4 collective-permute-start.41
  152.7 1.5 collective-permute-start.38
  154.2 2.0 collective-permute-start.40
  156.3 1.5 collective-permute-start.39
  159.9 7.2 %shard_map.35 = (bf16[144,640]{1,0:T(8,128)(2,1)}, bf16[80,640]{1,0:T(8,128)(2,1)}, bf16[64,640]{1,0:T(8,128)(2,1)}, f32[8,640]{1,0:T(8,128)}) custom-call(s32[5]{0:T(128)} %stack.31.flags, bf16[144,640]{1,0:T(8,128)(2,1)} %get-tuple-element.116.block, bf16[80,640]{1,0:T(8,128)(2,1)} %copy-done.29, bf16[64,640]{1,0:T(8,128)(2,1)} %copy-done.35, ...), custom_call_target="tpu_custom_call" | custom-call | flops 943718400 | bytes 4000000 | tf_op jit(solution)/shard_map/pallas_call | solution.py:385
  167.1 1.6 collective-permute-start.50
  173.6 7.1 %shard_map.36 = (bf16[144,640]{1,0:T(8,128)(2,1)}, bf16[80,640]{1,0:T(8,128)(2,1)}, bf16[64,640]{1,0:T(8,128)(2,1)}, f32[8,640]{1,0:T(8,128)}) custom-call(s32[5]{0:T(128)} %stack.31.flags, bf16[144,640]{1,0:T(8,128)(2,1)} %copy-done.11, bf16[80,640]{1,0:T(8,128)(2,1)} %copy-done.28, bf16[64,640]{1,0:T(8,128)(2,1)} %copy-done.34, f32[8,640]{1,0:T(8,128)} %copy-done.37, ...), custom_call_target="tpu_custom_call" | custom-call | flops 943718400 | bytes 4000000 | tf_op jit(solution)/shard_map/pallas_call | solution.py:385
  180.7 1.6 collective-permute-start.56
  182.3 1.4 collective-permute-start.59
  183.6 1.4 collective-permute-start.58
  185.0 1.5 collective-permute-start.57
  188.7 7.2 %shard_map.37 = (bf16[144,640]{1,0:T(8,128)(2,1)}, bf16[80,640]{1,0:T(8,128)(2,1)}, bf16[64,640]{1,0:T(8,128)(2,1)}, f32[8,640]{1,0:T(8,128)}) custom-call(s32[5]{0:T(128)} %stack.31.flags, bf16[144,640]{1,0:T(8,128)(2,1)} %get-tuple-element.125.block, bf16[80,640]{1,0:T(8,128)(2,1)} %copy-done.30, bf16[64,640]{1,0:T(8,128)(2,1)} %copy-done.33, ...), custom_call_target="tpu_custom_call" | custom-call | flops 943718400 | bytes 4000000 | tf_op jit(solution)/shard_map/pallas_call | solution.py:385
  195.9 1.6 collective-permute-start.61
  201.4 9.1 %shard_map.38 = (bf16[528,320]{1,0:T(8,128)(2,1)}, bf16[144,320]{1,0:T(8,128)(2,1)}, bf16[128,320]{1,0:T(8,128)(2,1)}, f32[8,320]{1,0:T(8,128)}) custom-call(s32[5]{0:T(128)} %stack.31.flags, bf16[144,640]{1,0:T(8,128)(2,1)} %copy-done.27, bf16[80,640]{1,0:T(8,128)(2,1)} %copy-done.53, bf16[64,640]{1,0:T(8,128)(2,1)} %copy-done.57, ...), custom_call_target="tpu_custom_call" | custom-call | flops 1887436800 | bytes 4000000 | tf_op jit(solution)/shard_map/pallas_call | solution.py:424
  210.6 1.6 collective-permute-start.64
  212.1 1.4 collective-permute-start.67
  213.5 1.4 collective-permute-start.66
  214.8 1.5 collective-permute-start.65
  218.5 9.8 %shard_map.39 = (bf16[528,320]{1,0:T(8,128)(2,1)}, bf16[144,320]{1,0:T(8,128)(2,1)}, bf16[128,320]{1,0:T(8,128)(2,1)}, f32[8,320]{1,0:T(8,128)}) custom-call(s32[5]{0:T(128)} %stack.31.flags, bf16[528,320]{1,0:T(8,128)(2,1)} %get-tuple-element.131.block.u_ref, bf16[144,320]{1,0:T(8,128)(2,1)} %copy-done.50, bf16[128,320]{1,0:T(8,128)(2,1)} %copy-done.56, ...), custom_call_target="tpu_custom_call" | custom-call | flops 1887436800 | bytes 4000000 | tf_op jit(solution)/shard_map/pallas_call | solution.py:465
  228.3 1.6 collective-permute-start.69
  229.9 1.4 collective-permute-start.72
  232.6 1.5 collective-permute-start.70
  236.2 7.9 %shard_map.40 = (bf16[8,16,320]{2,1,0:T(8,128)(2,1)}, bf16[8,16,320]{2,1,0:T(8,128)(2,1)}, bf16[8,16,320]{2,1,0:T(8,128)(2,1)}, bf16[8,16,320]{2,1,0:T(8,128)(2,1)}) custom-call(s32[5]{0:T(128)} %stack.31.flags, bf16[528,320]{1,0:T(8,128)(2,1)} %get-tuple-element.135.block, bf16[144,320]{1,0:T(8,128)(2,1)} %copy-done.31, bf16[128,320]{1,0:T(8,128)(2,1)} %copy-done.32, ...), custom_call_target="tpu_custom_call" | custom-call | flops 1153433600 | bytes 4000000 | tf_op jit(solution)/shard_map/pallas_call | solution.py:539
  244.1 1.6 collective-permute-start.74
  245.7 1.5 collective-permute-start.75
  247.2 103.5 %collective-permute-start.76 = (bf16[8,16,320]{2,1,0:T(8,128)(2,1)}, bf16[8,16,320]{2,1,0:T(8,128)(2,1)S(1)}, u32[]{:S(2)}, u32[]{:S(2)}) collective-permute-start(bf16[8,16,320]{2,1,0:T(8,128)(2,1)} %get-tuple-element.141), channel_id=1, source_target_pairs={{0,24},{1,25},{2,26},{3,27},{4,28},{5,29},{6,30},{7,31},{8,8},{9,9... | collective-permute-start | bytes 245768 | tf_op jit(solution)/shard_map/ppermute | solution.py:581
  350.7 3.6 %collective-permute-done.76 = bf16[8,16,320]{2,1,0:T(8,128)(2,1)S(1)} collective-permute-done((bf16[8,16,320]{2,1,0:T(8,128)(2,1)}, bf16[8,16,320]{2,1,0:T(8,128)(2,1)S(1)}, u32[]{:S(2)}, u32[]{:S(2)}) %collective-permute-start.76) | collective-permute-done | bytes 81952 | tf_op jit(solution)/shard_map/ppermute | solution.py:581
  (282 shorter events, 53.9 us)
Async XLA Ops:
  4.8 13.2 %collective-permute-start.3 = (bf16[144,320]{1,0:T(8,128)(2,1)}, bf16[144,320]{1,0:T(8,128)(2,1)S(1)}, u32[]{:S(2)}, u32[]{:S(2)}) collective-permute-start(bf16[144,320]{1,0:T(8,128)(2,1)} %get-tuple-element.81), channel_id=1, source_target_pairs={{0,7},{1,2},{2,1},{3,4},{4,3},{5,6},{6,5},{7,0},{8,8},{9,9},{10,10... | collective-permute-start | bytes 276488 | tf_op jit(solution)/shard_map/ppermute | solution.py:581
  12.0 14.8 %collective-permute-start = (bf16[80,1536]{1,0:T(8,128)(2,1)}, bf16[80,1536]{1,0:T(8,128)(2,1)S(1)}, u32[]{:S(2)}, u32[]{:S(2)}) collective-permute-start(bf16[80,1536]{1,0:T(8,128)(2,1)} %shard_map.29.rest_0_), channel_id=1, source_target_pairs={{0,2},{1,3},{2,0},{3,1},{4,6},{5,7},{6,4},{7,5},{8,10},{9,11},{10,... | collective-permute-start | bytes 737288 | tf_op jit(solution)/shard_map/ppermute | solution.py:585
  12.1 14.7 %collective-permute-start.1 = (bf16[80,1536]{1,0:T(8,128)(2,1)}, bf16[80,1536]{1,0:T(8,128)(2,1)S(1)}, u32[]{:S(2)}, u32[]{:S(2)}) collective-permute-start(bf16[80,1536]{1,0:T(8,128)(2,1)} %shard_map.29.rest_0_), channel_id=1, source_target_pairs={{0,4},{1,5},{2,6},{3,7},{4,0},{5,1},{6,2},{7,3},{8,12},{9,13},{10,... | collective-permute-start | bytes 737288 | tf_op jit(solution)/shard_map/ppermute | solution.py:585
  13.2 13.6 %collective-permute-start.2 = (bf16[80,1536]{1,0:T(8,128)(2,1)}, bf16[80,1536]{1,0:T(8,128)(2,1)S(1)}, u32[]{:S(2)}, u32[]{:S(2)}) collective-permute-start(bf16[80,1536]{1,0:T(8,128)(2,1)} %shard_map.29.rest_0_), channel_id=1, source_target_pairs={{0,6},{1,7},{2,4},{3,5},{4,2},{5,3},{6,0},{7,1},{8,14},{9,15},{10,... | collective-permute-start | bytes 737288 | tf_op jit(solution)/shard_map/ppermute | solution.py:585
  15.5 11.2 %collective-permute-start.6 = (f32[8,320]{1,0:T(8,128)S(1)}, f32[8,320]{1,0:T(8,128)S(1)}, u32[]{:S(2)}, u32[]{:S(2)}) collective-permute-start(f32[8,320]{1,0:T(8,128)S(1)} %copy-done.47), channel_id=1, source_target_pairs={{0,4},{1,5},{2,6},{3,7},{4,0},{5,1},{6,2},{7,3},{8,8},{9,9},{10,10... | collective-permute-start | bytes 30728 | tf_op jit(solution)/shard_map/ppermute | solution.py:581
  18.0 8.7 %collective-permute-start.5 = (f32[8,320]{1,0:T(8,128)S(1)}, f32[8,320]{1,0:T(8,128)S(1)}, u32[]{:S(2)}, u32[]{:S(2)}) collective-permute-start(f32[8,320]{1,0:T(8,128)S(1)} %copy-done.47), channel_id=1, source_target_pairs={{0,2},{1,7},{2,4},{3,1},{4,6},{5,3},{6,0},{7,5},{8,8},{9,9},{10,10... | collective-permute-start | bytes 30728 | tf_op jit(solution)/shard_map/ppermute | solution.py:581
  26.8 9.4 %collective-permute-start.8 = (bf16[80,1536]{1,0:T(8,128)(2,1)}, bf16[80,1536]{1,0:T(8,128)(2,1)S(1)}, u32[]{:S(2)}, u32[]{:S(2)}) collective-permute-start(bf16[80,1536]{1,0:T(8,128)(2,1)} %shard_map.29.rest_0_), channel_id=1, source_target_pairs={{0,1},{1,0},{2,3},{3,2},{4,5},{5,4},{6,7},{7,6},{8,9},{9,8},{10,11... | collective-permute-start | bytes 737288 | tf_op jit(solution)/shard_map/ppermute | solution.py:585
  26.9 9.4 %collective-permute-start.9 = (bf16[80,1536]{1,0:T(8,128)(2,1)S(1)}, bf16[80,1536]{1,0:T(8,128)(2,1)S(1)}, u32[]{:S(2)}, u32[]{:S(2)}) collective-permute-start(bf16[80,1536]{1,0:T(8,128)(2,1)S(1)} %collective-permute-done.rest_1_), channel_id=1, source_target_pairs={{0,1},{1,0},{2,3},{3,2},{4,5},{5,4},{6,7},{7,6},{8,9},{9,8},{10,11... | collective-permute-start | bytes 737288 | tf_op jit(solution)/shard_map/ppermute | solution.py:585
  27.4 8.9 %collective-permute-start.10 = (bf16[80,1536]{1,0:T(8,128)(2,1)S(1)}, bf16[80,1536]{1,0:T(8,128)(2,1)S(1)}, u32[]{:S(2)}, u32[]{:S(2)}) collective-permute-start(bf16[80,1536]{1,0:T(8,128)(2,1)S(1)} %collective-permute-done.1.rest_2_), channel_id=1, source_target_pairs={{0,1},{1,0},{2,3},{3,2},{4,5},{5,4},{6,7},{7,6},{8,9},{9,8},{10,11... | collective-permute-start | bytes 737288 | tf_op jit(solution)/shard_map/ppermute | solution.py:585
  27.5 8.8 %collective-permute-start.11 = (bf16[80,1536]{1,0:T(8,128)(2,1)S(1)}, bf16[80,1536]{1,0:T(8,128)(2,1)S(1)}, u32[]{:S(2)}, u32[]{:S(2)}) collective-permute-start(bf16[80,1536]{1,0:T(8,128)(2,1)S(1)} %collective-permute-done.2.rest_3_), channel_id=1, source_target_pairs={{0,1},{1,0},{2,3},{3,2},{4,5},{5,4},{6,7},{7,6},{8,9},{9,8},{10,11... | collective-permute-start | bytes 737288 | tf_op jit(solution)/shard_map/ppermute | solution.py:585
  27.9 3.2 collective-permute-start.4
  31.1 5.1 %collective-permute-start.7 = (f32[8,320]{1,0:T(8,128)S(1)}, f32[8,320]{1,0:T(8,128)S(1)}, u32[]{:S(2)}, u32[]{:S(2)}) collective-permute-start(f32[8,320]{1,0:T(8,128)S(1)} %add_add_fusion.7.sa), channel_id=1, source_target_pairs={{0,1},{1,0},{2,3},{3,2},{4,5},{5,4},{6,7},{7,6},{8,8},{9,9},{10,10... | collective-permute-start | bytes 30728 | tf_op jit(solution)/shard_map/ppermute | solution.py:581
  44.8 10.5 %collective-permute-start.15 = (bf16[272,320]{1,0:T(8,128)(2,1)}, bf16[272,320]{1,0:T(8,128)(2,1)S(1)}, u32[]{:S(2)}, u32[]{:S(2)}) collective-permute-start(bf16[272,320]{1,0:T(8,128)(2,1)} %get-tuple-element.90), channel_id=1, source_target_pairs={{0,7},{1,2},{2,1},{3,4},{4,3},{5,6},{6,5},{7,0},{8,8},{9,9},{10,10... | collective-permute-start | bytes 522248 | tf_op jit(solution)/shard_map/ppermute | solution.py:581
  48.2 17.5 %collective-permute-start.12 = (bf16[80,1536]{1,0:T(8,128)(2,1)S(1)}, bf16[80,1536]{1,0:T(8,128)(2,1)S(1)}, u32[]{:S(2)}, u32[]{:S(2)}) collective-permute-start(bf16[80,1536]{1,0:T(8,128)(2,1)S(1)} %copy-done.19), channel_id=1, source_target_pairs={{0,2},{1,3},{2,0},{3,1},{4,6},{5,7},{6,4},{7,5},{8,10},{9,11},{10,... | collective-permute-start | bytes 737288 | tf_op jit(solution)/shard_map/ppermute | solution.py:585
  48.8 16.9 %collective-permute-start.13 = (bf16[80,1536]{1,0:T(8,128)(2,1)S(1)}, bf16[80,1536]{1,0:T(8,128)(2,1)S(1)}, u32[]{:S(2)}, u32[]{:S(2)}) collective-permute-start(bf16[80,1536]{1,0:T(8,128)(2,1)S(1)} %copy-done.19), channel_id=1, source_target_pairs={{0,4},{1,5},{2,6},{3,7},{4,0},{5,1},{6,2},{7,3},{8,12},{9,13},{10,... | collective-permute-start | bytes 737288 | tf_op jit(solution)/shard_map/ppermute | solution.py:585
  49.2 16.6 %collective-permute-start.14 = (bf16[80,1536]{1,0:T(8,128)(2,1)S(1)}, bf16[80,1536]{1,0:T(8,128)(2,1)S(1)}, u32[]{:S(2)}, u32[]{:S(2)}) collective-permute-start(bf16[80,1536]{1,0:T(8,128)(2,1)S(1)} %copy-done.19), channel_id=1, source_target_pairs={{0,6},{1,7},{2,4},{3,5},{4,2},{5,3},{6,0},{7,1},{8,14},{9,15},{10,... | collective-permute-start | bytes 737288 | tf_op jit(solution)/shard_map/ppermute | solution.py:585
  51.8 7.0 %collective-permute-start.17 = (f32[8,320]{1,0:T(8,128)}, f32[8,320]{1,0:T(8,128)S(1)}, u32[]{:S(2)}, u32[]{:S(2)}) collective-permute-start(f32[8,320]{1,0:T(8,128)} %get-tuple-element.89), channel_id=1, source_target_pairs={{0,4},{1,5},{2,6},{3,7},{4,0},{5,1},{6,2},{7,3},{8,8},{9,9},{10,10... | collective-permute-start | bytes 30728 | tf_op jit(solution)/shard_map/ppermute | solution.py:581
  55.3 9.7 %collective-permute-start.16 = (f32[8,320]{1,0:T(8,128)}, f32[8,320]{1,0:T(8,128)S(1)}, u32[]{:S(2)}, u32[]{:S(2)}) collective-permute-start(f32[8,320]{1,0:T(8,128)} %get-tuple-element.89), channel_id=1, source_target_pairs={{0,2},{1,7},{2,4},{3,1},{4,6},{5,3},{6,0},{7,5},{8,8},{9,9},{10,10... | collective-permute-start | bytes 30728 | tf_op jit(solution)/shard_map/ppermute | solution.py:581
  58.7 10.9 %collective-permute-start.18 = (bf16[256,320]{1,0:T(8,128)(2,1)}, bf16[256,320]{1,0:T(8,128)(2,1)S(1)}, u32[]{:S(2)}, u32[]{:S(2)}) collective-permute-start(bf16[256,320]{1,0:T(8,128)(2,1)} %get-tuple-element.93), channel_id=1, source_target_pairs={{0,1},{1,0},{2,3},{3,2},{4,5},{5,4},{6,7},{7,6},{8,8},{9,9},{10,10... | collective-permute-start | bytes 491528 | tf_op jit(solution)/shard_map/ppermute | solution.py:581
  65.8 6.1 %collective-permute-start.20 = (bf16[80,1536]{1,0:T(8,128)(2,1)S(1)}, bf16[80,1536]{1,0:T(8,128)(2,1)S(1)}, u32[]{:S(2)}, u32[]{:S(2)}) collective-permute-start(bf16[80,1536]{1,0:T(8,128)(2,1)S(1)} %copy-done.19), channel_id=1, source_target_pairs={{0,1},{1,0},{2,3},{3,2},{4,5},{5,4},{6,7},{7,6},{8,9},{9,8},{10,11... | collective-permute-start | bytes 737288 | tf_op jit(solution)/shard_map/ppermute | solution.py:585
  65.9 6.1 %collective-permute-start.21 = (bf16[80,1536]{1,0:T(8,128)(2,1)S(1)}, bf16[80,1536]{1,0:T(8,128)(2,1)S(1)}, u32[]{:S(2)}, u32[]{:S(2)}) collective-permute-start(bf16[80,1536]{1,0:T(8,128)(2,1)S(1)} %collective-permute-done.12.rest_4_.rest_9_), channel_id=1, source_target_pairs={{0,1},{1,0},{2,3},{3,2},{4,5},{5,4},{6,7},{7,6},{8,9},{9,8},{10,11... | collective-permute-start | bytes 737288 | tf_op jit(solution)/shard_map/ppermute | solution.py:585
  66.4 4.3 %collective-permute-start.19 = (f32[8,320]{1,0:T(8,128)S(1)}, f32[8,320]{1,0:T(8,128)S(1)}, u32[]{:S(2)}, u32[]{:S(2)}) collective-permute-start(f32[8,320]{1,0:T(8,128)S(1)} %add_add_fusion.6.sa), channel_id=1, source_target_pairs={{0,1},{1,0},{2,3},{3,2},{4,5},{5,4},{6,7},{7,6},{8,8},{9,9},{10,10... | collective-permute-start | bytes 30728 | tf_op jit(solution)/shard_map/ppermute | solution.py:581
  68.4 14.6 %collective-permute-start.24 = (bf16[80,3072]{1,0:T(8,128)(2,1)S(1)}, bf16[80,3072]{1,0:T(8,128)(2,1)S(1)}, u32[]{:S(2)}, u32[]{:S(2)}) collective-permute-start(bf16[80,3072]{1,0:T(8,128)(2,1)S(1)} %copy-done.3), channel_id=1, source_target_pairs={{0,2},{1,3},{2,0},{3,1},{4,6},{5,7},{6,4},{7,5},{8,10},{9,11},{10,... | collective-permute-start | bytes 1474568 | tf_op jit(solution)/shard_map/ppermute | solution.py:585
  69.7 22.4 %collective-permute-start.25 = (bf16[80,3072]{1,0:T(8,128)(2,1)S(1)}, bf16[80,3072]{1,0:T(8,128)(2,1)S(1)}, u32[]{:S(2)}, u32[]{:S(2)}) collective-permute-start(bf16[80,3072]{1,0:T(8,128)(2,1)S(1)} %copy-done.3), channel_id=1, source_target_pairs={{0,4},{1,5},{2,6},{3,7},{4,0},{5,1},{6,2},{7,3},{8,12},{9,13},{10,... | collective-permute-start | bytes 1474568 | tf_op jit(solution)/shard_map/ppermute | solution.py:585
  70.7 22.7 %collective-permute-start.26 = (bf16[80,3072]{1,0:T(8,128)(2,1)S(1)}, bf16[80,3072]{1,0:T(8,128)(2,1)S(1)}, u32[]{:S(2)}, u32[]{:S(2)}) collective-permute-start(bf16[80,3072]{1,0:T(8,128)(2,1)S(1)} %copy-done.3), channel_id=1, source_target_pairs={{0,6},{1,7},{2,4},{3,5},{4,2},{5,3},{6,0},{7,1},{8,14},{9,15},{10,... | collective-permute-start | bytes 1474568 | tf_op jit(solution)/shard_map/ppermute | solution.py:585
  72.0 1.8 collective-permute-start.23
  93.4 1.9 collective-permute-start.27
  93.4 2.6 collective-permute-start.28
  93.9 2.8 collective-permute-start.29
  93.9 3.6 %collective-permute-start.30 = (bf16[80,3072]{1,0:T(8,128)(2,1)S(1)}, bf16[80,3072]{1,0:T(8,128)(2,1)}, u32[]{:S(2)}, u32[]{:S(2)}) collective-permute-start(bf16[80,3072]{1,0:T(8,128)(2,1)S(1)} %collective-permute-done.26.rest_3_.rest_19_), channel_id=1, source_target_pairs={{0,1},{1,0},{2,3},{3,2},{4,5},{5,4},{6,7},{7,6},{8,9},{9,8},{10,11... | collective-permute-start | bytes 1474568 | tf_op jit(solution)/shard_map/ppermute | solution.py:585
  102.7 8.9 %collective-permute-start.31 = (bf16[144,640]{1,0:T(8,128)(2,1)}, bf16[144,640]{1,0:T(8,128)(2,1)}, u32[]{:S(2)}, u32[]{:S(2)}) collective-permute-start(bf16[144,640]{1,0:T(8,128)(2,1)} %get-tuple-element.105), channel_id=1, source_target_pairs={{0,8},{1,9},{2,10},{3,11},{4,12},{5,13},{6,14},{7,15},{8,0},{9,1},... | collective-permute-start | bytes 552968 | tf_op jit(solution)/shard_map/ppermute | solution.py:581
  104.7 39.3 %collective-permute-start.43 = (bf16[80,6144]{1,0:T(8,128)(2,1)S(1)}, bf16[80,6144]{1,0:T(8,128)(2,1)S(1)}, u32[]{:S(2)}, u32[]{:S(2)}) collective-permute-start(bf16[80,6144]{1,0:T(8,128)(2,1)S(1)} %copy-done), channel_id=1, source_target_pairs={{0,2},{1,3},{2,0},{3,1},{4,6},{5,7},{6,4},{7,5},{8,10},{9,11},{10,... | collective-permute-start | bytes 2949128 | tf_op jit(solution)/shard_map/ppermute | solution.py:585
  105.6 43.7 %collective-permute-start.44 = (bf16[80,6144]{1,0:T(8,128)(2,1)S(1)}, bf16[80,6144]{1,0:T(8,128)(2,1)S(1)}, u32[]{:S(2)}, u32[]{:S(2)}) collective-permute-start(bf16[80,6144]{1,0:T(8,128)(2,1)S(1)} %copy-done), channel_id=1, source_target_pairs={{0,4},{1,5},{2,6},{3,7},{4,0},{5,1},{6,2},{7,3},{8,12},{9,13},{10,... | collective-permute-start | bytes 2949128 | tf_op jit(solution)/shard_map/ppermute | solution.py:585
  107.1 43.2 %collective-permute-start.45 = (bf16[80,6144]{1,0:T(8,128)(2,1)S(1)}, bf16[80,6144]{1,0:T(8,128)(2,1)}, u32[]{:S(2)}, u32[]{:S(2)}) collective-permute-start(bf16[80,6144]{1,0:T(8,128)(2,1)S(1)} %copy-done), channel_id=1, source_target_pairs={{0,6},{1,7},{2,4},{3,5},{4,2},{5,3},{6,0},{7,1},{8,14},{9,15},{10,... | collective-permute-start | bytes 2949128 | tf_op jit(solution)/shard_map/ppermute | solution.py:585
  114.6 8.3 %collective-permute-start.32 = (bf16[80,640]{1,0:T(8,128)(2,1)}, bf16[80,640]{1,0:T(8,128)(2,1)}, u32[]{:S(2)}, u32[]{:S(2)}) collective-permute-start(bf16[80,640]{1,0:T(8,128)(2,1)} %pad_maximum_fusion), channel_id=1, source_target_pairs={{0,0},{1,1},{2,2},{3,3},{4,4},{5,5},{6,6},{7,7},{8,15},{9,10},{10,... | collective-permute-start | bytes 307208 | tf_op jit(solution)/shard_map/ppermute | solution.py:581
  120.9 8.1 %collective-permute-start.35 = (f32[8,640]{1,0:T(8,128)}, f32[8,640]{1,0:T(8,128)}, u32[]{:S(2)}, u32[]{:S(2)}) collective-permute-start(f32[8,640]{1,0:T(8,128)} %concatenate.42), channel_id=1, source_target_pairs={{0,0},{1,1},{2,2},{3,3},{4,4},{5,5},{6,6},{7,7},{8,12},{9,13},{10,... | collective-permute-start | bytes 61448 | tf_op jit(solution)/shard_map/ppermute | solution.py:581
  122.9 8.3 %collective-permute-start.34 = (f32[8,640]{1,0:T(8,128)}, f32[8,640]{1,0:T(8,128)}, u32[]{:S(2)}, u32[]{:S(2)}) collective-permute-start(f32[8,640]{1,0:T(8,128)} %concatenate.42), channel_id=1, source_target_pairs={{0,0},{1,1},{2,2},{3,3},{4,4},{5,5},{6,6},{7,7},{8,10},{9,15},{10,... | collective-permute-start | bytes 61448 | tf_op jit(solution)/shard_map/ppermute | solution.py:581
  129.0 4.7 %collective-permute-start.33 = (bf16[64,640]{1,0:T(8,128)(2,1)}, bf16[64,640]{1,0:T(8,128)(2,1)}, u32[]{:S(2)}, u32[]{:S(2)}) collective-permute-start(bf16[64,640]{1,0:T(8,128)(2,1)} %get-tuple-element.147), channel_id=1, source_target_pairs={{0,0},{1,1},{2,2},{3,3},{4,4},{5,5},{6,6},{7,7},{8,9},{9,8},{10,11... | collective-permute-start | bytes 245768 | tf_op jit(solution)/shard_map/ppermute | solution.py:581
  134.8 16.6 %collective-permute-start.37 = (bf16[768,320]{0,1:T(8,128)(2,1)}, bf16[768,320]{0,1:T(8,128)(2,1)S(1)}, u32[]{:S(2)}, u32[]{:S(2)}) collective-permute-start(bf16[768,320]{0,1:T(8,128)(2,1)} %copy.10), channel_id=1, source_target_pairs={{0,24},{1,25},{2,26},{3,27},{4,28},{5,29},{6,30},{7,31},{8,8},{9,9... | collective-permute-start | bytes 1474568 | tf_op jit(solution)/shard_map/ppermute | solution.py:581
  150.3 9.0 %collective-permute-start.46 = (bf16[80,6144]{1,0:T(8,128)(2,1)S(1)}, bf16[80,6144]{1,0:T(8,128)(2,1)}, u32[]{:S(2)}, u32[]{:S(2)}) collective-permute-start(bf16[80,6144]{1,0:T(8,128)(2,1)S(1)} %copy-done), channel_id=1, source_target_pairs={{0,1},{1,0},{2,3},{3,2},{4,5},{5,4},{6,7},{7,6},{8,9},{9,8},{10,11... | collective-permute-start | bytes 2949128 | tf_op jit(solution)/shard_map/ppermute | solution.py:585
  150.3 9.0 %collective-permute-start.47 = (bf16[80,6144]{1,0:T(8,128)(2,1)S(1)}, bf16[80,6144]{1,0:T(8,128)(2,1)}, u32[]{:S(2)}, u32[]{:S(2)}) collective-permute-start(bf16[80,6144]{1,0:T(8,128)(2,1)S(1)} %collective-permute-done.43.rest_2_.rest_1_), channel_id=1, source_target_pairs={{0,1},{1,0},{2,3},{3,2},{4,5},{5,4},{6,7},{7,6},{8,9},{9,8},{10,11... | collective-permute-start | bytes 2949128 | tf_op jit(solution)/shard_map/ppermute | solution.py:585
  150.8 8.5 %collective-permute-start.48 = (bf16[80,6144]{1,0:T(8,128)(2,1)S(1)}, bf16[80,6144]{1,0:T(8,128)(2,1)}, u32[]{:S(2)}, u32[]{:S(2)}) collective-permute-start(bf16[80,6144]{1,0:T(8,128)(2,1)S(1)} %collective-permute-done.44.rest_3_.rest_2_), channel_id=1, source_target_pairs={{0,1},{1,0},{2,3},{3,2},{4,5},{5,4},{6,7},{7,6},{8,9},{9,8},{10,11... | collective-permute-start | bytes 2949128 | tf_op jit(solution)/shard_map/ppermute | solution.py:585
  150.8 8.5 %collective-permute-start.49 = (bf16[80,6144]{1,0:T(8,128)(2,1)}, bf16[80,6144]{1,0:T(8,128)(2,1)}, u32[]{:S(2)}, u32[]{:S(2)}) collective-permute-start(bf16[80,6144]{1,0:T(8,128)(2,1)} %collective-permute-done.45.rest_4_.rest_3_), channel_id=1, source_target_pairs={{0,1},{1,0},{2,3},{3,2},{4,5},{5,4},{6,7},{7,6},{8,9},{9,8},{10,11... | collective-permute-start | bytes 2949128 | tf_op jit(solution)/shard_map/ppermute | solution.py:585
  154.2 2.0 collective-permute-start.40
  156.3 2.3 collective-permute-start.39
  168.7 2.8 collective-permute-start.51
  169.5 2.1 collective-permute-start.54
  180.7 5.8 %collective-permute-start.56 = (bf16[80,640]{1,0:T(8,128)(2,1)}, bf16[80,640]{1,0:T(8,128)(2,1)S(1)}, u32[]{:S(2)}, u32[]{:S(2)}) collective-permute-start(bf16[80,640]{1,0:T(8,128)(2,1)} %get-tuple-element.126), channel_id=1, source_target_pairs={{0,0},{1,1},{2,2},{3,3},{4,4},{5,5},{6,6},{7,7},{8,8},{9,9},{10,10... | collective-permute-start | bytes 307208 | tf_op jit(solution)/shard_map/ppermute | solution.py:581
  182.3 4.4 %collective-permute-start.59 = (f32[8,640]{1,0:T(8,128)}, f32[8,640]{1,0:T(8,128)S(1)}, u32[]{:S(2)}, u32[]{:S(2)}) collective-permute-start(f32[8,640]{1,0:T(8,128)} %get-tuple-element.128), channel_id=1, source_target_pairs={{0,0},{1,1},{2,2},{3,3},{4,4},{5,5},{6,6},{7,7},{8,8},{9,9},{10,10... | collective-permute-start | bytes 61448 | tf_op jit(solution)/shard_map/ppermute | solution.py:581
  183.6 3.0 collective-permute-start.58
  185.0 3.0 collective-permute-start.57
  197.5 2.6 collective-permute-start.62
  198.2 2.0 collective-permute-start.63
  210.6 5.8 %collective-permute-start.64 = (bf16[144,320]{1,0:T(8,128)(2,1)}, bf16[144,320]{1,0:T(8,128)(2,1)S(1)}, u32[]{:S(2)}, u32[]{:S(2)}) collective-permute-start(bf16[144,320]{1,0:T(8,128)(2,1)} %get-tuple-element.132), channel_id=1, source_target_pairs={{0,0},{1,1},{2,2},{3,3},{4,4},{5,5},{6,6},{7,7},{8,8},{9,9},{10,10... | collective-permute-start | bytes 276488 | tf_op jit(solution)/shard_map/ppermute | solution.py:581
  212.1 4.3 %collective-permute-start.67 = (f32[8,320]{1,0:T(8,128)}, f32[8,320]{1,0:T(8,128)S(1)}, u32[]{:S(2)}, u32[]{:S(2)}) collective-permute-start(f32[8,320]{1,0:T(8,128)} %get-tuple-element.134), channel_id=1, source_target_pairs={{0,0},{1,1},{2,2},{3,3},{4,4},{5,5},{6,6},{7,7},{8,8},{9,9},{10,10... | collective-permute-start | bytes 30728 | tf_op jit(solution)/shard_map/ppermute | solution.py:581
  213.5 3.0 collective-permute-start.66
  214.8 3.0 collective-permute-start.65
  228.3 5.8 %collective-permute-start.69 = (bf16[144,320]{1,0:T(8,128)(2,1)}, bf16[144,320]{1,0:T(8,128)(2,1)S(1)}, u32[]{:S(2)}, u32[]{:S(2)}) collective-permute-start(bf16[144,320]{1,0:T(8,128)(2,1)} %get-tuple-element.136), channel_id=1, source_target_pairs={{0,0},{1,1},{2,2},{3,3},{4,4},{5,5},{6,6},{7,7},{8,8},{9,9},{10,10... | collective-permute-start | bytes 276488 | tf_op jit(solution)/shard_map/ppermute | solution.py:581
  229.9 4.3 %collective-permute-start.72 = (f32[8,320]{1,0:T(8,128)}, f32[8,320]{1,0:T(8,128)S(1)}, u32[]{:S(2)}, u32[]{:S(2)}) collective-permute-start(f32[8,320]{1,0:T(8,128)} %get-tuple-element.138), channel_id=1, source_target_pairs={{0,0},{1,1},{2,2},{3,3},{4,4},{5,5},{6,6},{7,7},{8,8},{9,9},{10,10... | collective-permute-start | bytes 30728 | tf_op jit(solution)/shard_map/ppermute | solution.py:581
  231.2 3.0 collective-permute-start.71
  232.6 3.0 collective-permute-start.70
  244.1 106.6 %collective-permute-start.74 = (bf16[8,16,320]{2,1,0:T(8,128)(2,1)}, bf16[8,16,320]{2,1,0:T(8,128)(2,1)S(1)}, u32[]{:S(2)}, u32[]{:S(2)}) collective-permute-start(bf16[8,16,320]{2,1,0:T(8,128)(2,1)} %get-tuple-element.139), channel_id=1, source_target_pairs={{0,0},{1,1},{2,2},{3,3},{4,4},{5,5},{6,6},{7,7},{8,8},{9,9},{10,10... | collective-permute-start | bytes 245768 | tf_op jit(solution)/shard_map/ppermute | solution.py:581
  245.7 105.0 %collective-permute-start.75 = (bf16[8,16,320]{2,1,0:T(8,128)(2,1)}, bf16[8,16,320]{2,1,0:T(8,128)(2,1)S(1)}, u32[]{:S(2)}, u32[]{:S(2)}) collective-permute-start(bf16[8,16,320]{2,1,0:T(8,128)(2,1)} %get-tuple-element.140), channel_id=1, source_target_pairs={{0,0},{1,1},{2,2},{3,3},{4,4},{5,5},{6,6},{7,7},{8,24},{9,25},{10,... | collective-permute-start | bytes 245768 | tf_op jit(solution)/shard_map/ppermute | solution.py:581
  247.2 107.2 %collective-permute-start.76 = (bf16[8,16,320]{2,1,0:T(8,128)(2,1)}, bf16[8,16,320]{2,1,0:T(8,128)(2,1)S(1)}, u32[]{:S(2)}, u32[]{:S(2)}) collective-permute-start(bf16[8,16,320]{2,1,0:T(8,128)(2,1)} %get-tuple-element.141), channel_id=1, source_target_pairs={{0,24},{1,25},{2,26},{3,27},{4,28},{5,29},{6,30},{7,31},{8,8},{9,9... | collective-permute-start | bytes 245768 | tf_op jit(solution)/shard_map/ppermute | solution.py:581
  (74 other events, 348.8 us)
where the time goes:
time: 358 us; the launch traced here: 355 us
  starting transfers between devices  199 us (56%)
  Pallas kernels  82.6 us (23%)
  waiting for transfers between devices  41.6 us (12%)
  local copies, waits for them, and re-layouts  18.6 us (5%)
  other arithmetic  11.9 us (3%)
    ppermute x49, starting transfers between devices, permute(): return lax.ppermute(value, ('section', 'space'), pairs)  181 us
    pallas_call x4, Pallas kernels, coarse_conv(): call(body, 1, 5 + extra, len(pieces), outs, scratch_of(weights, rows + 2,...  28.6 us
    ppermute x49, waiting for transfers between devices, permute(): return lax.ppermute(value, ('section', 'space'), pairs)  21.3 us
    ppermute x28, waiting for transfers between devices, within(): return lax.ppermute(value, ('section', 'space'), pairs)  20.3 us
    ppermute x28, starting transfers between devices, within(): return lax.ppermute(value, ('section', 'space'), pairs)  18.4 us
    pallas_call x2, Pallas kernels, fine_conv(): call(body, 1, 5 + extra, n_pieces, outs, scratch_of(weights, image_rows,...  15.1 us
    unnamed x123, local copies, waits for them, and re-layouts  9.95 us
    pallas_call x1, Pallas kernels, join_conv(): call(body, 1, 6, len(pieces), outs, scratch, flops)  9.82 us
  transfers between devices with their start and end apart: 77, of which 16 were waited for; matrix products, arithmetic and copies ran while one was open for 5% of the time, Pallas kernels for 6%

commit v1 on v0

--- a/solution.py
+++ b/solution.py
@@ -574,6 +574,8 @@
     bounds = list(zip(cuts[:-1], cuts[1:], strict=True))
 
     def permute(value, source, target, move):
+        if source == target:
+            return within(value, move)
         other = {source: target, target: source}
         pairs = [
             (s * n + i, other[s] * n + move(i) if s in other else s * n + i) for s in range(n_section) for i in range(n)
@@ -596,11 +598,12 @@
     def partner(i):
         return i ^ 1
 
-    def sums_of(tail):
-        tail = tail[: TAIL // 4 * 3].astype(F32).reshape(-1, 3, tail.shape[1]).sum(1)
-        return jnp.concatenate([tail, jnp.zeros((8 - tail.shape[0], tail.shape[1]), F32)], 0)
-
-    def exchange(made, source, target, with_stats=True):
+    def sums_of(tail, count):
+        tail = tail.astype(F32)
+        rows = [tail[i : i + 1] + tail[i + 1 : i + 2] + tail[i + 2 : i + 3] for i in range(0, 3 * count, 3)]
+        return jnp.concatenate(rows + [jnp.zeros((8 - count, tail.shape[1]), F32)], 0)
+
+    def exchange(made, source, target, with_stats=True, count=2):
         block, outer, inner, own = made
         if source != target:
             block = permute(block, source, target, lambda i: i)
@@ -608,7 +611,7 @@
             top, bottom, tail = block[:size], block[rows - size : rows], block[rows:]
             outer = jnp.concatenate([jnp.where(flags[0] == 0, top, bottom), tail], 0)
             inner = jnp.where(flags[0] == 0, bottom, top)
-            own = sums_of(tail)
+            own = sums_of(tail, count)
         stats = own
         outer = permute(outer, target, target, to_outer)
         inner = permute(inner, target, target, partner)
@@ -617,7 +620,7 @@
         if n == 8:
             b = permute(stats, target, target, ahead)
             c = permute(stats, target, target, across)
-            mine = own + sums_of(outer[-TAIL:]) + b + c
+            mine = own + sums_of(outer[-TAIL:], count) + b + c
             other = permute(mine, target, target, partner)
         else:
             mine = lax.psum(own, "space")
@@ -645,9 +648,14 @@
         got = jnp.pad(got, ((0, 0), (0, 0), (0, 0), (0, shape.lanes - shape.blk)))
         return list(got.reshape(shape.m, shape.cols_of, -1))
 
-    def finish(number, got, *deps):
+    def finish(number, got, *deps, last_dep=None):
         if n == 8:
-            got = after(got, *deps)
+            early, late = list(got[:3]), list(got[3:])
+            if last_dep is not None:
+                late = after(late, last_dep)
+            if deps:
+                early = after(early, *deps)
+            got = early + late
             shared = [within(part, partner) for part in got]
             near = [lambda flags, j=j: ((flags[4] // 2) ^ j) * 2 + flags[0] for j in range(4)]
             far = [lambda flags, j=j: ((flags[4] // 2) ^ j) * 2 + 1 - flags[0] for j in range(4)]
@@ -689,13 +697,14 @@
             skip = permute(skip, 0, n_section - 1, lambda i: i)
         hidden = coarse_conv(shape, flags, *weights(0, wide, wide), got, 1)
         if section == 1:
-            finish(3, sent, hidden[3])
             hidden, skip = lax.optimization_barrier((hidden, skip))
         then = exchange(hidden, section, section)
+        if section == 1:
+            finish(3, sent, hidden[3], last_dep=then[3])
         coarse = coarse_conv(shape, flags, *weights(36 * q_rows, wide, wide), then, 1, residual=got[0])
     got = exchange(coarse, 2, 3, with_stats=False)
     up = up_conv(shape, flags, *weights(0, wide, narrow), got, skip, 1)
-    got = exchange(up, 3, 3)
+    got = exchange(up, 3, 3, count=4)
     hidden = join_conv(shape, flags, *weights(18 * q_rows, wide, narrow), got, skip, 1)
     then = exchange(hidden, 3, 3)
     outs = last_conv(shape, flags, *weights(36 * q_rows, narrow, narrow), then, got[0], skip, 45 * q_rows, n_section)

time: 358 us -> 288 us (0.80)
  starting transfers between devices: 199 us -> 81.3 us
  waiting for transfers between devices: 41.6 us -> 100 us
  other arithmetic: 11.9 us -> 6.25 us
    ppermute x49 -> x7, starting transfers between devices: 181 us -> 33.3 us  [permute(): return lax.ppermute(value, ('section', 'space'), pairs)]
    ppermute x28 -> x70, waiting for transfers between devices: 20.3 us -> 89.7 us  [within(): return lax.ppermute(value, ('section', 'space'), pairs)]
    ppermute x28 -> x70, starting transfers between devices: 18.4 us -> 48 us  [within(): return lax.ppermute(value, ('section', 'space'), pairs)]
    ppermute x49 -> x7, waiting for transfers between devices: 21.3 us -> 10.8 us  [permute(): return lax.ppermute(value, ('section', 'space'), pairs)]
    unnamed x123 -> x131, local copies, waits for them, and re-layouts: 9.95 us -> 10.8 us
  transfers between devices with their start and end apart: 77 -> 77, of which waited for: 16 -> 35; matrix products, arithmetic and copies ran while one was open for 5% -> 3% of each run, Pallas kernels for 6% -> 7%
where the time goes in v1:
time: 288 us; the launch traced here: 287 us
  waiting for transfers between devices  100 us (35%)
  Pallas kernels  82.6 us (29%)
  starting transfers between devices  81.3 us (28%)
  local copies, waits for them, and re-layouts  15.2 us (5%)
  other arithmetic  6.25 us (2%)
    ppermute x70, waiting for transfers between devices, within(): return lax.ppermute(value, ('section', 'space'), pairs)  89.7 us
    ppermute x70, starting transfers between devices, within(): return lax.ppermute(value, ('section', 'space'), pairs)  48 us
    ppermute x7, starting transfers between devices, permute(): return lax.ppermute(value, ('section', 'space'), pairs)  33.3 us
    pallas_call x4, Pallas kernels, coarse_conv(): call(body, 1, 5 + extra, len(pieces), outs, scratch_of(weights, rows + 2,...  28.6 us
    pallas_call x2, Pallas kernels, fine_conv(): call(body, 1, 5 + extra, n_pieces, outs, scratch_of(weights, image_rows,...  15.1 us
    ppermute x7, waiting for transfers between devices, permute(): return lax.ppermute(value, ('section', 'space'), pairs)  10.8 us
    unnamed x131, local copies, waits for them, and re-layouts  10.8 us
    pallas_call x1, Pallas kernels, join_conv(): call(body, 1, 6, len(pieces), outs, scratch, flops)  9.81 us
  transfers between devices with their start and end apart: 77, of which 35 were waited for; matrix products, arithmetic and copies ran while one was open for 3% of the time, Pallas kernels for 7%

profile of v1, /device:TPU:0, one launch (start us, length us, event | category | flops | bytes accessed | tf_op | source)
XLA Modules:
  0.0 286.7 jit_solution(11793188069074286355)
XLA Ops:
  0.0 1.2 copy.8
  2.6 2.0 shard_map.28
  4.7 3.4 %collective-permute-start.3 = (bf16[144,320]{1,0:T(8,128)(2,1)}, bf16[144,320]{1,0:T(8,128)(2,1)S(1)}, u32[]{:S(2)}, u32[]{:S(2)}) collective-permute-start(bf16[144,320]{1,0:T(8,128)(2,1)} %get-tuple-element.78), channel_id=1, source_target_pairs={{0,7},{1,2},{2,1},{3,4},{4,3},{5,6},{6,5},{7,0},{8,15},{9,10},{10,... | collective-permute-start | bytes 276488 | tf_op jit(solution)/shard_map/ppermute | solution.py:587
  8.1 1.2 collective-permute-start.6
  9.3 1.8 shard_map.29.rest_0_
  11.1 2.4 collective-permute-start
  14.0 1.0 collective-permute-start.2
  15.2 5.3 %collective-permute-done.rest_1_ = bf16[80,1536]{1,0:T(8,128)(2,1)S(1)} collective-permute-done((bf16[80,1536]{1,0:T(8,128)(2,1)}, bf16[80,1536]{1,0:T(8,128)(2,1)S(1)}, u32[]{:S(2)}, u32[]{:S(2)}) %collective-permute-start) | collective-permute-done | bytes 245792 | tf_op jit(solution)/shard_map/ppermute | solution.py:587
  20.4 5.3 %collective-permute-done.1.rest_2_ = bf16[80,1536]{1,0:T(8,128)(2,1)S(1)} collective-permute-done((bf16[80,1536]{1,0:T(8,128)(2,1)}, bf16[80,1536]{1,0:T(8,128)(2,1)S(1)}, u32[]{:S(2)}, u32[]{:S(2)}) %collective-permute-start.1) | collective-permute-done | bytes 245792 | tf_op jit(solution)/shard_map/ppermute | solution.py:587
  26.8 1.6 collective-permute-done.4.inner.rest_2_
  28.8 3.1 %shard_map.30 = (bf16[80,1536]{1,0:T(8,128)(2,1)}, bf16[80,3072]{1,0:T(8,128)(2,1)}, bf16[80,6144]{1,0:T(8,128)(2,1)}) custom-call(bf16[80,11520]{1,0:T(8,128)(2,1)} %bitcast.16), custom_call_target="tpu_custom_call" | custom-call | flops 1000 | bytes 4000000 | tf_op jit(solution)/shard_map/pallas_call | solution.py:561
  33.4 7.0 %shard_map.31 = (bf16[528,320]{1,0:T(8,128)(2,1)}, bf16[272,320]{1,0:T(8,128)(2,1)}, bf16[256,320]{1,0:T(8,128)(2,1)}, f32[8,320]{1,0:T(8,128)}) custom-call(s32[5]{0:T(128)} %stack.31.flags, bf16[528,320]{1,0:T(8,128)(2,1)} %get-tuple-element.77.block.rest_0_, bf16[144,320]{1,0:T(8,128)(2,1)} %copy-done.53, bf16[128,320]{1,0:T(8,128)(2,1)} %copy-done.58, ...), custom_call_target="tpu_custom_call" | custom-call | flops 943718400 | bytes 4000000 | tf_op jit(solution)/shard_map/pallas_call | solution.py:312
  40.8 1.5 collective-permute-start.12
  43.2 1.5 collective-permute-start.14
  44.6 1.2 collective-permute-start.16
  45.8 3.3 %collective-permute-done.15.outer = bf16[272,320]{1,0:T(8,128)(2,1)S(1)} collective-permute-done((bf16[272,320]{1,0:T(8,128)(2,1)}, bf16[272,320]{1,0:T(8,128)(2,1)S(1)}, u32[]{:S(2)}, u32[]{:S(2)}) %collective-permute-start.15) | collective-permute-done | bytes 174112 | tf_op jit(solution)/shard_map/ppermute | solution.py:587
  49.1 8.4 %collective-permute-done.14.rest_6_.rest_11_ = bf16[80,1536]{1,0:T(8,128)(2,1)S(1)} collective-permute-done((bf16[80,1536]{1,0:T(8,128)(2,1)S(1)}, bf16[80,1536]{1,0:T(8,128)(2,1)S(1)}, u32[]{:S(2)}, u32[]{:S(2)}) %collective-permute-start.14) | collective-permute-done | bytes 245792 | tf_op jit(solution)/shard_map/ppermute | solution.py:587
  60.0 1.4 collective-permute-start.24
  61.4 1.1 collective-permute-start.25
  66.5 8.1 %shard_map.32.skip_ref = bf16[768,320]{1,0:T(8,128)(2,1)} custom-call(s32[5]{0:T(128)} %stack.31.flags, bf16[528,320]{1,0:T(8,128)(2,1)} %get-tuple-element.88.block, bf16[272,320]{1,0:T(8,128)(2,1)} %copy-done.55, bf16[256,320]{1,0:T(8,128)(2,1)} %copy-done.56, f32[8,320]{1,0:T(8,128)} %copy-done.50, f32[8,320]{1,0:T(8,128)} %copy-done.62, ...), custom_call_target="tpu_custom_call" | custom-call | flops 1415577600 | bytes 4000000 | tf_op jit(solution)/shard_map/pallas_call | solution.py:312
  74.6 9.2 %collective-permute-done.25.rest_2_.rest_18_ = bf16[80,3072]{1,0:T(8,128)(2,1)S(1)} collective-permute-done((bf16[80,3072]{1,0:T(8,128)(2,1)S(1)}, bf16[80,3072]{1,0:T(8,128)(2,1)S(1)}, u32[]{:S(2)}, u32[]{:S(2)}) %collective-permute-start.25) | collective-permute-done | bytes 491552 | tf_op jit(solution)/shard_map/ppermute | solution.py:587
  87.9 5.2 %shard_map.33 = (bf16[144,640]{1,0:T(8,128)(2,1)}, bf16[80,640]{1,0:T(8,128)(2,1)}, bf16[64,640]{1,0:T(8,128)(2,1)}, f32[8,640]{1,0:T(8,128)}) custom-call(s32[5]{0:T(128)} %stack.31.flags, bf16[768,320]{1,0:T(8,128)(2,1)} %shard_map.32.skip_ref, bf16[80,3072]{1,0:T(8,128)(2,1)} %get-tuple-element.96.rest_0_.rest_16_, bf16[80,3072]{1,0:T(8,128)(2,1)} %copy-done.7, ...), custom_call_target="tpu_custom_call" | custom-call | flops 471859200 | bytes 4000000 | tf_op jit(solution)/shard_map/pallas_call | solution.py:349
  93.1 5.4 %collective-permute-start.31 = (bf16[144,640]{1,0:T(8,128)(2,1)}, bf16[144,640]{1,0:T(8,128)(2,1)}, u32[]{:S(2)}, u32[]{:S(2)}) collective-permute-start(bf16[144,640]{1,0:T(8,128)(2,1)} %get-tuple-element.99), channel_id=1, source_target_pairs={{0,8},{1,9},{2,10},{3,11},{4,12},{5,13},{6,14},{7,15},{8,0},{9,1},... | collective-permute-start | bytes 552968 | tf_op jit(solution)/shard_map/ppermute | solution.py:583
  98.6 1.5 collective-permute-start.44
  100.1 3.7 %collective-permute-done.31.block.rest_0_ = bf16[144,640]{1,0:T(8,128)(2,1)} collective-permute-done((bf16[144,640]{1,0:T(8,128)(2,1)}, bf16[144,640]{1,0:T(8,128)(2,1)}, u32[]{:S(2)}, u32[]{:S(2)}) %collective-permute-start.31) | collective-permute-done | bytes 184352 | tf_op jit(solution)/shard_map/ppermute | solution.py:583
  105.6 1.2 collective-permute-start.34
  106.8 1.4 collective-permute-start.35
  108.2 15.8 %collective-permute-done.32.outer = bf16[80,640]{1,0:T(8,128)(2,1)S(1)} collective-permute-done((bf16[80,640]{1,0:T(8,128)(2,1)S(1)}, bf16[80,640]{1,0:T(8,128)(2,1)S(1)}, u32[]{:S(2)}, u32[]{:S(2)}) %collective-permute-start.32) | collective-permute-done | bytes 102432 | tf_op jit(solution)/shard_map/ppermute | solution.py:587
  126.3 1.3 collective-permute-done.36.sb
  128.6 5.4 %collective-permute-start.37 = (bf16[768,320]{0,1:T(8,128)(2,1)}, bf16[768,320]{0,1:T(8,128)(2,1)S(1)}, u32[]{:S(2)}, u32[]{:S(2)}) collective-permute-start(bf16[768,320]{0,1:T(8,128)(2,1)} %copy.10), channel_id=1, source_target_pairs={{0,24},{1,25},{2,26},{3,27},{4,28},{5,29},{6,30},{7,31},{8,8},{9,9... | collective-permute-start | bytes 1474568 | tf_op jit(solution)/shard_map/ppermute | solution.py:583
  134.9 7.1 %shard_map.34 = (bf16[144,640]{1,0:T(8,128)(2,1)}, bf16[80,640]{1,0:T(8,128)(2,1)}, bf16[64,640]{1,0:T(8,128)(2,1)}, f32[8,640]{1,0:T(8,128)}) custom-call(s32[5]{0:T(128)} %stack.31.flags, bf16[144,640]{1,0:T(8,128)(2,1)} %collective-permute-done.31.block.rest_0_, bf16[80,640]{1,0:T(8,128)(2,1)} %copy-done.32, ...), custom_call_target="tpu_custom_call" | custom-call | flops 943718400 | bytes 4000000 | tf_op jit(solution)/shard_map/pallas_call | solution.py:385
  142.0 3.8 %collective-permute-done.37 = bf16[768,320]{0,1:T(8,128)(2,1)S(1)} collective-permute-done((bf16[768,320]{0,1:T(8,128)(2,1)}, bf16[768,320]{0,1:T(8,128)(2,1)S(1)}, u32[]{:S(2)}, u32[]{:S(2)}) %collective-permute-start.37) | collective-permute-done | bytes 491552 | tf_op jit(solution)/shard_map/ppermute | solution.py:583
  146.8 1.2 collective-permute-start.41
  147.9 1.4 collective-permute-start.46
  149.3 10.4 %collective-permute-done.38.outer = bf16[80,640]{1,0:T(8,128)(2,1)S(1)} collective-permute-done((bf16[80,640]{1,0:T(8,128)(2,1)}, bf16[80,640]{1,0:T(8,128)(2,1)S(1)}, u32[]{:S(2)}, u32[]{:S(2)}) %collective-permute-start.38) | collective-permute-done | bytes 102432 | tf_op jit(solution)/shard_map/ppermute | solution.py:587
  162.7 2.8 collective-permute-done.39.inner
  169.0 7.2 %shard_map.35 = (bf16[144,640]{1,0:T(8,128)(2,1)}, bf16[80,640]{1,0:T(8,128)(2,1)}, bf16[64,640]{1,0:T(8,128)(2,1)}, f32[8,640]{1,0:T(8,128)}) custom-call(s32[5]{0:T(128)} %stack.31.flags, bf16[144,640]{1,0:T(8,128)(2,1)} %get-tuple-element.110.block, bf16[80,640]{1,0:T(8,128)(2,1)} %copy-done.31, bf16[64,640]{1,0:T(8,128)(2,1)} %copy-done.39, ...), custom_call_target="tpu_custom_call" | custom-call | flops 943718400 | bytes 4000000 | tf_op jit(solution)/shard_map/pallas_call | solution.py:385
  176.2 1.6 collective-permute-start.50
  177.9 1.3 collective-permute-start.51
  181.6 2.4 collective-permute-done.51.outer
  184.6 1.2 collective-permute-done.55.sb
  186.4 7.1 %shard_map.36 = (bf16[144,640]{1,0:T(8,128)(2,1)}, bf16[80,640]{1,0:T(8,128)(2,1)}, bf16[64,640]{1,0:T(8,128)(2,1)}, f32[8,640]{1,0:T(8,128)}) custom-call(s32[5]{0:T(128)} %stack.31.flags, bf16[144,640]{1,0:T(8,128)(2,1)} %copy-done.14, bf16[80,640]{1,0:T(8,128)(2,1)} %copy-done.33, bf16[64,640]{1,0:T(8,128)(2,1)} %copy-done.38, f32[8,640]{1,0:T(8,128)} %copy-done.43, ...), custom_call_target="tpu_custom_call" | custom-call | flops 943718400 | bytes 4000000 | tf_op jit(solution)/shard_map/pallas_call | solution.py:385
  193.6 1.4 collective-permute-start.56
  197.2 2.9 collective-permute-done.56.outer
  201.2 1.1 collective-permute-done.60.sb
  202.9 7.2 %shard_map.37 = (bf16[144,640]{1,0:T(8,128)(2,1)}, bf16[80,640]{1,0:T(8,128)(2,1)}, bf16[64,640]{1,0:T(8,128)(2,1)}, f32[8,640]{1,0:T(8,128)}) custom-call(s32[5]{0:T(128)} %stack.31.flags, bf16[144,640]{1,0:T(8,128)(2,1)} %get-tuple-element.119.block, bf16[80,640]{1,0:T(8,128)(2,1)} %copy-done.34, bf16[64,640]{1,0:T(8,128)(2,1)} %copy-done.37, ...), custom_call_target="tpu_custom_call" | custom-call | flops 943718400 | bytes 4000000 | tf_op jit(solution)/shard_map/pallas_call | solution.py:385
  210.1 1.6 collective-permute-start.61
  211.7 1.5 collective-permute-start.62
  213.2 1.1 copy.11.skip_ref
  214.5 3.3 %collective-permute-done.62.outer = bf16[80,640]{1,0:T(8,128)(2,1)S(1)} collective-permute-done((bf16[80,640]{1,0:T(8,128)(2,1)S(1)}, bf16[80,640]{1,0:T(8,128)(2,1)S(1)}, u32[]{:S(2)}, u32[]{:S(2)}) %collective-permute-start.62) | collective-permute-done | bytes 102432 | tf_op jit(solution)/shard_map/ppermute | solution.py:587
  218.4 9.1 %shard_map.38 = (bf16[528,320]{1,0:T(8,128)(2,1)}, bf16[144,320]{1,0:T(8,128)(2,1)}, bf16[128,320]{1,0:T(8,128)(2,1)}, f32[8,320]{1,0:T(8,128)}) custom-call(s32[5]{0:T(128)} %stack.31.flags, bf16[144,640]{1,0:T(8,128)(2,1)} %copy-done.30, bf16[80,640]{1,0:T(8,128)(2,1)} %copy-done.57, bf16[64,640]{1,0:T(8,128)(2,1)} %copy-done.61, ...), custom_call_target="tpu_custom_call" | custom-call | flops 1887436800 | bytes 4000000 | tf_op jit(solution)/shard_map/pallas_call | solution.py:424
  228.7 1.1 collective-permute-start.67
  229.8 1.2 collective-permute-start.65
  231.1 2.5 collective-permute-done.64.outer
  234.4 1.1 collective-permute-done.68.sb
  236.2 9.8 %shard_map.39 = (bf16[528,320]{1,0:T(8,128)(2,1)}, bf16[144,320]{1,0:T(8,128)(2,1)}, bf16[128,320]{1,0:T(8,128)(2,1)}, f32[8,320]{1,0:T(8,128)}) custom-call(s32[5]{0:T(128)} %stack.31.flags, bf16[528,320]{1,0:T(8,128)(2,1)} %get-tuple-element.125.block.u_ref, bf16[144,320]{1,0:T(8,128)(2,1)} %copy-done.54, bf16[128,320]{1,0:T(8,128)(2,1)} %copy-done.60, ...), custom_call_target="tpu_custom_call" | custom-call | flops 1887436800 | bytes 4000000 | tf_op jit(solution)/shard_map/pallas_call | solution.py:465
  246.0 1.3 collective-permute-start.69
  249.5 3.0 %collective-permute-done.69.outer = bf16[144,320]{1,0:T(8,128)(2,1)S(1)} collective-permute-done((bf16[144,320]{1,0:T(8,128)(2,1)}, bf16[144,320]{1,0:T(8,128)(2,1)S(1)}, u32[]{:S(2)}, u32[]{:S(2)}) %collective-permute-start.69) | collective-permute-done | bytes 92192 | tf_op jit(solution)/shard_map/ppermute | solution.py:587
  253.4 1.1 collective-permute-done.73.sb
  255.2 7.9 %shard_map.40 = (bf16[8,16,320]{2,1,0:T(8,128)(2,1)}, bf16[8,16,320]{2,1,0:T(8,128)(2,1)}, bf16[8,16,320]{2,1,0:T(8,128)(2,1)}, bf16[8,16,320]{2,1,0:T(8,128)(2,1)}) custom-call(s32[5]{0:T(128)} %stack.31.flags, bf16[528,320]{1,0:T(8,128)(2,1)} %get-tuple-element.129.block, bf16[144,320]{1,0:T(8,128)(2,1)} %copy-done.35, bf16[128,320]{1,0:T(8,128)(2,1)} %copy-done.36, ...), custom_call_target="tpu_custom_call" | custom-call | flops 1153433600 | bytes 4000000 | tf_op jit(solution)/shard_map/pallas_call | solution.py:539
  263.1 1.6 collective-permute-start.74
  264.6 1.5 collective-permute-start.75
  266.1 16.3 %collective-permute-start.76 = (bf16[8,16,320]{2,1,0:T(8,128)(2,1)}, bf16[8,16,320]{2,1,0:T(8,128)(2,1)S(1)}, u32[]{:S(2)}, u32[]{:S(2)}) collective-permute-start(bf16[8,16,320]{2,1,0:T(8,128)(2,1)} %get-tuple-element.135), channel_id=1, source_target_pairs={{0,24},{1,25},{2,26},{3,27},{4,28},{5,29},{6,30},{7,31},{8,8},{9,9... | collective-permute-start | bytes 245768 | tf_op jit(solution)/shard_map/ppermute | solution.py:583
  282.5 3.4 %collective-permute-done.76 = bf16[8,16,320]{2,1,0:T(8,128)(2,1)S(1)} collective-permute-done((bf16[8,16,320]{2,1,0:T(8,128)(2,1)}, bf16[8,16,320]{2,1,0:T(8,128)(2,1)S(1)}, u32[]{:S(2)}, u32[]{:S(2)}) %collective-permute-start.76) | collective-permute-done | bytes 81952 | tf_op jit(solution)/shard_map/ppermute | solution.py:583
  (282 shorter events, 45.9 us)
Async XLA Ops:
  4.7 9.4 %collective-permute-start.3 = (bf16[144,320]{1,0:T(8,128)(2,1)}, bf16[144,320]{1,0:T(8,128)(2,1)S(1)}, u32[]{:S(2)}, u32[]{:S(2)}) collective-permute-start(bf16[144,320]{1,0:T(8,128)(2,1)} %get-tuple-element.78), channel_id=1, source_target_pairs={{0,7},{1,2},{2,1},{3,4},{4,3},{5,6},{6,5},{7,0},{8,15},{9,10},{10,... | collective-permute-start | bytes 276488 | tf_op jit(solution)/shard_map/ppermute | solution.py:587
  8.1 7.0 %collective-permute-start.5 = (f32[8,320]{1,0:T(8,128)}, f32[8,320]{1,0:T(8,128)S(1)}, u32[]{:S(2)}, u32[]{:S(2)}) collective-permute-start(f32[8,320]{1,0:T(8,128)} %get-tuple-element.72), channel_id=1, source_target_pairs={{0,2},{1,7},{2,4},{3,1},{4,6},{5,3},{6,0},{7,5},{8,10},{9,15},{10,... | collective-permute-start | bytes 30728 | tf_op jit(solution)/shard_map/ppermute | solution.py:587
  8.1 7.0 %collective-permute-start.6 = (f32[8,320]{1,0:T(8,128)}, f32[8,320]{1,0:T(8,128)S(1)}, u32[]{:S(2)}, u32[]{:S(2)}) collective-permute-start(f32[8,320]{1,0:T(8,128)} %get-tuple-element.72), channel_id=1, source_target_pairs={{0,4},{1,5},{2,6},{3,7},{4,0},{5,1},{6,2},{7,3},{8,12},{9,13},{10,... | collective-permute-start | bytes 30728 | tf_op jit(solution)/shard_map/ppermute | solution.py:587
  11.1 9.4 %collective-permute-start = (bf16[80,1536]{1,0:T(8,128)(2,1)}, bf16[80,1536]{1,0:T(8,128)(2,1)S(1)}, u32[]{:S(2)}, u32[]{:S(2)}) collective-permute-start(bf16[80,1536]{1,0:T(8,128)(2,1)} %shard_map.29.rest_0_), channel_id=1, source_target_pairs={{0,2},{1,3},{2,0},{3,1},{4,6},{5,7},{6,4},{7,5},{8,10},{9,11},{10,... | collective-permute-start | bytes 737288 | tf_op jit(solution)/shard_map/ppermute | solution.py:587
  13.4 12.3 %collective-permute-start.1 = (bf16[80,1536]{1,0:T(8,128)(2,1)}, bf16[80,1536]{1,0:T(8,128)(2,1)S(1)}, u32[]{:S(2)}, u32[]{:S(2)}) collective-permute-start(bf16[80,1536]{1,0:T(8,128)(2,1)} %shard_map.29.rest_0_), channel_id=1, source_target_pairs={{0,4},{1,5},{2,6},{3,7},{4,0},{5,1},{6,2},{7,3},{8,12},{9,13},{10,... | collective-permute-start | bytes 737288 | tf_op jit(solution)/shard_map/ppermute | solution.py:587
  14.0 12.2 %collective-permute-start.2 = (bf16[80,1536]{1,0:T(8,128)(2,1)}, bf16[80,1536]{1,0:T(8,128)(2,1)S(1)}, u32[]{:S(2)}, u32[]{:S(2)}) collective-permute-start(bf16[80,1536]{1,0:T(8,128)(2,1)} %shard_map.29.rest_0_), channel_id=1, source_target_pairs={{0,6},{1,7},{2,4},{3,5},{4,2},{5,3},{6,0},{7,1},{8,14},{9,15},{10,... | collective-permute-start | bytes 737288 | tf_op jit(solution)/shard_map/ppermute | solution.py:587
  25.7 6.2 %collective-permute-start.10 = (bf16[80,1536]{1,0:T(8,128)(2,1)S(1)}, bf16[80,1536]{1,0:T(8,128)(2,1)S(1)}, u32[]{:S(2)}, u32[]{:S(2)}) collective-permute-start(bf16[80,1536]{1,0:T(8,128)(2,1)S(1)} %collective-permute-done.1.rest_2_), channel_id=1, source_target_pairs={{0,1},{1,0},{2,3},{3,2},{4,5},{5,4},{6,7},{7,6},{8,9},{9,8},{10,11... | collective-permute-start | bytes 737288 | tf_op jit(solution)/shard_map/ppermute | solution.py:587
  25.7 6.2 %collective-permute-start.8 = (bf16[80,1536]{1,0:T(8,128)(2,1)}, bf16[80,1536]{1,0:T(8,128)(2,1)S(1)}, u32[]{:S(2)}, u32[]{:S(2)}) collective-permute-start(bf16[80,1536]{1,0:T(8,128)(2,1)} %shard_map.29.rest_0_), channel_id=1, source_target_pairs={{0,1},{1,0},{2,3},{3,2},{4,5},{5,4},{6,7},{7,6},{8,9},{9,8},{10,11... | collective-permute-start | bytes 737288 | tf_op jit(solution)/shard_map/ppermute | solution.py:587
  26.2 5.7 %collective-permute-start.9 = (bf16[80,1536]{1,0:T(8,128)(2,1)S(1)}, bf16[80,1536]{1,0:T(8,128)(2,1)S(1)}, u32[]{:S(2)}, u32[]{:S(2)}) collective-permute-start(bf16[80,1536]{1,0:T(8,128)(2,1)S(1)} %collective-permute-done.rest_1_), channel_id=1, source_target_pairs={{0,1},{1,0},{2,3},{3,2},{4,5},{5,4},{6,7},{7,6},{8,9},{9,8},{10,11... | collective-permute-start | bytes 737288 | tf_op jit(solution)/shard_map/ppermute | solution.py:587
  26.2 5.7 %collective-permute-start.11 = (bf16[80,1536]{1,0:T(8,128)(2,1)S(1)}, bf16[80,1536]{1,0:T(8,128)(2,1)S(1)}, u32[]{:S(2)}, u32[]{:S(2)}) collective-permute-start(bf16[80,1536]{1,0:T(8,128)(2,1)S(1)} %collective-permute-done.2.rest_3_), channel_id=1, source_target_pairs={{0,1},{1,0},{2,3},{3,2},{4,5},{5,4},{6,7},{7,6},{8,9},{9,8},{10,11... | collective-permute-start | bytes 737288 | tf_op jit(solution)/shard_map/ppermute | solution.py:587
  28.4 3.5 %collective-permute-start.7 = (f32[8,320]{1,0:T(8,128)S(1)}, f32[8,320]{1,0:T(8,128)S(1)}, u32[]{:S(2)}, u32[]{:S(2)}) collective-permute-start(f32[8,320]{1,0:T(8,128)S(1)} %fusion.9.sa), channel_id=1, source_target_pairs={{0,1},{1,0},{2,3},{3,2},{4,5},{5,4},{6,7},{7,6},{8,9},{9,8},{10,11... | collective-permute-start | bytes 30728 | tf_op jit(solution)/shard_map/ppermute | solution.py:587
  40.4 8.6 %collective-permute-start.15 = (bf16[272,320]{1,0:T(8,128)(2,1)}, bf16[272,320]{1,0:T(8,128)(2,1)S(1)}, u32[]{:S(2)}, u32[]{:S(2)}) collective-permute-start(bf16[272,320]{1,0:T(8,128)(2,1)} %get-tuple-element.86), channel_id=1, source_target_pairs={{0,7},{1,2},{2,1},{3,4},{4,3},{5,6},{6,5},{7,0},{8,15},{9,10},{10,... | collective-permute-start | bytes 522248 | tf_op jit(solution)/shard_map/ppermute | solution.py:587
  40.8 18.6 %collective-permute-start.12 = (bf16[80,1536]{1,0:T(8,128)(2,1)S(1)}, bf16[80,1536]{1,0:T(8,128)(2,1)S(1)}, u32[]{:S(2)}, u32[]{:S(2)}) collective-permute-start(bf16[80,1536]{1,0:T(8,128)(2,1)S(1)} %copy-done.22), channel_id=1, source_target_pairs={{0,2},{1,3},{2,0},{3,1},{4,6},{5,7},{6,4},{7,5},{8,10},{9,11},{10,... | collective-permute-start | bytes 737288 | tf_op jit(solution)/shard_map/ppermute | solution.py:587
  42.3 17.1 %collective-permute-start.13 = (bf16[80,1536]{1,0:T(8,128)(2,1)S(1)}, bf16[80,1536]{1,0:T(8,128)(2,1)S(1)}, u32[]{:S(2)}, u32[]{:S(2)}) collective-permute-start(bf16[80,1536]{1,0:T(8,128)(2,1)S(1)} %copy-done.22), channel_id=1, source_target_pairs={{0,4},{1,5},{2,6},{3,7},{4,0},{5,1},{6,2},{7,3},{8,12},{9,13},{10,... | collective-permute-start | bytes 737288 | tf_op jit(solution)/shard_map/ppermute | solution.py:587
  43.2 14.4 %collective-permute-start.14 = (bf16[80,1536]{1,0:T(8,128)(2,1)S(1)}, bf16[80,1536]{1,0:T(8,128)(2,1)S(1)}, u32[]{:S(2)}, u32[]{:S(2)}) collective-permute-start(bf16[80,1536]{1,0:T(8,128)(2,1)S(1)} %copy-done.22), channel_id=1, source_target_pairs={{0,6},{1,7},{2,4},{3,5},{4,2},{5,3},{6,0},{7,1},{8,14},{9,15},{10,... | collective-permute-start | bytes 737288 | tf_op jit(solution)/shard_map/ppermute | solution.py:587
  44.6 13.9 %collective-permute-start.16 = (f32[8,320]{1,0:T(8,128)}, f32[8,320]{1,0:T(8,128)S(1)}, u32[]{:S(2)}, u32[]{:S(2)}) collective-permute-start(f32[8,320]{1,0:T(8,128)} %get-tuple-element.85), channel_id=1, source_target_pairs={{0,2},{1,7},{2,4},{3,1},{4,6},{5,3},{6,0},{7,5},{8,10},{9,15},{10,... | collective-permute-start | bytes 30728 | tf_op jit(solution)/shard_map/ppermute | solution.py:587
  49.1 9.5 %collective-permute-start.17 = (f32[8,320]{1,0:T(8,128)}, f32[8,320]{1,0:T(8,128)S(1)}, u32[]{:S(2)}, u32[]{:S(2)}) collective-permute-start(f32[8,320]{1,0:T(8,128)} %get-tuple-element.85), channel_id=1, source_target_pairs={{0,4},{1,5},{2,6},{3,7},{4,0},{5,1},{6,2},{7,3},{8,12},{9,13},{10,... | collective-permute-start | bytes 30728 | tf_op jit(solution)/shard_map/ppermute | solution.py:587
  57.5 3.9 %collective-permute-start.18 = (bf16[256,320]{1,0:T(8,128)(2,1)}, bf16[256,320]{1,0:T(8,128)(2,1)S(1)}, u32[]{:S(2)}, u32[]{:S(2)}) collective-permute-start(bf16[256,320]{1,0:T(8,128)(2,1)} %get-tuple-element.89), channel_id=1, source_target_pairs={{0,1},{1,0},{2,3},{3,2},{4,5},{5,4},{6,7},{7,6},{8,9},{9,8},{10,11... | collective-permute-start | bytes 491528 | tf_op jit(solution)/shard_map/ppermute | solution.py:587
  58.5 5.0 %collective-permute-start.23 = (bf16[80,1536]{1,0:T(8,128)(2,1)S(1)}, bf16[80,1536]{1,0:T(8,128)(2,1)S(1)}, u32[]{:S(2)}, u32[]{:S(2)}) collective-permute-start(bf16[80,1536]{1,0:T(8,128)(2,1)S(1)} %collective-permute-done.14.rest_6_.rest_11_), channel_id=1, source_target_pairs={{0,1},{1,0},{2,3},{3,2},{4,5},{5,4},{6,7},{7,6},{8,9},{9,8},{10,11... | collective-permute-start | bytes 737288 | tf_op jit(solution)/shard_map/ppermute | solution.py:587
  59.4 4.2 %collective-permute-start.20 = (bf16[80,1536]{1,0:T(8,128)(2,1)S(1)}, bf16[80,1536]{1,0:T(8,128)(2,1)S(1)}, u32[]{:S(2)}, u32[]{:S(2)}) collective-permute-start(bf16[80,1536]{1,0:T(8,128)(2,1)S(1)} %copy-done.22), channel_id=1, source_target_pairs={{0,1},{1,0},{2,3},{3,2},{4,5},{5,4},{6,7},{7,6},{8,9},{9,8},{10,11... | collective-permute-start | bytes 737288 | tf_op jit(solution)/shard_map/ppermute | solution.py:587
  59.9 2.6 collective-permute-start.19
  60.0 14.6 %collective-permute-start.24 = (bf16[80,3072]{1,0:T(8,128)(2,1)S(1)}, bf16[80,3072]{1,0:T(8,128)(2,1)S(1)}, u32[]{:S(2)}, u32[]{:S(2)}) collective-permute-start(bf16[80,3072]{1,0:T(8,128)(2,1)S(1)} %copy-done.6), channel_id=1, source_target_pairs={{0,2},{1,3},{2,0},{3,1},{4,6},{5,7},{6,4},{7,5},{8,10},{9,11},{10,... | collective-permute-start | bytes 1474568 | tf_op jit(solution)/shard_map/ppermute | solution.py:587
  61.4 22.4 %collective-permute-start.25 = (bf16[80,3072]{1,0:T(8,128)(2,1)S(1)}, bf16[80,3072]{1,0:T(8,128)(2,1)S(1)}, u32[]{:S(2)}, u32[]{:S(2)}) collective-permute-start(bf16[80,3072]{1,0:T(8,128)(2,1)S(1)} %copy-done.6), channel_id=1, source_target_pairs={{0,4},{1,5},{2,6},{3,7},{4,0},{5,1},{6,2},{7,3},{8,12},{9,13},{10,... | collective-permute-start | bytes 1474568 | tf_op jit(solution)/shard_map/ppermute | solution.py:587
  62.5 22.4 %collective-permute-start.26 = (bf16[80,3072]{1,0:T(8,128)(2,1)S(1)}, bf16[80,3072]{1,0:T(8,128)(2,1)S(1)}, u32[]{:S(2)}, u32[]{:S(2)}) collective-permute-start(bf16[80,3072]{1,0:T(8,128)(2,1)S(1)} %copy-done.6), channel_id=1, source_target_pairs={{0,6},{1,7},{2,4},{3,5},{4,2},{5,3},{6,0},{7,1},{8,14},{9,15},{10,... | collective-permute-start | bytes 1474568 | tf_op jit(solution)/shard_map/ppermute | solution.py:587
  83.8 2.6 collective-permute-start.28
  84.3 2.8 collective-permute-start.29
  84.9 3.0 %collective-permute-start.30 = (bf16[80,3072]{1,0:T(8,128)(2,1)S(1)}, bf16[80,3072]{1,0:T(8,128)(2,1)}, u32[]{:S(2)}, u32[]{:S(2)}) collective-permute-start(bf16[80,3072]{1,0:T(8,128)(2,1)S(1)} %collective-permute-done.26.rest_3_.rest_19_), channel_id=1, source_target_pairs={{0,1},{1,0},{2,3},{3,2},{4,5},{5,4},{6,7},{7,6},{8,9},{9,8},{10,11... | collective-permute-start | bytes 1474568 | tf_op jit(solution)/shard_map/ppermute | solution.py:587
  93.1 10.6 %collective-permute-start.31 = (bf16[144,640]{1,0:T(8,128)(2,1)}, bf16[144,640]{1,0:T(8,128)(2,1)}, u32[]{:S(2)}, u32[]{:S(2)}) collective-permute-start(bf16[144,640]{1,0:T(8,128)(2,1)} %get-tuple-element.99), channel_id=1, source_target_pairs={{0,8},{1,9},{2,10},{3,11},{4,12},{5,13},{6,14},{7,15},{8,0},{9,1},... | collective-permute-start | bytes 552968 | tf_op jit(solution)/shard_map/ppermute | solution.py:583
  98.5 48.2 %collective-permute-start.43 = (bf16[80,6144]{1,0:T(8,128)(2,1)S(1)}, bf16[80,6144]{1,0:T(8,128)(2,1)S(1)}, u32[]{:S(2)}, u32[]{:S(2)}) collective-permute-start(bf16[80,6144]{1,0:T(8,128)(2,1)S(1)} %copy-done), channel_id=1, source_target_pairs={{0,2},{1,3},{2,0},{3,1},{4,6},{5,7},{6,4},{7,5},{8,10},{9,11},{10,... | collective-permute-start | bytes 2949128 | tf_op jit(solution)/shard_map/ppermute | solution.py:587
  98.6 49.3 %collective-permute-start.44 = (bf16[80,6144]{1,0:T(8,128)(2,1)S(1)}, bf16[80,6144]{1,0:T(8,128)(2,1)S(1)}, u32[]{:S(2)}, u32[]{:S(2)}) collective-permute-start(bf16[80,6144]{1,0:T(8,128)(2,1)S(1)} %copy-done), channel_id=1, source_target_pairs={{0,4},{1,5},{2,6},{3,7},{4,0},{5,1},{6,2},{7,3},{8,12},{9,13},{10,... | collective-permute-start | bytes 2949128 | tf_op jit(solution)/shard_map/ppermute | solution.py:587
  105.5 18.6 %collective-permute-start.32 = (bf16[80,640]{1,0:T(8,128)(2,1)S(1)}, bf16[80,640]{1,0:T(8,128)(2,1)S(1)}, u32[]{:S(2)}, u32[]{:S(2)}) collective-permute-start(bf16[80,640]{1,0:T(8,128)(2,1)S(1)} %pad_maximum_fusion), channel_id=1, source_target_pairs={{0,7},{1,2},{2,1},{3,4},{4,3},{5,6},{6,5},{7,0},{8,15},{9,10},{10,... | collective-permute-start | bytes 307208 | tf_op jit(solution)/shard_map/ppermute | solution.py:587
  105.6 20.0 %collective-permute-start.34 = (f32[8,640]{1,0:T(8,128)S(1)}, f32[8,640]{1,0:T(8,128)S(1)}, u32[]{:S(2)}, u32[]{:S(2)}) collective-permute-start(f32[8,640]{1,0:T(8,128)S(1)} %maximum_maximum_fusion), channel_id=1, source_target_pairs={{0,2},{1,7},{2,4},{3,1},{4,6},{5,3},{6,0},{7,5},{8,10},{9,15},{10,... | collective-permute-start | bytes 61448 | tf_op jit(solution)/shard_map/ppermute | solution.py:587
  106.8 18.8 %collective-permute-start.35 = (f32[8,640]{1,0:T(8,128)S(1)}, f32[8,640]{1,0:T(8,128)S(1)}, u32[]{:S(2)}, u32[]{:S(2)}) collective-permute-start(f32[8,640]{1,0:T(8,128)S(1)} %maximum_maximum_fusion), channel_id=1, source_target_pairs={{0,4},{1,5},{2,6},{3,7},{4,0},{5,1},{6,2},{7,3},{8,12},{9,13},{10,... | collective-permute-start | bytes 61448 | tf_op jit(solution)/shard_map/ppermute | solution.py:587
  124.0 2.2 collective-permute-start.33
  128.6 17.2 %collective-permute-start.37 = (bf16[768,320]{0,1:T(8,128)(2,1)}, bf16[768,320]{0,1:T(8,128)(2,1)S(1)}, u32[]{:S(2)}, u32[]{:S(2)}) collective-permute-start(bf16[768,320]{0,1:T(8,128)(2,1)} %copy.10), channel_id=1, source_target_pairs={{0,24},{1,25},{2,26},{3,27},{4,28},{5,29},{6,30},{7,31},{8,8},{9,9... | collective-permute-start | bytes 1474568 | tf_op jit(solution)/shard_map/ppermute | solution.py:583
  134.0 28.0 %collective-permute-start.45 = (bf16[80,6144]{1,0:T(8,128)(2,1)S(1)}, bf16[80,6144]{1,0:T(8,128)(2,1)}, u32[]{:S(2)}, u32[]{:S(2)}) collective-permute-start(bf16[80,6144]{1,0:T(8,128)(2,1)S(1)} %copy-done), channel_id=1, source_target_pairs={{0,6},{1,7},{2,4},{3,5},{4,2},{5,3},{6,0},{7,1},{8,14},{9,15},{10,... | collective-permute-start | bytes 2949128 | tf_op jit(solution)/shard_map/ppermute | solution.py:587
  145.8 13.9 %collective-permute-start.38 = (bf16[80,640]{1,0:T(8,128)(2,1)}, bf16[80,640]{1,0:T(8,128)(2,1)S(1)}, u32[]{:S(2)}, u32[]{:S(2)}) collective-permute-start(bf16[80,640]{1,0:T(8,128)(2,1)} %get-tuple-element.111), channel_id=1, source_target_pairs={{0,7},{1,2},{2,1},{3,4},{4,3},{5,6},{6,5},{7,0},{8,15},{9,10},{10,... | collective-permute-start | bytes 307208 | tf_op jit(solution)/shard_map/ppermute | solution.py:587
  145.8 15.4 %collective-permute-start.40 = (f32[8,640]{1,0:T(8,128)}, f32[8,640]{1,0:T(8,128)S(1)}, u32[]{:S(2)}, u32[]{:S(2)}) collective-permute-start(f32[8,640]{1,0:T(8,128)} %get-tuple-element.113), channel_id=1, source_target_pairs={{0,2},{1,7},{2,4},{3,1},{4,6},{5,3},{6,0},{7,5},{8,10},{9,15},{10,... | collective-permute-start | bytes 61448 | tf_op jit(solution)/shard_map/ppermute | solution.py:587
  146.8 14.4 %collective-permute-start.41 = (f32[8,640]{1,0:T(8,128)}, f32[8,640]{1,0:T(8,128)S(1)}, u32[]{:S(2)}, u32[]{:S(2)}) collective-permute-start(f32[8,640]{1,0:T(8,128)} %get-tuple-element.113), channel_id=1, source_target_pairs={{0,4},{1,5},{2,6},{3,7},{4,0},{5,1},{6,2},{7,3},{8,12},{9,13},{10,... | collective-permute-start | bytes 61448 | tf_op jit(solution)/shard_map/ppermute | solution.py:587
  147.9 18.7 %collective-permute-start.46 = (bf16[80,6144]{1,0:T(8,128)(2,1)S(1)}, bf16[80,6144]{1,0:T(8,128)(2,1)S(1)}, u32[]{:S(2)}, u32[]{:S(2)}) collective-permute-start(bf16[80,6144]{1,0:T(8,128)(2,1)S(1)} %copy-done), channel_id=1, source_target_pairs={{0,1},{1,0},{2,3},{3,2},{4,5},{5,4},{6,7},{7,6},{8,9},{9,8},{10,11... | collective-permute-start | bytes 2949128 | tf_op jit(solution)/shard_map/ppermute | solution.py:587
  159.7 7.0 %collective-permute-start.47 = (bf16[80,6144]{1,0:T(8,128)(2,1)S(1)}, bf16[80,6144]{1,0:T(8,128)(2,1)S(1)}, u32[]{:S(2)}, u32[]{:S(2)}) collective-permute-start(bf16[80,6144]{1,0:T(8,128)(2,1)S(1)} %collective-permute-done.43.rest_2_.rest_1_), channel_id=1, source_target_pairs={{0,1},{1,0},{2,3},{3,2},{4,5},{5,4},{6,7},{7,6},{8,9},{9,8},{10,11... | collective-permute-start | bytes 2949128 | tf_op jit(solution)/shard_map/ppermute | solution.py:587
  161.2 5.5 %collective-permute-start.48 = (bf16[80,6144]{1,0:T(8,128)(2,1)S(1)}, bf16[80,6144]{1,0:T(8,128)(2,1)S(1)}, u32[]{:S(2)}, u32[]{:S(2)}) collective-permute-start(bf16[80,6144]{1,0:T(8,128)(2,1)S(1)} %collective-permute-done.44.rest_3_.rest_2_), channel_id=1, source_target_pairs={{0,1},{1,0},{2,3},{3,2},{4,5},{5,4},{6,7},{7,6},{8,9},{9,8},{10,11... | collective-permute-start | bytes 2949128 | tf_op jit(solution)/shard_map/ppermute | solution.py:587
  162.0 7.0 %collective-permute-start.49 = (bf16[80,6144]{1,0:T(8,128)(2,1)}, bf16[80,6144]{1,0:T(8,128)(2,1)}, u32[]{:S(2)}, u32[]{:S(2)}) collective-permute-start(bf16[80,6144]{1,0:T(8,128)(2,1)} %collective-permute-done.45.rest_4_.rest_3_), channel_id=1, source_target_pairs={{0,1},{1,0},{2,3},{3,2},{4,5},{5,4},{6,7},{7,6},{8,9},{9,8},{10,11... | collective-permute-start | bytes 2949128 | tf_op jit(solution)/shard_map/ppermute | solution.py:587
  162.6 2.9 %collective-permute-start.39 = (bf16[64,640]{1,0:T(8,128)(2,1)}, bf16[64,640]{1,0:T(8,128)(2,1)S(1)}, u32[]{:S(2)}, u32[]{:S(2)}) collective-permute-start(bf16[64,640]{1,0:T(8,128)(2,1)} %get-tuple-element.112), channel_id=1, source_target_pairs={{0,1},{1,0},{2,3},{3,2},{4,5},{5,4},{6,7},{7,6},{8,9},{9,8},{10,11... | collective-permute-start | bytes 245768 | tf_op jit(solution)/shard_map/ppermute | solution.py:587
  177.9 6.1 %collective-permute-start.51 = (bf16[80,640]{1,0:T(8,128)(2,1)S(1)}, bf16[80,640]{1,0:T(8,128)(2,1)S(1)}, u32[]{:S(2)}, u32[]{:S(2)}) collective-permute-start(bf16[80,640]{1,0:T(8,128)(2,1)S(1)} %pad_maximum_fusion.1), channel_id=1, source_target_pairs={{0,7},{1,2},{2,1},{3,4},{4,3},{5,6},{6,5},{7,0},{8,15},{9,10},{10,... | collective-permute-start | bytes 307208 | tf_op jit(solution)/shard_map/ppermute | solution.py:587
  179.3 5.2 %collective-permute-start.53 = (f32[8,640]{1,0:T(8,128)S(1)}, f32[8,640]{1,0:T(8,128)S(1)}, u32[]{:S(2)}, u32[]{:S(2)}) collective-permute-start(f32[8,640]{1,0:T(8,128)S(1)} %maximum_maximum_fusion.1), channel_id=1, source_target_pairs={{0,2},{1,7},{2,4},{3,1},{4,6},{5,3},{6,0},{7,5},{8,10},{9,15},{10,... | collective-permute-start | bytes 61448 | tf_op jit(solution)/shard_map/ppermute | solution.py:587
  180.0 4.5 %collective-permute-start.54 = (f32[8,640]{1,0:T(8,128)S(1)}, f32[8,640]{1,0:T(8,128)S(1)}, u32[]{:S(2)}, u32[]{:S(2)}) collective-permute-start(f32[8,640]{1,0:T(8,128)S(1)} %maximum_maximum_fusion.1), channel_id=1, source_target_pairs={{0,4},{1,5},{2,6},{3,7},{4,0},{5,1},{6,2},{7,3},{8,12},{9,13},{10,... | collective-permute-start | bytes 61448 | tf_op jit(solution)/shard_map/ppermute | solution.py:587
  181.1 3.6 %collective-permute-start.52 = (bf16[64,640]{1,0:T(8,128)(2,1)S(1)}, bf16[64,640]{1,0:T(8,128)(2,1)S(1)}, u32[]{:S(2)}, u32[]{:S(2)}) collective-permute-start(bf16[64,640]{1,0:T(8,128)(2,1)S(1)} %get-tuple-element.141), channel_id=1, source_target_pairs={{0,1},{1,0},{2,3},{3,2},{4,5},{5,4},{6,7},{7,6},{8,9},{9,8},{10,11... | collective-permute-start | bytes 245768 | tf_op jit(solution)/shard_map/ppermute | solution.py:587
  193.6 6.5 %collective-permute-start.56 = (bf16[80,640]{1,0:T(8,128)(2,1)}, bf16[80,640]{1,0:T(8,128)(2,1)S(1)}, u32[]{:S(2)}, u32[]{:S(2)}) collective-permute-start(bf16[80,640]{1,0:T(8,128)(2,1)} %get-tuple-element.120), channel_id=1, source_target_pairs={{0,7},{1,2},{2,1},{3,4},{4,3},{5,6},{6,5},{7,0},{8,15},{9,10},{10,... | collective-permute-start | bytes 307208 | tf_op jit(solution)/shard_map/ppermute | solution.py:587
  194.9 5.3 %collective-permute-start.58 = (f32[8,640]{1,0:T(8,128)}, f32[8,640]{1,0:T(8,128)S(1)}, u32[]{:S(2)}, u32[]{:S(2)}) collective-permute-start(f32[8,640]{1,0:T(8,128)} %get-tuple-element.122), channel_id=1, source_target_pairs={{0,2},{1,7},{2,4},{3,1},{4,6},{5,3},{6,0},{7,5},{8,10},{9,15},{10,... | collective-permute-start | bytes 61448 | tf_op jit(solution)/shard_map/ppermute | solution.py:587
  195.4 4.8 %collective-permute-start.59 = (f32[8,640]{1,0:T(8,128)}, f32[8,640]{1,0:T(8,128)S(1)}, u32[]{:S(2)}, u32[]{:S(2)}) collective-permute-start(f32[8,640]{1,0:T(8,128)} %get-tuple-element.122), channel_id=1, source_target_pairs={{0,4},{1,5},{2,6},{3,7},{4,0},{5,1},{6,2},{7,3},{8,12},{9,13},{10,... | collective-permute-start | bytes 61448 | tf_op jit(solution)/shard_map/ppermute | solution.py:587
  196.5 4.7 %collective-permute-start.57 = (bf16[64,640]{1,0:T(8,128)(2,1)}, bf16[64,640]{1,0:T(8,128)(2,1)S(1)}, u32[]{:S(2)}, u32[]{:S(2)}) collective-permute-start(bf16[64,640]{1,0:T(8,128)(2,1)} %get-tuple-element.121), channel_id=1, source_target_pairs={{0,1},{1,0},{2,3},{3,2},{4,5},{5,4},{6,7},{7,6},{8,9},{9,8},{10,11... | collective-permute-start | bytes 245768 | tf_op jit(solution)/shard_map/ppermute | solution.py:587
  211.7 6.1 %collective-permute-start.62 = (bf16[80,640]{1,0:T(8,128)(2,1)S(1)}, bf16[80,640]{1,0:T(8,128)(2,1)S(1)}, u32[]{:S(2)}, u32[]{:S(2)}) collective-permute-start(bf16[80,640]{1,0:T(8,128)(2,1)S(1)} %pad_maximum_fusion.2), channel_id=1, source_target_pairs={{0,7},{1,2},{2,1},{3,4},{4,3},{5,6},{6,5},{7,0},{8,15},{9,10},{10,... | collective-permute-start | bytes 307208 | tf_op jit(solution)/shard_map/ppermute | solution.py:587
  227.5 6.1 %collective-permute-start.64 = (bf16[144,320]{1,0:T(8,128)(2,1)}, bf16[144,320]{1,0:T(8,128)(2,1)S(1)}, u32[]{:S(2)}, u32[]{:S(2)}) collective-permute-start(bf16[144,320]{1,0:T(8,128)(2,1)} %get-tuple-element.126), channel_id=1, source_target_pairs={{0,7},{1,2},{2,1},{3,4},{4,3},{5,6},{6,5},{7,0},{8,15},{9,10},{10,... | collective-permute-start | bytes 276488 | tf_op jit(solution)/shard_map/ppermute | solution.py:587
  228.3 5.4 %collective-permute-start.66 = (f32[8,320]{1,0:T(8,128)}, f32[8,320]{1,0:T(8,128)S(1)}, u32[]{:S(2)}, u32[]{:S(2)}) collective-permute-start(f32[8,320]{1,0:T(8,128)} %get-tuple-element.128), channel_id=1, source_target_pairs={{0,2},{1,7},{2,4},{3,1},{4,6},{5,3},{6,0},{7,5},{8,10},{9,15},{10,... | collective-permute-start | bytes 30728 | tf_op jit(solution)/shard_map/ppermute | solution.py:587
  228.7 4.9 %collective-permute-start.67 = (f32[8,320]{1,0:T(8,128)}, f32[8,320]{1,0:T(8,128)S(1)}, u32[]{:S(2)}, u32[]{:S(2)}) collective-permute-start(f32[8,320]{1,0:T(8,128)} %get-tuple-element.128), channel_id=1, source_target_pairs={{0,4},{1,5},{2,6},{3,7},{4,0},{5,1},{6,2},{7,3},{8,12},{9,13},{10,... | collective-permute-start | bytes 30728 | tf_op jit(solution)/shard_map/ppermute | solution.py:587
  229.8 4.6 %collective-permute-start.65 = (bf16[128,320]{1,0:T(8,128)(2,1)}, bf16[128,320]{1,0:T(8,128)(2,1)S(1)}, u32[]{:S(2)}, u32[]{:S(2)}) collective-permute-start(bf16[128,320]{1,0:T(8,128)(2,1)} %get-tuple-element.127), channel_id=1, source_target_pairs={{0,1},{1,0},{2,3},{3,2},{4,5},{5,4},{6,7},{7,6},{8,9},{9,8},{10,11... | collective-permute-start | bytes 245768 | tf_op jit(solution)/shard_map/ppermute | solution.py:587
  246.0 6.5 %collective-permute-start.69 = (bf16[144,320]{1,0:T(8,128)(2,1)}, bf16[144,320]{1,0:T(8,128)(2,1)S(1)}, u32[]{:S(2)}, u32[]{:S(2)}) collective-permute-start(bf16[144,320]{1,0:T(8,128)(2,1)} %get-tuple-element.130), channel_id=1, source_target_pairs={{0,7},{1,2},{2,1},{3,4},{4,3},{5,6},{6,5},{7,0},{8,15},{9,10},{10,... | collective-permute-start | bytes 276488 | tf_op jit(solution)/shard_map/ppermute | solution.py:587
  247.3 5.3 %collective-permute-start.71 = (f32[8,320]{1,0:T(8,128)}, f32[8,320]{1,0:T(8,128)S(1)}, u32[]{:S(2)}, u32[]{:S(2)}) collective-permute-start(f32[8,320]{1,0:T(8,128)} %get-tuple-element.132), channel_id=1, source_target_pairs={{0,2},{1,7},{2,4},{3,1},{4,6},{5,3},{6,0},{7,5},{8,10},{9,15},{10,... | collective-permute-start | bytes 30728 | tf_op jit(solution)/shard_map/ppermute | solution.py:587
  247.9 4.7 %collective-permute-start.72 = (f32[8,320]{1,0:T(8,128)}, f32[8,320]{1,0:T(8,128)S(1)}, u32[]{:S(2)}, u32[]{:S(2)}) collective-permute-start(f32[8,320]{1,0:T(8,128)} %get-tuple-element.132), channel_id=1, source_target_pairs={{0,4},{1,5},{2,6},{3,7},{4,0},{5,1},{6,2},{7,3},{8,12},{9,13},{10,... | collective-permute-start | bytes 30728 | tf_op jit(solution)/shard_map/ppermute | solution.py:587
  248.8 4.6 %collective-permute-start.70 = (bf16[128,320]{1,0:T(8,128)(2,1)}, bf16[128,320]{1,0:T(8,128)(2,1)S(1)}, u32[]{:S(2)}, u32[]{:S(2)}) collective-permute-start(bf16[128,320]{1,0:T(8,128)(2,1)} %get-tuple-element.131), channel_id=1, source_target_pairs={{0,1},{1,0},{2,3},{3,2},{4,5},{5,4},{6,7},{7,6},{8,9},{9,8},{10,11... | collective-permute-start | bytes 245768 | tf_op jit(solution)/shard_map/ppermute | solution.py:587
  263.1 19.4 %collective-permute-start.74 = (bf16[8,16,320]{2,1,0:T(8,128)(2,1)}, bf16[8,16,320]{2,1,0:T(8,128)(2,1)S(1)}, u32[]{:S(2)}, u32[]{:S(2)}) collective-permute-start(bf16[8,16,320]{2,1,0:T(8,128)(2,1)} %get-tuple-element.133), channel_id=1, source_target_pairs={{0,0},{1,1},{2,2},{3,3},{4,4},{5,5},{6,6},{7,7},{8,8},{9,9},{10,10... | collective-permute-start | bytes 245768 | tf_op jit(solution)/shard_map/ppermute | solution.py:583
  264.6 17.9 %collective-permute-start.75 = (bf16[8,16,320]{2,1,0:T(8,128)(2,1)}, bf16[8,16,320]{2,1,0:T(8,128)(2,1)S(1)}, u32[]{:S(2)}, u32[]{:S(2)}) collective-permute-start(bf16[8,16,320]{2,1,0:T(8,128)(2,1)} %get-tuple-element.134), channel_id=1, source_target_pairs={{0,0},{1,1},{2,2},{3,3},{4,4},{5,5},{6,6},{7,7},{8,24},{9,25},{10,... | collective-permute-start | bytes 245768 | tf_op jit(solution)/shard_map/ppermute | solution.py:583
  266.1 19.7 %collective-permute-start.76 = (bf16[8,16,320]{2,1,0:T(8,128)(2,1)}, bf16[8,16,320]{2,1,0:T(8,128)(2,1)S(1)}, u32[]{:S(2)}, u32[]{:S(2)}) collective-permute-start(bf16[8,16,320]{2,1,0:T(8,128)(2,1)} %get-tuple-element.135), channel_id=1, source_target_pairs={{0,24},{1,25},{2,26},{3,27},{4,28},{5,29},{6,30},{7,31},{8,8},{9,9... | collective-permute-start | bytes 245768 | tf_op jit(solution)/shard_map/ppermute | solution.py:583
  (78 other events, 395.4 us)

commit v2 on v1

--- a/solution.py
+++ b/solution.py
@@ -11,6 +11,7 @@
 GROUPS = 32
 EPSILON = 1e-05
 TAIL = 16
+RELAYED = (2, 3)
 BF16 = jnp.bfloat16
 F32 = jnp.float32
 
@@ -122,32 +123,26 @@
 
 
 class Weights:
-    def __init__(self, shape, bounds, start, c_in, c_out):
+    def __init__(self, shape, entries, start, c_in, c_out):
         self.shape = shape
         self.c_in = c_in
         self.c_out = c_out
         self.split = c_out != shape.wide
         self.blocks = 3 * c_in * c_out // shape.wide // shape.blk
         self.start = start // shape.blk
-        self.bounds = bounds
+        self.entries = entries
         self.depth = self.blocks * shape.lanes
         self.width = (2 if self.split else 1) * self.depth
 
-    def stacks(self, refs):
-        refs = list(refs)
-        return {low: [refs.pop(0) for _ in owners] for low, _, owners in self.bounds}
-
-    def copies(self, flags, stack_refs, buffer, sems):
+    def copies(self, flags, refs, buffer, sems):
         made = []
         lanes = self.shape.lanes
         for dy in range(3):
             mine = []
             begin = self.start + dy * self.blocks
-            for low, high, owners in self.bounds:
+            for ref, (owner, low, high) in zip(refs, self.entries, strict=True):
                 a, b = max(begin, low), min(begin + self.blocks, high)
-                if a >= b:
-                    continue
-                for ref, owner in zip(stack_refs[low], owners, strict=True):
+                if a < b:
                     mine.append(
                         pltpu.make_async_copy(
                             ref.at[:, (a - low) * lanes : (b - low) * lanes],
@@ -276,7 +271,7 @@
         rest = rest[extra + n_pieces :]
         outs = rest[:-4]
         buffer, image, acc, sems = rest[-4:]
-        copies = weights.copies(flags, weights.stacks(piece_refs), buffer, sems)
+        copies = weights.copies(flags, piece_refs, buffer, sems)
         for mine in copies:
             for copy in mine:
                 copy.start()
@@ -304,9 +299,10 @@
             for row in range(out_rows):
                 own, _ = ext_row(row, res[0], res[1], res[2], flags, rows, out_halo, width)
                 span = slice(row * width, (row + 1) * width)
-                out_ref[span, :] = (own + acc[span, :] * scale).astype(BF16)
-
-    outs = message_outs(rows, width, c, keep) if residual is None else [((out_rows * width, c), BF16)]
+                out_ref[span, 0:c] = (own + acc[span, :] * scale).astype(BF16)
+                out_ref[span, c:] = jnp.zeros((width, out_ref.shape[1] - c), BF16)
+
+    outs = message_outs(rows, width, c, keep) if residual is None else [((out_rows * width, -(-c // 128) * 128), BF16)]
     args = (flags,) + tuple(got) + (() if residual is None else tuple(residual)) + tuple(pieces)
     flops = 2 * out_rows * width * 9 * c * c
     return call(body, 1, 5 + extra, n_pieces, outs, scratch_of(weights, image_rows, out_rows, width), flops)(*args)
@@ -320,13 +316,13 @@
         piece_refs = rest[: len(pieces)]
         outs = rest[len(pieces) : -4]
         buffer, image, acc, sems = rest[-4:]
-        copies = weights.copies(flags, weights.stacks(piece_refs), buffer, sems)
+        copies = weights.copies(flags, piece_refs, buffer, sems)
         for mine in copies:
             for copy in mine:
                 copy.start()
         weights.clear(image)
         for row in range(rows + 1):
-            value = skip_ref[row * width : (row + 1) * width, :].astype(F32)
+            value = skip_ref[row * width : (row + 1) * width, 0:c].astype(F32)
             if row == 0:
                 value = masked(value, flags[1] != 0)
             even, odd = value[:half], value[half:]
@@ -358,7 +354,7 @@
         piece_refs = rest[extra : extra + len(pieces)]
         outs = rest[extra + len(pieces) : -4]
         buffer, image, acc, sems = rest[-4:]
-        copies = weights.copies(flags, weights.stacks(piece_refs), buffer, sems)
+        copies = weights.copies(flags, piece_refs, buffer, sems)
         for mine in copies:
             for copy in mine:
                 copy.start()
@@ -393,7 +389,7 @@
         piece_refs = rest[: len(pieces)]
         outs = rest[len(pieces) : -4]
         buffer, image, acc, sems = rest[-4:]
-        copies = weights.copies(flags, weights.stacks(piece_refs), buffer, sems)
+        copies = weights.copies(flags, piece_refs, buffer, sems)
         for mine in copies:
             for copy in mine:
                 copy.start()
@@ -414,7 +410,7 @@
         out_ref, outer_ref, inner_ref, stats_ref = outs
         value = (acc[...] * (1.0 / math.sqrt(9 * c))).astype(BF16)
         out_ref[0 : rows * width, :] = value
-        own = skip_ref[width : (rows + 1) * width, :].astype(F32)
+        own = skip_ref[width : (rows + 1) * width, 0:c_out].astype(F32)
         sums = moments_of(value.astype(F32)) + moments_of(own)
         emit(flags, out_ref, outer_ref, inner_ref, stats_ref, keep, rows, width, sums)
 
@@ -431,7 +427,7 @@
         piece_refs = rest[: len(pieces)]
         outs = rest[len(pieces) : -4]
         buffer, image, acc, sems = rest[-4:]
-        copies = weights.copies(flags, weights.stacks(piece_refs), buffer, sems)
+        copies = weights.copies(flags, piece_refs, buffer, sems)
         for mine in copies:
             for copy in mine:
                 copy.start()
@@ -448,7 +444,7 @@
                 if part == 0:
                     value, outside = ext_row(row, block, outer, inner, flags, rows, 1, width)
                 else:
-                    value = skip_ref[row * width : (row + 1) * width, :].astype(F32)
+                    value = skip_ref[row * width : (row + 1) * width, 0:c].astype(F32)
                     outside = flags[1] != 0 if row == 0 else flags[2] != 0 if row == rows + 1 else None
                 value = masked(silu((value - mean) * inv), outside).astype(BF16)
                 value = jnp.dot(value, mix, preferred_element_type=F32)
@@ -488,19 +484,18 @@
         piece_refs = rest[: len(pieces)]
         outs = rest[len(pieces) : -6]
         buffer, image, acc, sems, jbuf, jsem = rest[-6:]
-        copies = weights.copies(flags, weights.stacks(piece_refs), buffer, sems)
+        copies = weights.copies(flags, piece_refs, buffer, sems)
         for mine in copies:
             for copy in mine:
                 copy.start()
         weights.clear(image)
-        for low, high, owners in weights.bounds:
+        for ref, (owner, low, high) in zip(piece_refs, weights.entries, strict=True):
             if low <= j_block < high:
-                for ref, owner in zip(weights.stacks(piece_refs)[low], owners, strict=True):
-                    pltpu.make_async_copy(
-                        ref.at[:, (j_block - low) * shape.lanes : (j_block - low + 1) * shape.lanes],
-                        jbuf.at[owner(flags)],
-                        jsem,
-                    ).start()
+                pltpu.make_async_copy(
+                    ref.at[:, (j_block - low) * shape.lanes : (j_block - low + 1) * shape.lanes],
+                    jbuf.at[owner(flags)],
+                    jsem,
+                ).start()
         mean, inv = group_terms(sa[...] + sb[...], shape.fine_count)
         mix = parity_matrix(c)
 
@@ -515,7 +510,7 @@
         run_conv(weights, buffer, image, acc, sems, rows, width)
         pltpu.make_async_copy(jbuf, jbuf, jsem).wait()
         right = jbuf[...].reshape(2 * c, shape.lanes)
-        left = [u_ref[0 : rows * width, :], skip_ref[width : (rows + 1) * width, :]]
+        left = [u_ref[0 : rows * width, :], skip_ref[width : (rows + 1) * width, 0:c]]
         left = [jnp.dot(part, mix, preferred_element_type=F32).astype(BF16) for part in left]
         made = jnp.zeros((rows * width, c), F32)
         for odd in range(2):
@@ -576,9 +571,8 @@
     def permute(value, source, target, move):
         if source == target:
             return within(value, move)
-        other = {source: target, target: source}
         pairs = [
-            (s * n + i, other[s] * n + move(i) if s in other else s * n + i) for s in range(n_section) for i in range(n)
+            (s * n + i, (s + target - source) % n_section * n + move(i)) for s in range(n_section) for i in range(n)
         ]
         return lax.ppermute(value, ("section", "space"), pairs)
 
@@ -639,7 +633,7 @@
         low, high = bounds[number]
         if n == 8:
             got = [after(packed[number], *deps)]
-            for k in range(1, 4):
+            for k in range(1, 3 if number in RELAYED else 4):
                 got.append(within(got[0], lambda i, k=k: i ^ (2 * k)))
             return got
         got = lax.all_gather(pack[low * shape.blk : high * shape.blk], "space")
@@ -648,27 +642,34 @@
         got = jnp.pad(got, ((0, 0), (0, 0), (0, 0), (0, shape.lanes - shape.blk)))
         return list(got.reshape(shape.m, shape.cols_of, -1))
 
-    def finish(number, got, *deps, last_dep=None):
-        if n == 8:
-            early, late = list(got[:3]), list(got[3:])
-            if last_dep is not None:
-                late = after(late, last_dep)
-            if deps:
-                early = after(early, *deps)
-            got = early + late
-            shared = [within(part, partner) for part in got]
-            near = [lambda flags, j=j: ((flags[4] // 2) ^ j) * 2 + flags[0] for j in range(4)]
-            far = [lambda flags, j=j: ((flags[4] // 2) ^ j) * 2 + 1 - flags[0] for j in range(4)]
-            pieces[number] = (list(got) + shared, near + far)
-        else:
-            pieces[number] = (got, [lambda flags, j=j: j for j in range(shape.m)])
-
-    def weights(start, c_in, c_out):
+    def relay(got, *deps):
+        if n != 8:
+            return []
+        half = got[1].shape[1] // 2
+        first, second = after((got[1][:, :half], got[2][:, half:]), *deps)
+        made = []
+        for k, part in ((2, first), (1, second)):
+            made.append(within(part, lambda i, k=k: i ^ (2 * k)))
+        return made
+
+    def share(number, got, first=0):
+        low, high = bounds[number]
+        middle = (low + high) // 2
+        spans = [(low, high)] * len(got) if n != 8 or first == 0 else [(low, middle), (middle, high)]
+        mine = pieces.setdefault(number, [])
+        for place, (part, span) in enumerate(zip(got, spans, strict=True)):
+            if n == 8:
+                j = min(first + place, 3)
+                mine.append((part, lambda flags, j=j: ((flags[4] // 2) ^ j) * 2 + flags[0]) + span)
+                mine.append((within(part, partner), lambda flags, j=j: ((flags[4] // 2) ^ j) * 2 + 1 - flags[0]) + span)
+            else:
+                mine.append((part, lambda flags, j=place: j) + span)
+
+    def weights(start, c_in, c_out, extra=0):
         first = start // shape.blk
         end = (start + 9 * c_in * c_out // shape.wide) // shape.blk
-        used = [i for i, (a, b) in enumerate(bounds) if a < end and b > first]
-        made = Weights(shape, [bounds[i] + (pieces[i][1],) for i in used], start, c_in, c_out)
-        return made, [stack for i in used for stack in pieces[i][0]]
+        used = [e for number in sorted(pieces) for e in pieces[number] if e[2] < end + extra and e[3] > first]
+        return Weights(shape, [e[1:] for e in used], start, c_in, c_out), [e[0] for e in used]
 
     narrow, wide = shape.narrow, shape.wide
     x = features[0].reshape(shape.rows, shape.half, 2, narrow).transpose(0, 2, 1, 3).reshape(-1, narrow)
@@ -677,37 +678,46 @@
     if n == 8:
         packed += pack_blocks(shape, after(pack.T, sent[0]), bounds[1:])
     first = exchange(ready, 0, 0)
-    finish(0, sent, first[3])
+    sent = after(sent, first[3])
+    share(0, sent)
     sent = send(1, sent)
     first = (after(first[0], sent[0]),) + first[1:]
     hidden = fine_conv(shape, flags, *weights(0, narrow, narrow), first, 1, 0, 2)
     second = exchange(hidden, 0, 0)
-    finish(1, sent, second[3])
-    sent = send(2, sent, second[3])
+    sent = after(sent, second[3])
+    share(1, sent)
+    sent = send(2, sent)
     second = (after(second[0], sent[0]),) + second[1:]
     (skip,) = fine_conv(shape, flags, *weights(9 * q_rows, narrow, narrow), second, 2, 1, 0, residual=first[:3])
-    finish(2, sent, skip)
+    sent = after(sent, skip)
+    opposite = relay(sent)
+    share(2, sent)
+    share(2, opposite, 3)
     sent = send(3, sent)
     skip = after(skip, sent[0])
     coarse = down_conv(shape, flags, *weights(18 * q_rows, narrow, wide), skip, 1)
     for section in (1, 2):
         got = exchange(coarse, section - 1, section)
         if section == 1:
+            opposite = relay(sent, got[3])
             skip, got = lax.optimization_barrier((skip, got))
             skip = permute(skip, 0, n_section - 1, lambda i: i)
         hidden = coarse_conv(shape, flags, *weights(0, wide, wide), got, 1)
         if section == 1:
+            share(3, after(sent, hidden[3]))
             hidden, skip = lax.optimization_barrier((hidden, skip))
         then = exchange(hidden, section, section)
         if section == 1:
-            finish(3, sent, hidden[3], last_dep=then[3])
+            share(3, after(opposite, then[3]), 3)
         coarse = coarse_conv(shape, flags, *weights(36 * q_rows, wide, wide), then, 1, residual=got[0])
     got = exchange(coarse, 2, 3, with_stats=False)
     up = up_conv(shape, flags, *weights(0, wide, narrow), got, skip, 1)
     got = exchange(up, 3, 3, count=4)
     hidden = join_conv(shape, flags, *weights(18 * q_rows, wide, narrow), got, skip, 1)
     then = exchange(hidden, 3, 3)
-    outs = last_conv(shape, flags, *weights(36 * q_rows, narrow, narrow), then, got[0], skip, 45 * q_rows, n_section)
+    outs = last_conv(
+        shape, flags, *weights(36 * q_rows, narrow, narrow, 1), then, got[0], skip, 45 * q_rows, n_section
+    )
     result = outs[3]
     for target in range(3):
         result = jnp.where(section_id == target, permute(outs[target], 3, target, lambda i: i), result)

time: 288 us -> 282 us (0.979)
  the two profiles are of different devices: /device:TPU:0 before, /device:TPU:16 now
where the time goes in v2:
time: 282 us; the launch traced here: 281 us
  waiting for transfers between devices  113 us (40%)
  Pallas kernels  83.1 us (29%)
  starting transfers between devices  64.6 us (23%)
  local copies, waits for them, and re-layouts  14 us (5%)
  other arithmetic  4.74 us (2%)
    ppermute x74, waiting for transfers between devices, within(): return lax.ppermute(value, ('section', 'space'), pairs)  85.6 us
    ppermute x74, starting transfers between devices, within(): return lax.ppermute(value, ('section', 'space'), pairs)  50.8 us
    pallas_call x4, Pallas kernels, coarse_conv(): call(body, 1, 5 + extra, len(pieces), outs, scratch_of(weights, rows + 2,...  29.1 us
    ppermute x7, waiting for transfers between devices, permute(): return lax.ppermute(value, ('section', 'space'), pairs)  27.7 us
    pallas_call x2, Pallas kernels, fine_conv(): call(body, 1, 5 + extra, n_pieces, outs, scratch_of(weights, image_rows,...  15.1 us
    ppermute x7, starting transfers between devices, permute(): return lax.ppermute(value, ('section', 'space'), pairs)  13.8 us
    unnamed x151, local copies, waits for them, and re-layouts  11.5 us
    pallas_call x1, Pallas kernels, join_conv(): call(body, 1, 6, len(pieces), outs, scratch, flops)  9.79 us
  transfers between devices with their start and end apart: 81, of which 43 were waited for; matrix products, arithmetic and copies ran while one was open for 1% of the time, Pallas kernels for 7%

profile of v2, /device:TPU:16, one launch (start us, length us, event | category | flops | bytes accessed | tf_op | source)
XLA Modules:
  0.0 280.7 jit_solution(2418108556095813444)
XLA Ops:
  0.0 1.2 copy.5
  2.7 2.0 shard_map.28
  4.7 1.9 collective-permute-start.3
  6.7 1.2 collective-permute-start.5
  7.9 1.8 shard_map.29.rest_0_
  9.7 2.4 collective-permute-start
  13.8 5.3 %collective-permute-done.rest_2_ = bf16[80,1536]{1,0:T(8,128)(2,1)S(1)} collective-permute-done((bf16[80,1536]{1,0:T(8,128)(2,1)}, bf16[80,1536]{1,0:T(8,128)(2,1)S(1)}, u32[]{:S(2)}, u32[]{:S(2)}) %collective-permute-start) | collective-permute-done | bytes 245792 | tf_op jit(solution)/shard_map/ppermute | solution.py:581
  19.1 5.3 %collective-permute-done.1.rest_4_ = bf16[80,1536]{1,0:T(8,128)(2,1)S(1)} collective-permute-done((bf16[80,1536]{1,0:T(8,128)(2,1)}, bf16[80,1536]{1,0:T(8,128)(2,1)S(1)}, u32[]{:S(2)}, u32[]{:S(2)}) %collective-permute-start.1) | collective-permute-done | bytes 245792 | tf_op jit(solution)/shard_map/ppermute | solution.py:581
  25.5 1.6 collective-permute-done.6.inner.rest_2_
  27.3 3.1 %shard_map.30 = (bf16[80,1536]{1,0:T(8,128)(2,1)}, bf16[80,3072]{1,0:T(8,128)(2,1)}, bf16[80,6144]{1,0:T(8,128)(2,1)}) custom-call(bf16[80,11520]{1,0:T(8,128)(2,1)} %bitcast.16), custom_call_target="tpu_custom_call" | custom-call | flops 1000 | bytes 4000000 | tf_op jit(solution)/shard_map/pallas_call | solution.py:556
  32.0 7.0 %shard_map.31 = (bf16[528,320]{1,0:T(8,128)(2,1)}, bf16[272,320]{1,0:T(8,128)(2,1)}, bf16[256,320]{1,0:T(8,128)(2,1)}, f32[8,320]{1,0:T(8,128)}) custom-call(s32[5]{0:T(128)} %stack.31.flags, bf16[528,320]{1,0:T(8,128)(2,1)} %get-tuple-element.89.block.rest_0_, bf16[144,320]{1,0:T(8,128)(2,1)} %copy-done.62, bf16[128,320]{1,0:T(8,128)(2,1)} %copy-done.67, ...), custom_call_target="tpu_custom_call" | custom-call | flops 943718400 | bytes 4000000 | tf_op jit(solution)/shard_map/pallas_call | solution.py:308
  38.9 1.4 collective-permute-start.15
  42.1 1.8 collective-permute-start.14
  44.5 2.9 %collective-permute-done.15.outer = bf16[272,320]{1,0:T(8,128)(2,1)S(1)} collective-permute-done((bf16[272,320]{1,0:T(8,128)(2,1)}, bf16[272,320]{1,0:T(8,128)(2,1)S(1)}, u32[]{:S(2)}, u32[]{:S(2)}) %collective-permute-start.15) | collective-permute-done | bytes 174112 | tf_op jit(solution)/shard_map/ppermute | solution.py:581
  47.4 1.2 collective-permute-start.17
  48.7 9.7 %collective-permute-done.16 = f32[8,320]{1,0:T(8,128)S(1)} collective-permute-done((f32[8,320]{1,0:T(8,128)}, f32[8,320]{1,0:T(8,128)S(1)}, u32[]{:S(2)}, u32[]{:S(2)}) %collective-permute-start.16) | collective-permute-done | bytes 10272 | tf_op jit(solution)/shard_map/ppermute | solution.py:581
  65.1 8.1 %shard_map.32.skip_ref = bf16[768,384]{1,0:T(8,128)(2,1)} custom-call(s32[5]{0:T(128)} %stack.31.flags, bf16[528,320]{1,0:T(8,128)(2,1)} %get-tuple-element.100.block, bf16[272,320]{1,0:T(8,128)(2,1)} %copy-done.64, bf16[256,320]{1,0:T(8,128)(2,1)} %copy-done.65, f32[8,320]{1,0:T(8,128)} %copy-done.58, f32[8,320]{1,0:T(8,128)} %copy-done.72, ...), custom_call_target="tpu_custom_call" | custom-call | flops 1415577600 | bytes 4000000 | tf_op jit(solution)/shard_map/pallas_call | solution.py:308
  73.3 1.4 collective-permute-start.29
  74.7 1.5 collective-permute-start.31
  76.7 4.7 %collective-permute-done.29.rest_6_.rest_22_ = bf16[80,1536]{1,0:T(8,128)(2,1)S(1)} collective-permute-done((bf16[80,1536]{1,0:T(8,128)(2,1)S(1)}, bf16[80,1536]{1,0:T(8,128)(2,1)S(1)}, u32[]{:S(2)}, u32[]{:S(2)}) %collective-permute-start.29) | collective-permute-done | bytes 245792 | tf_op jit(solution)/shard_map/ppermute | solution.py:581
  82.9 1.1 collective-permute-done.32.rest_9_.rest_25_
  86.3 5.2 %shard_map.33 = (bf16[144,640]{1,0:T(8,128)(2,1)}, bf16[80,640]{1,0:T(8,128)(2,1)}, bf16[64,640]{1,0:T(8,128)(2,1)}, f32[8,640]{1,0:T(8,128)}) custom-call(s32[5]{0:T(128)} %stack.31.flags, bf16[768,384]{1,0:T(8,128)(2,1)} %shard_map.32.skip_ref, bf16[80,3072]{1,0:T(8,128)(2,1)} %get-tuple-element.103.rest_0_.rest_16_, bf16[80,3072]{1,0:T(8,128)(2,1)} %copy-done.9, ...), custom_call_target="tpu_custom_call" | custom-call | flops 471859200 | bytes 4000000 | tf_op jit(solution)/shard_map/pallas_call | solution.py:345
  91.4 1.6 collective-permute-start.33
  93.1 1.5 collective-permute-start.45
  95.7 2.7 collective-permute-done.33.block.rest_0_
  101.2 16.8 %collective-permute-done.34.outer = bf16[80,640]{1,0:T(8,128)(2,1)S(1)} collective-permute-done((bf16[80,640]{1,0:T(8,128)(2,1)S(1)}, bf16[80,640]{1,0:T(8,128)(2,1)S(1)}, u32[]{:S(2)}, u32[]{:S(2)}) %collective-permute-start.34) | collective-permute-done | bytes 102432 | tf_op jit(solution)/shard_map/ppermute | solution.py:581
  118.0 1.1 collective-permute-start.35
  121.5 7.2 %shard_map.34 = (bf16[144,640]{1,0:T(8,128)(2,1)}, bf16[80,640]{1,0:T(8,128)(2,1)}, bf16[64,640]{1,0:T(8,128)(2,1)}, f32[8,640]{1,0:T(8,128)}) custom-call(s32[5]{0:T(128)} %stack.31.flags, bf16[144,640]{1,0:T(8,128)(2,1)} %copy-done.19, bf16[80,640]{1,0:T(8,128)(2,1)} %copy-done.38, bf16[64,640]{1,0:T(8,128)(2,1)} %copy-done.45, f32[8,640]{1,0:T(8,128)} %copy-done.48, ...), custom_call_target="tpu_custom_call" | custom-call | flops 943718400 | bytes 4000000 | tf_op jit(solution)/shard_map/pallas_call | solution.py:381
  128.7 7.9 %collective-permute-done.39.skip_ref = bf16[768,384]{1,0:T(8,128)(2,1)} collective-permute-done((bf16[768,384]{1,0:T(8,128)(2,1)}, bf16[768,384]{1,0:T(8,128)(2,1)}, u32[]{:S(2)}, u32[]{:S(2)}) %collective-permute-start.39) | collective-permute-done | bytes 589856 | tf_op jit(solution)/shard_map/ppermute | solution.py:577
  137.3 1.2 collective-permute-start.50
  140.1 1.8 collective-permute-start.51
  142.0 1.3 collective-permute-done.42
  143.3 9.8 %collective-permute-done.43 = f32[8,640]{1,0:T(8,128)S(1)} collective-permute-done((f32[8,640]{1,0:T(8,128)S(1)}, f32[8,640]{1,0:T(8,128)S(1)}, u32[]{:S(2)}, u32[]{:S(2)}) %collective-permute-start.43) | collective-permute-done | bytes 20512 | tf_op jit(solution)/shard_map/ppermute | solution.py:581
  154.3 2.8 collective-permute-done.41.inner
  160.5 7.3 %shard_map.35 = (bf16[144,640]{1,0:T(8,128)(2,1)}, bf16[80,640]{1,0:T(8,128)(2,1)}, bf16[64,640]{1,0:T(8,128)(2,1)}, f32[8,640]{1,0:T(8,128)}) custom-call(s32[5]{0:T(128)} %stack.31.flags, bf16[144,640]{1,0:T(8,128)(2,1)} %get-tuple-element.121.block, bf16[80,640]{1,0:T(8,128)(2,1)} %copy-done.37, bf16[64,640]{1,0:T(8,128)(2,1)} %copy-done.43, ...), custom_call_target="tpu_custom_call" | custom-call | flops 943718400 | bytes 4000000 | tf_op jit(solution)/shard_map/pallas_call | solution.py:381
  167.9 2.2 collective-permute-start.54
  170.1 4.7 %collective-permute-done.54.block.rest_0_ = bf16[144,640]{1,0:T(8,128)(2,1)S(1)} collective-permute-done((bf16[144,640]{1,0:T(8,128)(2,1)}, bf16[144,640]{1,0:T(8,128)(2,1)S(1)}, u32[]{:S(2)}, u32[]{:S(2)}) %collective-permute-start.54) | collective-permute-done | bytes 184352 | tf_op jit(solution)/shard_map/ppermute | solution.py:577
  176.9 1.6 collective-permute-start.56
  178.5 1.8 collective-permute-done.55.outer
  182.5 7.2 %shard_map.36 = (bf16[144,640]{1,0:T(8,128)(2,1)}, bf16[80,640]{1,0:T(8,128)(2,1)}, bf16[64,640]{1,0:T(8,128)(2,1)}, f32[8,640]{1,0:T(8,128)}) custom-call(s32[5]{0:T(128)} %stack.31.flags, bf16[144,640]{1,0:T(8,128)(2,1)} %copy-done.20, bf16[80,640]{1,0:T(8,128)(2,1)} %copy-done.39, bf16[64,640]{1,0:T(8,128)(2,1)} %copy-done.46, f32[8,640]{1,0:T(8,128)} %copy-done.50, ...), custom_call_target="tpu_custom_call" | custom-call | flops 943718400 | bytes 4000000 | tf_op jit(solution)/shard_map/pallas_call | solution.py:381
  189.7 1.3 collective-permute-start.60
  191.6 1.1 collective-permute-start.63
  193.3 2.8 collective-permute-done.60.outer
  197.3 1.2 collective-permute-done.64.sb
  199.1 7.3 %shard_map.37 = (bf16[144,640]{1,0:T(8,128)(2,1)}, bf16[80,640]{1,0:T(8,128)(2,1)}, bf16[64,640]{1,0:T(8,128)(2,1)}, f32[8,640]{1,0:T(8,128)}) custom-call(s32[5]{0:T(128)} %stack.31.flags, bf16[144,640]{1,0:T(8,128)(2,1)} %get-tuple-element.133.block, bf16[80,640]{1,0:T(8,128)(2,1)} %copy-done.40, bf16[64,640]{1,0:T(8,128)(2,1)} %copy-done.44, ...), custom_call_target="tpu_custom_call" | custom-call | flops 943718400 | bytes 4000000 | tf_op jit(solution)/shard_map/pallas_call | solution.py:381
  206.4 2.4 collective-permute-start.65
  208.8 4.8 %collective-permute-done.65.block = bf16[144,640]{1,0:T(8,128)(2,1)S(1)} collective-permute-done((bf16[144,640]{1,0:T(8,128)(2,1)}, bf16[144,640]{1,0:T(8,128)(2,1)S(1)}, u32[]{:S(2)}, u32[]{:S(2)}) %collective-permute-start.65) | collective-permute-done | bytes 184352 | tf_op jit(solution)/shard_map/ppermute | solution.py:577
  216.0 3.0 %collective-permute-done.66.outer = bf16[80,640]{1,0:T(8,128)(2,1)S(1)} collective-permute-done((bf16[80,640]{1,0:T(8,128)(2,1)S(1)}, bf16[80,640]{1,0:T(8,128)(2,1)S(1)}, u32[]{:S(2)}, u32[]{:S(2)}) %collective-permute-start.66) | collective-permute-done | bytes 102432 | tf_op jit(solution)/shard_map/ppermute | solution.py:581
  219.6 9.1 %shard_map.38 = (bf16[528,320]{1,0:T(8,128)(2,1)}, bf16[144,320]{1,0:T(8,128)(2,1)}, bf16[128,320]{1,0:T(8,128)(2,1)}, f32[8,320]{1,0:T(8,128)}) custom-call(s32[5]{0:T(128)} %stack.31.flags, bf16[144,640]{1,0:T(8,128)(2,1)} %copy-done.36, bf16[80,640]{1,0:T(8,128)(2,1)} %copy-done.66, bf16[64,640]{1,0:T(8,128)(2,1)} %copy-done.71, ...), custom_call_target="tpu_custom_call" | custom-call | flops 1887436800 | bytes 4000000 | tf_op jit(solution)/shard_map/pallas_call | solution.py:420
  228.7 1.1 collective-permute-start.68
  229.8 1.3 collective-permute-start.71
  231.1 1.3 collective-permute-start.69
  232.4 1.8 collective-permute-done.68.outer
  237.1 9.8 %shard_map.39 = (bf16[528,320]{1,0:T(8,128)(2,1)}, bf16[144,320]{1,0:T(8,128)(2,1)}, bf16[128,320]{1,0:T(8,128)(2,1)}, f32[8,320]{1,0:T(8,128)}) custom-call(s32[5]{0:T(128)} %stack.31.flags, bf16[528,320]{1,0:T(8,128)(2,1)} %get-tuple-element.139.block.u_ref, bf16[144,320]{1,0:T(8,128)(2,1)} %copy-done.63, bf16[128,320]{1,0:T(8,128)(2,1)} %copy-done.69, ...), custom_call_target="tpu_custom_call" | custom-call | flops 1887436800 | bytes 4000000 | tf_op jit(solution)/shard_map/pallas_call | solution.py:461
  246.9 1.9 collective-permute-start.73
  248.9 1.2 collective-permute-start.76
  250.7 2.5 collective-permute-done.73.outer
  254.5 1.1 collective-permute-done.77.sb
  256.3 7.9 %shard_map.40 = (bf16[8,16,320]{2,1,0:T(8,128)(2,1)}, bf16[8,16,320]{2,1,0:T(8,128)(2,1)}, bf16[8,16,320]{2,1,0:T(8,128)(2,1)}, bf16[8,16,320]{2,1,0:T(8,128)(2,1)}) custom-call(s32[5]{0:T(128)} %stack.31.flags, bf16[528,320]{1,0:T(8,128)(2,1)} %get-tuple-element.143.block, bf16[144,320]{1,0:T(8,128)(2,1)} %copy-done.41, bf16[128,320]{1,0:T(8,128)(2,1)} %copy-done.42, ...), custom_call_target="tpu_custom_call" | custom-call | flops 1153433600 | bytes 4000000 | tf_op jit(solution)/shard_map/pallas_call | solution.py:534
  264.2 2.2 collective-permute-start.78
  266.4 3.0 %collective-permute-start.79 = (bf16[8,16,320]{2,1,0:T(8,128)(2,1)}, bf16[8,16,320]{2,1,0:T(8,128)(2,1)S(1)}, u32[]{:S(2)}, u32[]{:S(2)}) collective-permute-start(bf16[8,16,320]{2,1,0:T(8,128)(2,1)} %get-tuple-element.148), channel_id=1, source_target_pairs={{0,16},{1,17},{2,18},{3,19},{4,20},{5,21},{6,22},{7,23},{8,24},{9,... | collective-permute-start | bytes 245768 | tf_op jit(solution)/shard_map/ppermute | solution.py:577
  269.4 1.9 collective-permute-start.80
  271.3 5.0 %collective-permute-done.79 = bf16[8,16,320]{2,1,0:T(8,128)(2,1)S(1)} collective-permute-done((bf16[8,16,320]{2,1,0:T(8,128)(2,1)}, bf16[8,16,320]{2,1,0:T(8,128)(2,1)S(1)}, u32[]{:S(2)}, u32[]{:S(2)}) %collective-permute-start.79) | collective-permute-done | bytes 81952 | tf_op jit(solution)/shard_map/ppermute | solution.py:577
  276.3 2.6 collective-permute-done.80
  (312 shorter events, 49.9 us)
Async XLA Ops:
  4.7 7.9 %collective-permute-start.3 = (bf16[144,320]{1,0:T(8,128)(2,1)}, bf16[144,320]{1,0:T(8,128)(2,1)S(1)}, u32[]{:S(2)}, u32[]{:S(2)}) collective-permute-start(bf16[144,320]{1,0:T(8,128)(2,1)} %get-tuple-element.83), channel_id=1, source_target_pairs={{0,7},{1,2},{2,1},{3,4},{4,3},{5,6},{6,5},{7,0},{8,15},{9,10},{10,... | collective-permute-start | bytes 276488 | tf_op jit(solution)/shard_map/ppermute | solution.py:581
  6.7 7.0 %collective-permute-start.4 = (f32[8,320]{1,0:T(8,128)}, f32[8,320]{1,0:T(8,128)S(1)}, u32[]{:S(2)}, u32[]{:S(2)}) collective-permute-start(f32[8,320]{1,0:T(8,128)} %get-tuple-element.79), channel_id=1, source_target_pairs={{0,2},{1,7},{2,4},{3,1},{4,6},{5,3},{6,0},{7,5},{8,10},{9,15},{10,... | collective-permute-start | bytes 30728 | tf_op jit(solution)/shard_map/ppermute | solution.py:581
  6.7 7.0 %collective-permute-start.5 = (f32[8,320]{1,0:T(8,128)}, f32[8,320]{1,0:T(8,128)S(1)}, u32[]{:S(2)}, u32[]{:S(2)}) collective-permute-start(f32[8,320]{1,0:T(8,128)} %get-tuple-element.79), channel_id=1, source_target_pairs={{0,4},{1,5},{2,6},{3,7},{4,0},{5,1},{6,2},{7,3},{8,12},{9,13},{10,... | collective-permute-start | bytes 30728 | tf_op jit(solution)/shard_map/ppermute | solution.py:581
  9.7 9.4 %collective-permute-start = (bf16[80,1536]{1,0:T(8,128)(2,1)}, bf16[80,1536]{1,0:T(8,128)(2,1)S(1)}, u32[]{:S(2)}, u32[]{:S(2)}) collective-permute-start(bf16[80,1536]{1,0:T(8,128)(2,1)} %shard_map.29.rest_0_), channel_id=1, source_target_pairs={{0,2},{1,3},{2,0},{3,1},{4,6},{5,7},{6,4},{7,5},{8,10},{9,11},{10,... | collective-permute-start | bytes 737288 | tf_op jit(solution)/shard_map/ppermute | solution.py:581
  12.0 12.3 %collective-permute-start.1 = (bf16[80,1536]{1,0:T(8,128)(2,1)}, bf16[80,1536]{1,0:T(8,128)(2,1)S(1)}, u32[]{:S(2)}, u32[]{:S(2)}) collective-permute-start(bf16[80,1536]{1,0:T(8,128)(2,1)} %shard_map.29.rest_0_), channel_id=1, source_target_pairs={{0,4},{1,5},{2,6},{3,7},{4,0},{5,1},{6,2},{7,3},{8,12},{9,13},{10,... | collective-permute-start | bytes 737288 | tf_op jit(solution)/shard_map/ppermute | solution.py:581
  12.6 11.7 %collective-permute-start.2 = (bf16[80,1536]{1,0:T(8,128)(2,1)}, bf16[80,1536]{1,0:T(8,128)(2,1)S(1)}, u32[]{:S(2)}, u32[]{:S(2)}) collective-permute-start(bf16[80,1536]{1,0:T(8,128)(2,1)} %shard_map.29.rest_0_), channel_id=1, source_target_pairs={{0,6},{1,7},{2,4},{3,5},{4,2},{5,3},{6,0},{7,1},{8,14},{9,15},{10,... | collective-permute-start | bytes 737288 | tf_op jit(solution)/shard_map/ppermute | solution.py:581
  24.3 6.1 %collective-permute-start.10 = (bf16[80,1536]{1,0:T(8,128)(2,1)S(1)}, bf16[80,1536]{1,0:T(8,128)(2,1)S(1)}, u32[]{:S(2)}, u32[]{:S(2)}) collective-permute-start(bf16[80,1536]{1,0:T(8,128)(2,1)S(1)} %collective-permute-done.1.rest_4_), channel_id=1, source_target_pairs={{0,1},{1,0},{2,3},{3,2},{4,5},{5,4},{6,7},{7,6},{8,9},{9,8},{10,11... | collective-permute-start | bytes 737288 | tf_op jit(solution)/shard_map/ppermute | solution.py:581
  24.4 6.0 %collective-permute-start.11 = (bf16[80,1536]{1,0:T(8,128)(2,1)S(1)}, bf16[80,1536]{1,0:T(8,128)(2,1)S(1)}, u32[]{:S(2)}, u32[]{:S(2)}) collective-permute-start(bf16[80,1536]{1,0:T(8,128)(2,1)S(1)} %collective-permute-done.2.rest_6_), channel_id=1, source_target_pairs={{0,1},{1,0},{2,3},{3,2},{4,5},{5,4},{6,7},{7,6},{8,9},{9,8},{10,11... | collective-permute-start | bytes 737288 | tf_op jit(solution)/shard_map/ppermute | solution.py:581
  24.9 5.5 %collective-permute-start.8 = (bf16[80,1536]{1,0:T(8,128)(2,1)}, bf16[80,1536]{1,0:T(8,128)(2,1)S(1)}, u32[]{:S(2)}, u32[]{:S(2)}) collective-permute-start(bf16[80,1536]{1,0:T(8,128)(2,1)} %shard_map.29.rest_0_), channel_id=1, source_target_pairs={{0,1},{1,0},{2,3},{3,2},{4,5},{5,4},{6,7},{7,6},{8,9},{9,8},{10,11... | collective-permute-start | bytes 737288 | tf_op jit(solution)/shard_map/ppermute | solution.py:581
  25.0 5.5 %collective-permute-start.9 = (bf16[80,1536]{1,0:T(8,128)(2,1)S(1)}, bf16[80,1536]{1,0:T(8,128)(2,1)S(1)}, u32[]{:S(2)}, u32[]{:S(2)}) collective-permute-start(bf16[80,1536]{1,0:T(8,128)(2,1)S(1)} %collective-permute-done.rest_2_), channel_id=1, source_target_pairs={{0,1},{1,0},{2,3},{3,2},{4,5},{5,4},{6,7},{7,6},{8,9},{9,8},{10,11... | collective-permute-start | bytes 737288 | tf_op jit(solution)/shard_map/ppermute | solution.py:581
  27.1 3.3 %collective-permute-start.7 = (f32[8,320]{1,0:T(8,128)S(1)}, f32[8,320]{1,0:T(8,128)S(1)}, u32[]{:S(2)}, u32[]{:S(2)}) collective-permute-start(f32[8,320]{1,0:T(8,128)S(1)} %fusion.9.sa), channel_id=1, source_target_pairs={{0,1},{1,0},{2,3},{3,2},{4,5},{5,4},{6,7},{7,6},{8,9},{9,8},{10,11... | collective-permute-start | bytes 30728 | tf_op jit(solution)/shard_map/ppermute | solution.py:581
  38.9 8.5 %collective-permute-start.15 = (bf16[272,320]{1,0:T(8,128)(2,1)}, bf16[272,320]{1,0:T(8,128)(2,1)S(1)}, u32[]{:S(2)}, u32[]{:S(2)}) collective-permute-start(bf16[272,320]{1,0:T(8,128)(2,1)} %get-tuple-element.94), channel_id=1, source_target_pairs={{0,7},{1,2},{2,1},{3,4},{4,3},{5,6},{6,5},{7,0},{8,15},{9,10},{10,... | collective-permute-start | bytes 522248 | tf_op jit(solution)/shard_map/ppermute | solution.py:581
  40.4 18.8 %collective-permute-start.12 = (bf16[80,1536]{1,0:T(8,128)(2,1)S(1)}, bf16[80,1536]{1,0:T(8,128)(2,1)S(1)}, u32[]{:S(2)}, u32[]{:S(2)}) collective-permute-start(bf16[80,1536]{1,0:T(8,128)(2,1)S(1)} %copy-done.28), channel_id=1, source_target_pairs={{0,2},{1,3},{2,0},{3,1},{4,6},{5,7},{6,4},{7,5},{8,10},{9,11},{10,... | collective-permute-start | bytes 737288 | tf_op jit(solution)/shard_map/ppermute | solution.py:581
  41.0 18.2 %collective-permute-start.13 = (bf16[80,1536]{1,0:T(8,128)(2,1)S(1)}, bf16[80,1536]{1,0:T(8,128)(2,1)S(1)}, u32[]{:S(2)}, u32[]{:S(2)}) collective-permute-start(bf16[80,1536]{1,0:T(8,128)(2,1)S(1)} %copy-done.28), channel_id=1, source_target_pairs={{0,4},{1,5},{2,6},{3,7},{4,0},{5,1},{6,2},{7,3},{8,12},{9,13},{10,... | collective-permute-start | bytes 737288 | tf_op jit(solution)/shard_map/ppermute | solution.py:581
  42.1 17.1 %collective-permute-start.14 = (bf16[80,1536]{1,0:T(8,128)(2,1)S(1)}, bf16[80,1536]{1,0:T(8,128)(2,1)S(1)}, u32[]{:S(2)}, u32[]{:S(2)}) collective-permute-start(bf16[80,1536]{1,0:T(8,128)(2,1)S(1)} %copy-done.28), channel_id=1, source_target_pairs={{0,6},{1,7},{2,4},{3,5},{4,2},{5,3},{6,0},{7,1},{8,14},{9,15},{10,... | collective-permute-start | bytes 737288 | tf_op jit(solution)/shard_map/ppermute | solution.py:581
  43.9 14.5 %collective-permute-start.16 = (f32[8,320]{1,0:T(8,128)}, f32[8,320]{1,0:T(8,128)S(1)}, u32[]{:S(2)}, u32[]{:S(2)}) collective-permute-start(f32[8,320]{1,0:T(8,128)} %get-tuple-element.93), channel_id=1, source_target_pairs={{0,2},{1,7},{2,4},{3,1},{4,6},{5,3},{6,0},{7,5},{8,10},{9,15},{10,... | collective-permute-start | bytes 30728 | tf_op jit(solution)/shard_map/ppermute | solution.py:581
  47.4 11.0 %collective-permute-start.17 = (f32[8,320]{1,0:T(8,128)}, f32[8,320]{1,0:T(8,128)S(1)}, u32[]{:S(2)}, u32[]{:S(2)}) collective-permute-start(f32[8,320]{1,0:T(8,128)} %get-tuple-element.93), channel_id=1, source_target_pairs={{0,4},{1,5},{2,6},{3,7},{4,0},{5,1},{6,2},{7,3},{8,12},{9,13},{10,... | collective-permute-start | bytes 30728 | tf_op jit(solution)/shard_map/ppermute | solution.py:581
  59.2 3.1 %collective-permute-start.20 = (bf16[80,1536]{1,0:T(8,128)(2,1)S(1)}, bf16[80,1536]{1,0:T(8,128)(2,1)S(1)}, u32[]{:S(2)}, u32[]{:S(2)}) collective-permute-start(bf16[80,1536]{1,0:T(8,128)(2,1)S(1)} %copy-done.28), channel_id=1, source_target_pairs={{0,1},{1,0},{2,3},{3,2},{4,5},{5,4},{6,7},{7,6},{8,9},{9,8},{10,11... | collective-permute-start | bytes 737288 | tf_op jit(solution)/shard_map/ppermute | solution.py:581
  59.8 13.4 %collective-permute-start.24 = (bf16[80,3072]{1,0:T(8,128)(2,1)S(1)}, bf16[80,3072]{1,0:T(8,128)(2,1)S(1)}, u32[]{:S(2)}, u32[]{:S(2)}) collective-permute-start(bf16[80,3072]{1,0:T(8,128)(2,1)S(1)} %copy-done.8), channel_id=1, source_target_pairs={{0,2},{1,3},{2,0},{3,1},{4,6},{5,7},{6,4},{7,5},{8,10},{9,11},{10,... | collective-permute-start | bytes 1474568 | tf_op jit(solution)/shard_map/ppermute | solution.py:581
  60.3 12.9 %collective-permute-start.25 = (bf16[80,3072]{1,0:T(8,128)(2,1)S(1)}, bf16[80,3072]{1,0:T(8,128)(2,1)S(1)}, u32[]{:S(2)}, u32[]{:S(2)}) collective-permute-start(bf16[80,3072]{1,0:T(8,128)(2,1)S(1)} %copy-done.8), channel_id=1, source_target_pairs={{0,4},{1,5},{2,6},{3,7},{4,0},{5,1},{6,2},{7,3},{8,12},{9,13},{10,... | collective-permute-start | bytes 1474568 | tf_op jit(solution)/shard_map/ppermute | solution.py:581
  73.3 8.1 %collective-permute-start.29 = (bf16[80,1536]{1,0:T(8,128)(2,1)S(1)}, bf16[80,1536]{1,0:T(8,128)(2,1)S(1)}, u32[]{:S(2)}, u32[]{:S(2)}) collective-permute-start(bf16[80,1536]{1,0:T(8,128)(2,1)S(1)} %slice.275), channel_id=1, source_target_pairs={{0,4},{1,5},{2,6},{3,7},{4,0},{5,1},{6,2},{7,3},{8,12},{9,13},{10,... | collective-permute-start | bytes 737288 | tf_op jit(solution)/shard_map/ppermute | solution.py:581
  74.7 7.7 %collective-permute-start.31 = (bf16[80,1536]{1,0:T(8,128)(2,1)S(1)}, bf16[80,1536]{1,0:T(8,128)(2,1)S(1)}, u32[]{:S(2)}, u32[]{:S(2)}) collective-permute-start(bf16[80,1536]{1,0:T(8,128)(2,1)S(1)} %slice.276), channel_id=1, source_target_pairs={{0,2},{1,3},{2,0},{3,1},{4,6},{5,7},{6,4},{7,5},{8,10},{9,11},{10,... | collective-permute-start | bytes 737288 | tf_op jit(solution)/shard_map/ppermute | solution.py:581
  76.2 7.8 %collective-permute-start.26 = (bf16[80,3072]{1,0:T(8,128)(2,1)S(1)}, bf16[80,3072]{1,0:T(8,128)(2,1)S(1)}, u32[]{:S(2)}, u32[]{:S(2)}) collective-permute-start(bf16[80,3072]{1,0:T(8,128)(2,1)S(1)} %copy-done.8), channel_id=1, source_target_pairs={{0,1},{1,0},{2,3},{3,2},{4,5},{5,4},{6,7},{7,6},{8,9},{9,8},{10,11... | collective-permute-start | bytes 1474568 | tf_op jit(solution)/shard_map/ppermute | solution.py:581
  76.2 7.8 %collective-permute-start.27 = (bf16[80,3072]{1,0:T(8,128)(2,1)S(1)}, bf16[80,3072]{1,0:T(8,128)(2,1)S(1)}, u32[]{:S(2)}, u32[]{:S(2)}) collective-permute-start(bf16[80,3072]{1,0:T(8,128)(2,1)S(1)} %collective-permute-done.24.rest_2_.rest_18_), channel_id=1, source_target_pairs={{0,1},{1,0},{2,3},{3,2},{4,5},{5,4},{6,7},{7,6},{8,9},{9,8},{10,11... | collective-permute-start | bytes 1474568 | tf_op jit(solution)/shard_map/ppermute | solution.py:581
  76.7 8.0 %collective-permute-start.28 = (bf16[80,3072]{1,0:T(8,128)(2,1)S(1)}, bf16[80,3072]{1,0:T(8,128)(2,1)S(1)}, u32[]{:S(2)}, u32[]{:S(2)}) collective-permute-start(bf16[80,3072]{1,0:T(8,128)(2,1)S(1)} %collective-permute-done.25.rest_4_.rest_20_), channel_id=1, source_target_pairs={{0,1},{1,0},{2,3},{3,2},{4,5},{5,4},{6,7},{7,6},{8,9},{9,8},{10,11... | collective-permute-start | bytes 1474568 | tf_op jit(solution)/shard_map/ppermute | solution.py:581
  91.4 6.9 %collective-permute-start.33 = (bf16[144,640]{1,0:T(8,128)(2,1)}, bf16[144,640]{1,0:T(8,128)(2,1)S(1)}, u32[]{:S(2)}, u32[]{:S(2)}) collective-permute-start(bf16[144,640]{1,0:T(8,128)(2,1)} %get-tuple-element.110), channel_id=1, source_target_pairs={{0,8},{1,9},{2,10},{3,11},{4,12},{5,13},{6,14},{7,15},{8,16},{9,17... | collective-permute-start | bytes 552968 | tf_op jit(solution)/shard_map/ppermute | solution.py:577
  93.1 44.1 %collective-permute-start.45 = (bf16[80,6144]{1,0:T(8,128)(2,1)S(1)}, bf16[80,6144]{1,0:T(8,128)(2,1)S(1)}, u32[]{:S(2)}, u32[]{:S(2)}) collective-permute-start(bf16[80,6144]{1,0:T(8,128)(2,1)S(1)} %copy-done.2), channel_id=1, source_target_pairs={{0,2},{1,3},{2,0},{3,1},{4,6},{5,7},{6,4},{7,5},{8,10},{9,11},{10,... | collective-permute-start | bytes 2949128 | tf_op jit(solution)/shard_map/ppermute | solution.py:581
  94.6 42.7 %collective-permute-start.46 = (bf16[80,6144]{1,0:T(8,128)(2,1)S(1)}, bf16[80,6144]{1,0:T(8,128)(2,1)S(1)}, u32[]{:S(2)}, u32[]{:S(2)}) collective-permute-start(bf16[80,6144]{1,0:T(8,128)(2,1)S(1)} %copy-done.2), channel_id=1, source_target_pairs={{0,4},{1,5},{2,6},{3,7},{4,0},{5,1},{6,2},{7,3},{8,12},{9,13},{10,... | collective-permute-start | bytes 2949128 | tf_op jit(solution)/shard_map/ppermute | solution.py:581
  98.5 19.5 %collective-permute-start.34 = (bf16[80,640]{1,0:T(8,128)(2,1)S(1)}, bf16[80,640]{1,0:T(8,128)(2,1)S(1)}, u32[]{:S(2)}, u32[]{:S(2)}) collective-permute-start(bf16[80,640]{1,0:T(8,128)(2,1)S(1)} %pad_maximum_fusion), channel_id=1, source_target_pairs={{0,7},{1,2},{2,1},{3,4},{4,3},{5,6},{6,5},{7,0},{8,15},{9,10},{10,... | collective-permute-start | bytes 307208 | tf_op jit(solution)/shard_map/ppermute | solution.py:581
  99.5 20.0 %collective-permute-start.36 = (f32[8,640]{1,0:T(8,128)S(1)}, f32[8,640]{1,0:T(8,128)S(1)}, u32[]{:S(2)}, u32[]{:S(2)}) collective-permute-start(f32[8,640]{1,0:T(8,128)S(1)} %maximum_maximum_fusion), channel_id=1, source_target_pairs={{0,2},{1,7},{2,4},{3,1},{4,6},{5,3},{6,0},{7,5},{8,10},{9,15},{10,... | collective-permute-start | bytes 61448 | tf_op jit(solution)/shard_map/ppermute | solution.py:581
  100.1 19.4 %collective-permute-start.37 = (f32[8,640]{1,0:T(8,128)S(1)}, f32[8,640]{1,0:T(8,128)S(1)}, u32[]{:S(2)}, u32[]{:S(2)}) collective-permute-start(f32[8,640]{1,0:T(8,128)S(1)} %maximum_maximum_fusion), channel_id=1, source_target_pairs={{0,4},{1,5},{2,6},{3,7},{4,0},{5,1},{6,2},{7,3},{8,12},{9,13},{10,... | collective-permute-start | bytes 61448 | tf_op jit(solution)/shard_map/ppermute | solution.py:581
  120.9 15.7 %collective-permute-start.39 = (bf16[768,384]{1,0:T(8,128)(2,1)}, bf16[768,384]{1,0:T(8,128)(2,1)}, u32[]{:S(2)}, u32[]{:S(2)}) collective-permute-start(bf16[768,384]{1,0:T(8,128)(2,1)} %shard_map.32.skip_ref), channel_id=1, source_target_pairs={{0,24},{1,25},{2,26},{3,27},{4,28},{5,29},{6,30},{7,31},{8,0},{9,1... | collective-permute-start | bytes 1769480 | tf_op jit(solution)/shard_map/ppermute | solution.py:577
  136.6 16.5 %collective-permute-start.40 = (bf16[80,640]{1,0:T(8,128)(2,1)}, bf16[80,640]{1,0:T(8,128)(2,1)S(1)}, u32[]{:S(2)}, u32[]{:S(2)}) collective-permute-start(bf16[80,640]{1,0:T(8,128)(2,1)} %get-tuple-element.122), channel_id=1, source_target_pairs={{0,7},{1,2},{2,1},{3,4},{4,3},{5,6},{6,5},{7,0},{8,15},{9,10},{10,... | collective-permute-start | bytes 307208 | tf_op jit(solution)/shard_map/ppermute | solution.py:581
  137.3 16.3 %collective-permute-start.50 = (bf16[80,3072]{1,0:T(8,128)(2,1)S(1)}, bf16[80,3072]{1,0:T(8,128)(2,1)S(1)}, u32[]{:S(2)}, u32[]{:S(2)}) collective-permute-start(bf16[80,3072]{1,0:T(8,128)(2,1)S(1)} %slice.385), channel_id=1, source_target_pairs={{0,4},{1,5},{2,6},{3,7},{4,0},{5,1},{6,2},{7,3},{8,12},{9,13},{10,... | collective-permute-start | bytes 1474568 | tf_op jit(solution)/shard_map/ppermute | solution.py:581
  138.5 4.8 %collective-permute-start.42 = (f32[8,640]{1,0:T(8,128)S(1)}, f32[8,640]{1,0:T(8,128)S(1)}, u32[]{:S(2)}, u32[]{:S(2)}) collective-permute-start(f32[8,640]{1,0:T(8,128)S(1)} %copy-done.56), channel_id=1, source_target_pairs={{0,2},{1,7},{2,4},{3,1},{4,6},{5,3},{6,0},{7,5},{8,10},{9,15},{10,... | collective-permute-start | bytes 61448 | tf_op jit(solution)/shard_map/ppermute | solution.py:581
  139.0 14.0 %collective-permute-start.43 = (f32[8,640]{1,0:T(8,128)S(1)}, f32[8,640]{1,0:T(8,128)S(1)}, u32[]{:S(2)}, u32[]{:S(2)}) collective-permute-start(f32[8,640]{1,0:T(8,128)S(1)} %copy-done.56), channel_id=1, source_target_pairs={{0,4},{1,5},{2,6},{3,7},{4,0},{5,1},{6,2},{7,3},{8,12},{9,13},{10,... | collective-permute-start | bytes 61448 | tf_op jit(solution)/shard_map/ppermute | solution.py:581
  140.1 14.0 %collective-permute-start.51 = (bf16[80,3072]{1,0:T(8,128)(2,1)S(1)}, bf16[80,3072]{1,0:T(8,128)(2,1)S(1)}, u32[]{:S(2)}, u32[]{:S(2)}) collective-permute-start(bf16[80,3072]{1,0:T(8,128)(2,1)S(1)} %slice.386), channel_id=1, source_target_pairs={{0,2},{1,3},{2,0},{3,1},{4,6},{5,7},{6,4},{7,5},{8,10},{9,11},{10,... | collective-permute-start | bytes 1474568 | tf_op jit(solution)/shard_map/ppermute | solution.py:581
  143.3 14.4 %collective-permute-start.47 = (bf16[80,6144]{1,0:T(8,128)(2,1)S(1)}, bf16[80,6144]{1,0:T(8,128)(2,1)S(1)}, u32[]{:S(2)}, u32[]{:S(2)}) collective-permute-start(bf16[80,6144]{1,0:T(8,128)(2,1)S(1)} %copy-done.2), channel_id=1, source_target_pairs={{0,1},{1,0},{2,3},{3,2},{4,5},{5,4},{6,7},{7,6},{8,9},{9,8},{10,11... | collective-permute-start | bytes 2949128 | tf_op jit(solution)/shard_map/ppermute | solution.py:581
  153.0 4.6 %collective-permute-start.48 = (bf16[80,6144]{1,0:T(8,128)(2,1)S(1)}, bf16[80,6144]{1,0:T(8,128)(2,1)S(1)}, u32[]{:S(2)}, u32[]{:S(2)}) collective-permute-start(bf16[80,6144]{1,0:T(8,128)(2,1)S(1)} %collective-permute-done.45.rest_3_.rest_2_), channel_id=1, source_target_pairs={{0,1},{1,0},{2,3},{3,2},{4,5},{5,4},{6,7},{7,6},{8,9},{9,8},{10,11... | collective-permute-start | bytes 2949128 | tf_op jit(solution)/shard_map/ppermute | solution.py:581
  153.1 4.6 %collective-permute-start.49 = (bf16[80,6144]{1,0:T(8,128)(2,1)S(1)}, bf16[80,6144]{1,0:T(8,128)(2,1)S(1)}, u32[]{:S(2)}, u32[]{:S(2)}) collective-permute-start(bf16[80,6144]{1,0:T(8,128)(2,1)S(1)} %collective-permute-done.46.rest_5_.rest_4_), channel_id=1, source_target_pairs={{0,1},{1,0},{2,3},{3,2},{4,5},{5,4},{6,7},{7,6},{8,9},{9,8},{10,11... | collective-permute-start | bytes 2949128 | tf_op jit(solution)/shard_map/ppermute | solution.py:581
  153.6 3.5 %collective-permute-start.41 = (bf16[64,640]{1,0:T(8,128)(2,1)S(1)}, bf16[64,640]{1,0:T(8,128)(2,1)S(1)}, u32[]{:S(2)}, u32[]{:S(2)}) collective-permute-start(bf16[64,640]{1,0:T(8,128)(2,1)S(1)} %copy-done.70), channel_id=1, source_target_pairs={{0,1},{1,0},{2,3},{3,2},{4,5},{5,4},{6,7},{7,6},{8,9},{9,8},{10,11... | collective-permute-start | bytes 245768 | tf_op jit(solution)/shard_map/ppermute | solution.py:581
  154.1 3.1 %collective-permute-start.44 = (f32[8,640]{1,0:T(8,128)S(1)}, f32[8,640]{1,0:T(8,128)S(1)}, u32[]{:S(2)}, u32[]{:S(2)}) collective-permute-start(f32[8,640]{1,0:T(8,128)S(1)} %fusion.3.sa), channel_id=1, source_target_pairs={{0,1},{1,0},{2,3},{3,2},{4,5},{5,4},{6,7},{7,6},{8,9},{9,8},{10,11... | collective-permute-start | bytes 61448 | tf_op jit(solution)/shard_map/ppermute | solution.py:581
  167.9 6.9 %collective-permute-start.54 = (bf16[144,640]{1,0:T(8,128)(2,1)}, bf16[144,640]{1,0:T(8,128)(2,1)S(1)}, u32[]{:S(2)}, u32[]{:S(2)}) collective-permute-start(bf16[144,640]{1,0:T(8,128)(2,1)} %get-tuple-element.132), channel_id=1, source_target_pairs={{0,8},{1,9},{2,10},{3,11},{4,12},{5,13},{6,14},{7,15},{8,16},{9,17... | collective-permute-start | bytes 552968 | tf_op jit(solution)/shard_map/ppermute | solution.py:577
  174.9 5.4 %collective-permute-start.55 = (bf16[80,640]{1,0:T(8,128)(2,1)S(1)}, bf16[80,640]{1,0:T(8,128)(2,1)S(1)}, u32[]{:S(2)}, u32[]{:S(2)}) collective-permute-start(bf16[80,640]{1,0:T(8,128)(2,1)S(1)} %pad_maximum_fusion.1), channel_id=1, source_target_pairs={{0,7},{1,2},{2,1},{3,4},{4,3},{5,6},{6,5},{7,0},{8,15},{9,10},{10,... | collective-permute-start | bytes 307208 | tf_op jit(solution)/shard_map/ppermute | solution.py:581
  175.2 5.2 %collective-permute-start.57 = (f32[8,640]{1,0:T(8,128)S(1)}, f32[8,640]{1,0:T(8,128)S(1)}, u32[]{:S(2)}, u32[]{:S(2)}) collective-permute-start(f32[8,640]{1,0:T(8,128)S(1)} %maximum_maximum_fusion.1), channel_id=1, source_target_pairs={{0,2},{1,7},{2,4},{3,1},{4,6},{5,3},{6,0},{7,5},{8,10},{9,15},{10,... | collective-permute-start | bytes 61448 | tf_op jit(solution)/shard_map/ppermute | solution.py:581
  175.9 4.6 %collective-permute-start.58 = (f32[8,640]{1,0:T(8,128)S(1)}, f32[8,640]{1,0:T(8,128)S(1)}, u32[]{:S(2)}, u32[]{:S(2)}) collective-permute-start(f32[8,640]{1,0:T(8,128)S(1)} %maximum_maximum_fusion.1), channel_id=1, source_target_pairs={{0,4},{1,5},{2,6},{3,7},{4,0},{5,1},{6,2},{7,3},{8,12},{9,13},{10,... | collective-permute-start | bytes 61448 | tf_op jit(solution)/shard_map/ppermute | solution.py:581
  176.9 3.8 %collective-permute-start.56 = (bf16[64,640]{1,0:T(8,128)(2,1)S(1)}, bf16[64,640]{1,0:T(8,128)(2,1)S(1)}, u32[]{:S(2)}, u32[]{:S(2)}) collective-permute-start(bf16[64,640]{1,0:T(8,128)(2,1)S(1)} %get-tuple-element.155), channel_id=1, source_target_pairs={{0,1},{1,0},{2,3},{3,2},{4,5},{5,4},{6,7},{7,6},{8,9},{9,8},{10,11... | collective-permute-start | bytes 245768 | tf_op jit(solution)/shard_map/ppermute | solution.py:581
  189.7 6.5 %collective-permute-start.60 = (bf16[80,640]{1,0:T(8,128)(2,1)}, bf16[80,640]{1,0:T(8,128)(2,1)S(1)}, u32[]{:S(2)}, u32[]{:S(2)}) collective-permute-start(bf16[80,640]{1,0:T(8,128)(2,1)} %get-tuple-element.134), channel_id=1, source_target_pairs={{0,7},{1,2},{2,1},{3,4},{4,3},{5,6},{6,5},{7,0},{8,15},{9,10},{10,... | collective-permute-start | bytes 307208 | tf_op jit(solution)/shard_map/ppermute | solution.py:581
  191.0 5.5 %collective-permute-start.62 = (f32[8,640]{1,0:T(8,128)}, f32[8,640]{1,0:T(8,128)S(1)}, u32[]{:S(2)}, u32[]{:S(2)}) collective-permute-start(f32[8,640]{1,0:T(8,128)} %get-tuple-element.136), channel_id=1, source_target_pairs={{0,2},{1,7},{2,4},{3,1},{4,6},{5,3},{6,0},{7,5},{8,10},{9,15},{10,... | collective-permute-start | bytes 61448 | tf_op jit(solution)/shard_map/ppermute | solution.py:581
  191.6 4.9 %collective-permute-start.63 = (f32[8,640]{1,0:T(8,128)}, f32[8,640]{1,0:T(8,128)S(1)}, u32[]{:S(2)}, u32[]{:S(2)}) collective-permute-start(f32[8,640]{1,0:T(8,128)} %get-tuple-element.136), channel_id=1, source_target_pairs={{0,4},{1,5},{2,6},{3,7},{4,0},{5,1},{6,2},{7,3},{8,12},{9,13},{10,... | collective-permute-start | bytes 61448 | tf_op jit(solution)/shard_map/ppermute | solution.py:581
  192.6 4.7 %collective-permute-start.61 = (bf16[64,640]{1,0:T(8,128)(2,1)}, bf16[64,640]{1,0:T(8,128)(2,1)S(1)}, u32[]{:S(2)}, u32[]{:S(2)}) collective-permute-start(bf16[64,640]{1,0:T(8,128)(2,1)} %get-tuple-element.135), channel_id=1, source_target_pairs={{0,1},{1,0},{2,3},{3,2},{4,5},{5,4},{6,7},{7,6},{8,9},{9,8},{10,11... | collective-permute-start | bytes 245768 | tf_op jit(solution)/shard_map/ppermute | solution.py:581
  206.4 7.2 %collective-permute-start.65 = (bf16[144,640]{1,0:T(8,128)(2,1)}, bf16[144,640]{1,0:T(8,128)(2,1)S(1)}, u32[]{:S(2)}, u32[]{:S(2)}) collective-permute-start(bf16[144,640]{1,0:T(8,128)(2,1)} %get-tuple-element.137), channel_id=1, source_target_pairs={{0,8},{1,9},{2,10},{3,11},{4,12},{5,13},{6,14},{7,15},{8,16},{9,17... | collective-permute-start | bytes 552968 | tf_op jit(solution)/shard_map/ppermute | solution.py:577
  213.7 5.3 %collective-permute-start.66 = (bf16[80,640]{1,0:T(8,128)(2,1)S(1)}, bf16[80,640]{1,0:T(8,128)(2,1)S(1)}, u32[]{:S(2)}, u32[]{:S(2)}) collective-permute-start(bf16[80,640]{1,0:T(8,128)(2,1)S(1)} %pad_maximum_fusion.2), channel_id=1, source_target_pairs={{0,7},{1,2},{2,1},{3,4},{4,3},{5,6},{6,5},{7,0},{8,15},{9,10},{10,... | collective-permute-start | bytes 307208 | tf_op jit(solution)/shard_map/ppermute | solution.py:581
  228.7 5.6 %collective-permute-start.68 = (bf16[144,320]{1,0:T(8,128)(2,1)}, bf16[144,320]{1,0:T(8,128)(2,1)S(1)}, u32[]{:S(2)}, u32[]{:S(2)}) collective-permute-start(bf16[144,320]{1,0:T(8,128)(2,1)} %get-tuple-element.140), channel_id=1, source_target_pairs={{0,7},{1,2},{2,1},{3,4},{4,3},{5,6},{6,5},{7,0},{8,15},{9,10},{10,... | collective-permute-start | bytes 276488 | tf_op jit(solution)/shard_map/ppermute | solution.py:581
  229.8 4.8 %collective-permute-start.70 = (f32[8,320]{1,0:T(8,128)}, f32[8,320]{1,0:T(8,128)S(1)}, u32[]{:S(2)}, u32[]{:S(2)}) collective-permute-start(f32[8,320]{1,0:T(8,128)} %get-tuple-element.142), channel_id=1, source_target_pairs={{0,2},{1,7},{2,4},{3,1},{4,6},{5,3},{6,0},{7,5},{8,10},{9,15},{10,... | collective-permute-start | bytes 30728 | tf_op jit(solution)/shard_map/ppermute | solution.py:581
  229.8 4.8 %collective-permute-start.71 = (f32[8,320]{1,0:T(8,128)}, f32[8,320]{1,0:T(8,128)S(1)}, u32[]{:S(2)}, u32[]{:S(2)}) collective-permute-start(f32[8,320]{1,0:T(8,128)} %get-tuple-element.142), channel_id=1, source_target_pairs={{0,4},{1,5},{2,6},{3,7},{4,0},{5,1},{6,2},{7,3},{8,12},{9,13},{10,... | collective-permute-start | bytes 30728 | tf_op jit(solution)/shard_map/ppermute | solution.py:581
  231.1 4.3 %collective-permute-start.69 = (bf16[128,320]{1,0:T(8,128)(2,1)}, bf16[128,320]{1,0:T(8,128)(2,1)S(1)}, u32[]{:S(2)}, u32[]{:S(2)}) collective-permute-start(bf16[128,320]{1,0:T(8,128)(2,1)} %get-tuple-element.141), channel_id=1, source_target_pairs={{0,1},{1,0},{2,3},{3,2},{4,5},{5,4},{6,7},{7,6},{8,9},{9,8},{10,11... | collective-permute-start | bytes 245768 | tf_op jit(solution)/shard_map/ppermute | solution.py:581
  246.9 6.3 %collective-permute-start.73 = (bf16[144,320]{1,0:T(8,128)(2,1)}, bf16[144,320]{1,0:T(8,128)(2,1)S(1)}, u32[]{:S(2)}, u32[]{:S(2)}) collective-permute-start(bf16[144,320]{1,0:T(8,128)(2,1)} %get-tuple-element.144), channel_id=1, source_target_pairs={{0,7},{1,2},{2,1},{3,4},{4,3},{5,6},{6,5},{7,0},{8,15},{9,10},{10,... | collective-permute-start | bytes 276488 | tf_op jit(solution)/shard_map/ppermute | solution.py:581
  248.8 4.9 %collective-permute-start.75 = (f32[8,320]{1,0:T(8,128)}, f32[8,320]{1,0:T(8,128)S(1)}, u32[]{:S(2)}, u32[]{:S(2)}) collective-permute-start(f32[8,320]{1,0:T(8,128)} %get-tuple-element.146), channel_id=1, source_target_pairs={{0,2},{1,7},{2,4},{3,1},{4,6},{5,3},{6,0},{7,5},{8,10},{9,15},{10,... | collective-permute-start | bytes 30728 | tf_op jit(solution)/shard_map/ppermute | solution.py:581
  248.9 4.8 %collective-permute-start.76 = (f32[8,320]{1,0:T(8,128)}, f32[8,320]{1,0:T(8,128)S(1)}, u32[]{:S(2)}, u32[]{:S(2)}) collective-permute-start(f32[8,320]{1,0:T(8,128)} %get-tuple-element.146), channel_id=1, source_target_pairs={{0,4},{1,5},{2,6},{3,7},{4,0},{5,1},{6,2},{7,3},{8,12},{9,13},{10,... | collective-permute-start | bytes 30728 | tf_op jit(solution)/shard_map/ppermute | solution.py:581
  250.1 4.4 %collective-permute-start.74 = (bf16[128,320]{1,0:T(8,128)(2,1)}, bf16[128,320]{1,0:T(8,128)(2,1)S(1)}, u32[]{:S(2)}, u32[]{:S(2)}) collective-permute-start(bf16[128,320]{1,0:T(8,128)(2,1)} %get-tuple-element.145), channel_id=1, source_target_pairs={{0,1},{1,0},{2,3},{3,2},{4,5},{5,4},{6,7},{7,6},{8,9},{9,8},{10,11... | collective-permute-start | bytes 245768 | tf_op jit(solution)/shard_map/ppermute | solution.py:581
  264.2 7.1 %collective-permute-start.78 = (bf16[8,16,320]{2,1,0:T(8,128)(2,1)}, bf16[8,16,320]{2,1,0:T(8,128)(2,1)S(1)}, u32[]{:S(2)}, u32[]{:S(2)}) collective-permute-start(bf16[8,16,320]{2,1,0:T(8,128)(2,1)} %get-tuple-element.147), channel_id=1, source_target_pairs={{0,24},{1,25},{2,26},{3,27},{4,28},{5,29},{6,30},{7,31},{8,0},{9,1... | collective-permute-start | bytes 245768 | tf_op jit(solution)/shard_map/ppermute | solution.py:577
  266.4 9.9 %collective-permute-start.79 = (bf16[8,16,320]{2,1,0:T(8,128)(2,1)}, bf16[8,16,320]{2,1,0:T(8,128)(2,1)S(1)}, u32[]{:S(2)}, u32[]{:S(2)}) collective-permute-start(bf16[8,16,320]{2,1,0:T(8,128)(2,1)} %get-tuple-element.148), channel_id=1, source_target_pairs={{0,16},{1,17},{2,18},{3,19},{4,20},{5,21},{6,22},{7,23},{8,24},{9,... | collective-permute-start | bytes 245768 | tf_op jit(solution)/shard_map/ppermute | solution.py:577
  269.4 9.6 %collective-permute-start.80 = (bf16[8,16,320]{2,1,0:T(8,128)(2,1)}, bf16[8,16,320]{2,1,0:T(8,128)(2,1)S(1)}, u32[]{:S(2)}, u32[]{:S(2)}) collective-permute-start(bf16[8,16,320]{2,1,0:T(8,128)(2,1)} %get-tuple-element.149), channel_id=1, source_target_pairs={{0,8},{1,9},{2,10},{3,11},{4,12},{5,13},{6,14},{7,15},{8,16},{9,17... | collective-permute-start | bytes 245768 | tf_op jit(solution)/shard_map/ppermute | solution.py:577
  (92 other events, 426.4 us)

commit v3 on v2

--- a/solution.py
+++ b/solution.py
@@ -661,7 +661,8 @@
             if n == 8:
                 j = min(first + place, 3)
                 mine.append((part, lambda flags, j=j: ((flags[4] // 2) ^ j) * 2 + flags[0]) + span)
-                mine.append((within(part, partner), lambda flags, j=j: ((flags[4] // 2) ^ j) * 2 + 1 - flags[0]) + span)
+                theirs = within(part, partner)
+                mine.append((theirs, lambda flags, j=j: ((flags[4] // 2) ^ j) * 2 + 1 - flags[0]) + span)
             else:
                 mine.append((part, lambda flags, j=place: j) + span)
 
@@ -677,24 +678,21 @@
     sent = send(0, ready[3])
     if n == 8:
         packed += pack_blocks(shape, after(pack.T, sent[0]), bounds[1:])
+    third = send(1)
+    fourth = send(2)
     first = exchange(ready, 0, 0)
-    sent = after(sent, first[3])
-    share(0, sent)
-    sent = send(1, sent)
-    first = (after(first[0], sent[0]),) + first[1:]
+    share(0, after(sent, first[3]))
+    first = (after(first[0], third[0], fourth[0]),) + first[1:]
     hidden = fine_conv(shape, flags, *weights(0, narrow, narrow), first, 1, 0, 2)
     second = exchange(hidden, 0, 0)
-    sent = after(sent, second[3])
-    share(1, sent)
-    sent = send(2, sent)
+    fourth = after(fourth, second[3])
+    opposite = relay(fourth)
+    sent = send(3, second[3])
+    share(1, after(third, second[3]))
+    share(2, fourth)
     second = (after(second[0], sent[0]),) + second[1:]
     (skip,) = fine_conv(shape, flags, *weights(9 * q_rows, narrow, narrow), second, 2, 1, 0, residual=first[:3])
-    sent = after(sent, skip)
-    opposite = relay(sent)
-    share(2, sent)
-    share(2, opposite, 3)
-    sent = send(3, sent)
-    skip = after(skip, sent[0])
+    share(2, after(opposite, skip), 3)
     coarse = down_conv(shape, flags, *weights(18 * q_rows, narrow, wide), skip, 1)
     for section in (1, 2):
         got = exchange(coarse, section - 1, section)
@@ -705,10 +703,10 @@
         hidden = coarse_conv(shape, flags, *weights(0, wide, wide), got, 1)
         if section == 1:
             share(3, after(sent, hidden[3]))
-            hidden, skip = lax.optimization_barrier((hidden, skip))
         then = exchange(hidden, section, section)
         if section == 1:
             share(3, after(opposite, then[3]), 3)
+            then, skip = lax.optimization_barrier((then, skip))
         coarse = coarse_conv(shape, flags, *weights(36 * q_rows, wide, wide), then, 1, residual=got[0])
     got = exchange(coarse, 2, 3, with_stats=False)
     up = up_conv(shape, flags, *weights(0, wide, narrow), got, skip, 1)
@@ -720,7 +718,8 @@
     )
     result = outs[3]
     for target in range(3):
-        result = jnp.where(section_id == target, permute(outs[target], 3, target, lambda i: i), result)
+        pairs = [(3 * n + i, target * n + i) for i in range(n)]
+        result = jnp.where(section_id == target, lax.ppermute(outs[target], ("section", "space"), pairs), result)
     quarter = shape.half // n_section
     result = result.reshape(shape.rows, 2, quarter, narrow).transpose(0, 2, 1, 3)
     return result.reshape(1, shape.rows, 2 * quarter, narrow)

time: 282 us -> 294 us (1.043)
  the two profiles are of different devices: /device:TPU:16 before, /device:TPU:0 now
where the time goes in v3:
time: 294 us; the launch traced here: 293 us
  waiting for transfers between devices  128 us (44%)
  Pallas kernels  83 us (28%)
  starting transfers between devices  58.5 us (20%)
  local copies, waits for them, and re-layouts  17.9 us (6%)
  other arithmetic  4.57 us (2%)
    ppermute x74, waiting for transfers between devices, within(): return lax.ppermute(value, ('section', 'space'), pairs)  99.2 us
    ppermute x74, starting transfers between devices, within(): return lax.ppermute(value, ('section', 'space'), pairs)  50.7 us
    pallas_call x4, Pallas kernels, coarse_conv(): call(body, 1, 5 + extra, len(pieces), outs, scratch_of(weights, rows + 2,...  29.1 us
    ppermute x4, waiting for transfers between devices, permute(): return lax.ppermute(value, ('section', 'space'), pairs)  21.8 us
    pallas_call x2, Pallas kernels, fine_conv(): call(body, 1, 5 + extra, n_pieces, outs, scratch_of(weights, image_rows,...  15.1 us
    unnamed x143, local copies, waits for them, and re-layouts  12.3 us
    pallas_call x1, Pallas kernels, join_conv(): call(body, 1, 6, len(pieces), outs, scratch, flops)  9.77 us
    pallas_call x1, Pallas kernels, up_conv(): call(body, 1, 4, len(pieces), outs, scratch, flops)  9.12 us
  transfers between devices with their start and end apart: 81, of which 39 were waited for; matrix products, arithmetic and copies ran while one was open for 2% of the time, Pallas kernels for 7%

profile of v3, /device:TPU:0, one launch (start us, length us, event | category | flops | bytes accessed | tf_op | source)
XLA Modules:
  0.0 293.3 jit_solution(6964352259508462803)
XLA Ops:
  0.0 1.2 copy.5
  2.7 2.0 shard_map.28
  4.7 3.4 %collective-permute-start = (bf16[144,320]{1,0:T(8,128)(2,1)}, bf16[144,320]{1,0:T(8,128)(2,1)S(1)}, u32[]{:S(2)}, u32[]{:S(2)}) collective-permute-start(bf16[144,320]{1,0:T(8,128)(2,1)} %get-tuple-element.85), channel_id=1, source_target_pairs={{0,7},{1,2},{2,1},{3,4},{4,3},{5,6},{6,5},{7,0},{8,15},{9,10},{10,... | collective-permute-start | bytes 276488 | tf_op jit(solution)/shard_map/ppermute | solution.py:581
  9.4 1.8 shard_map.29.rest_0_
  11.1 2.4 collective-permute-start.5
  15.3 5.3 %collective-permute-done.5.rest_2_ = bf16[80,1536]{1,0:T(8,128)(2,1)S(1)} collective-permute-done((bf16[80,1536]{1,0:T(8,128)(2,1)}, bf16[80,1536]{1,0:T(8,128)(2,1)S(1)}, u32[]{:S(2)}, u32[]{:S(2)}) %collective-permute-start.5) | collective-permute-done | bytes 245792 | tf_op jit(solution)/shard_map/ppermute | solution.py:581
  20.5 5.3 %collective-permute-done.6.rest_4_ = bf16[80,1536]{1,0:T(8,128)(2,1)S(1)} collective-permute-done((bf16[80,1536]{1,0:T(8,128)(2,1)}, bf16[80,1536]{1,0:T(8,128)(2,1)S(1)}, u32[]{:S(2)}, u32[]{:S(2)}) %collective-permute-start.6) | collective-permute-done | bytes 245792 | tf_op jit(solution)/shard_map/ppermute | solution.py:581
  26.9 1.8 collective-permute-done.1.inner.rest_2_
  28.9 3.1 %shard_map.30 = (bf16[80,1536]{1,0:T(8,128)(2,1)}, bf16[80,3072]{1,0:T(8,128)(2,1)}, bf16[80,6144]{1,0:T(8,128)(2,1)}) custom-call(bf16[80,11520]{1,0:T(8,128)(2,1)} %bitcast.16), custom_call_target="tpu_custom_call" | custom-call | flops 1000 | bytes 4000000 | tf_op jit(solution)/shard_map/pallas_call | solution.py:556
  33.7 6.9 %shard_map.31 = (bf16[528,320]{1,0:T(8,128)(2,1)}, bf16[272,320]{1,0:T(8,128)(2,1)}, bf16[256,320]{1,0:T(8,128)(2,1)}, f32[8,320]{1,0:T(8,128)}) custom-call(s32[5]{0:T(128)} %stack.31.flags, bf16[528,320]{1,0:T(8,128)(2,1)} %get-tuple-element.84.block.rest_0_, bf16[144,320]{1,0:T(8,128)(2,1)} %copy-done.59, bf16[128,320]{1,0:T(8,128)(2,1)} %copy-done.64, ...), custom_call_target="tpu_custom_call" | custom-call | flops 943718400 | bytes 4000000 | tf_op jit(solution)/shard_map/pallas_call | solution.py:308
  40.6 1.2 collective-permute-start.12
  42.7 1.1 collective-permute-start.18
  43.8 1.8 collective-permute-start.24
  45.8 3.2 %collective-permute-done.12.outer = bf16[272,320]{1,0:T(8,128)(2,1)S(1)} collective-permute-done((bf16[272,320]{1,0:T(8,128)(2,1)}, bf16[272,320]{1,0:T(8,128)(2,1)S(1)}, u32[]{:S(2)}, u32[]{:S(2)}) %collective-permute-start.12) | collective-permute-done | bytes 174112 | tf_op jit(solution)/shard_map/ppermute | solution.py:581
  49.6 3.3 %collective-permute-done.14 = f32[8,320]{1,0:T(8,128)S(1)} collective-permute-done((f32[8,320]{1,0:T(8,128)}, f32[8,320]{1,0:T(8,128)S(1)}, u32[]{:S(2)}, u32[]{:S(2)}) %collective-permute-start.14) | collective-permute-done | bytes 10272 | tf_op jit(solution)/shard_map/ppermute | solution.py:581
  52.9 1.2 collective-permute-start.19
  54.1 11.4 %collective-permute-done.13 = f32[8,320]{1,0:T(8,128)S(1)} collective-permute-done((f32[8,320]{1,0:T(8,128)}, f32[8,320]{1,0:T(8,128)S(1)}, u32[]{:S(2)}, u32[]{:S(2)}) %collective-permute-start.13) | collective-permute-done | bytes 10272 | tf_op jit(solution)/shard_map/ppermute | solution.py:581
  67.3 3.4 %collective-permute-done.19.rest_9_.rest_14_ = bf16[80,1536]{1,0:T(8,128)(2,1)S(1)} collective-permute-done((bf16[80,1536]{1,0:T(8,128)(2,1)S(1)}, bf16[80,1536]{1,0:T(8,128)(2,1)S(1)}, u32[]{:S(2)}, u32[]{:S(2)}) %collective-permute-start.19) | collective-permute-done | bytes 245792 | tf_op jit(solution)/shard_map/ppermute | solution.py:581
  71.7 9.4 %collective-permute-done.25.rest_4_.rest_20_ = bf16[80,3072]{1,0:T(8,128)(2,1)S(1)} collective-permute-done((bf16[80,3072]{1,0:T(8,128)(2,1)S(1)}, bf16[80,3072]{1,0:T(8,128)(2,1)S(1)}, u32[]{:S(2)}, u32[]{:S(2)}) %collective-permute-start.25) | collective-permute-done | bytes 491552 | tf_op jit(solution)/shard_map/ppermute | solution.py:581
  81.1 1.6 collective-permute-done.15.inner
  84.3 1.1 collective-permute-start.29
  87.8 8.1 %shard_map.32.skip_ref = bf16[768,384]{1,0:T(8,128)(2,1)} custom-call(s32[5]{0:T(128)} %stack.31.flags, bf16[528,320]{1,0:T(8,128)(2,1)} %get-tuple-element.96.block, bf16[272,320]{1,0:T(8,128)(2,1)} %copy-done.61, bf16[256,320]{1,0:T(8,128)(2,1)} %copy-done.62, f32[8,320]{1,0:T(8,128)} %copy-done.55, f32[8,320]{1,0:T(8,128)} %copy-done.68, ...), custom_call_target="tpu_custom_call" | custom-call | flops 1415577600 | bytes 4000000 | tf_op jit(solution)/shard_map/pallas_call | solution.py:308
  96.5 1.2 collective-permute-done.31.rest_7_.rest_23_
  100.4 5.2 %shard_map.33 = (bf16[144,640]{1,0:T(8,128)(2,1)}, bf16[80,640]{1,0:T(8,128)(2,1)}, bf16[64,640]{1,0:T(8,128)(2,1)}, f32[8,640]{1,0:T(8,128)}) custom-call(s32[5]{0:T(128)} %stack.31.flags, bf16[768,384]{1,0:T(8,128)(2,1)} %shard_map.32.skip_ref, bf16[80,3072]{1,0:T(8,128)(2,1)} %get-tuple-element.102.rest_0_.rest_16_, bf16[80,3072]{1,0:T(8,128)(2,1)} %copy-done.10, ...), custom_call_target="tpu_custom_call" | custom-call | flops 471859200 | bytes 4000000 | tf_op jit(solution)/shard_map/pallas_call | solution.py:345
  105.5 1.6 collective-permute-start.33
  107.2 1.1 collective-permute-start.45
  109.2 5.1 %collective-permute-done.33.block.rest_0_ = bf16[144,640]{1,0:T(8,128)(2,1)S(1)} collective-permute-done((bf16[144,640]{1,0:T(8,128)(2,1)}, bf16[144,640]{1,0:T(8,128)(2,1)S(1)}, u32[]{:S(2)}, u32[]{:S(2)}) %collective-permute-start.33) | collective-permute-done | bytes 184352 | tf_op jit(solution)/shard_map/ppermute | solution.py:577
  115.1 1.1 collective-permute-start.37
  116.7 15.1 %collective-permute-done.34.outer = bf16[80,640]{1,0:T(8,128)(2,1)S(1)} collective-permute-done((bf16[80,640]{1,0:T(8,128)(2,1)S(1)}, bf16[80,640]{1,0:T(8,128)(2,1)S(1)}, u32[]{:S(2)}, u32[]{:S(2)}) %collective-permute-start.34) | collective-permute-done | bytes 102432 | tf_op jit(solution)/shard_map/ppermute | solution.py:581
  131.8 1.3 collective-permute-done.37
  135.2 1.5 collective-permute-start.50
  139.2 7.2 %shard_map.34 = (bf16[144,640]{1,0:T(8,128)(2,1)}, bf16[80,640]{1,0:T(8,128)(2,1)}, bf16[64,640]{1,0:T(8,128)(2,1)}, f32[8,640]{1,0:T(8,128)}) custom-call(s32[5]{0:T(128)} %stack.31.flags, bf16[144,640]{1,0:T(8,128)(2,1)} %copy-done.17, bf16[80,640]{1,0:T(8,128)(2,1)} %copy-done.37, bf16[64,640]{1,0:T(8,128)(2,1)} %copy-done.45, f32[8,640]{1,0:T(8,128)} %copy-done.47, ...), custom_call_target="tpu_custom_call" | custom-call | flops 943718400 | bytes 4000000 | tf_op jit(solution)/shard_map/pallas_call | solution.py:381
  148.3 1.8 collective-permute-start.41
  150.1 1.5 collective-permute-done.42
  151.6 2.4 collective-permute-start.44
  154.7 1.7 collective-permute-start.51
  157.2 11.3 %collective-permute-done.51.rest_9_ = bf16[80,3072]{1,0:T(8,128)(2,1)S(1)} collective-permute-done((bf16[80,3072]{1,0:T(8,128)(2,1)}, bf16[80,3072]{1,0:T(8,128)(2,1)S(1)}, u32[]{:S(2)}, u32[]{:S(2)}) %collective-permute-start.51) | collective-permute-done | bytes 491552 | tf_op jit(solution)/shard_map/ppermute | solution.py:581
  168.5 1.3 collective-permute-done.43.sb
  173.2 7.3 %shard_map.35 = (bf16[144,640]{1,0:T(8,128)(2,1)}, bf16[80,640]{1,0:T(8,128)(2,1)}, bf16[64,640]{1,0:T(8,128)(2,1)}, f32[8,640]{1,0:T(8,128)}) custom-call(s32[5]{0:T(128)} %stack.31.flags, bf16[144,640]{1,0:T(8,128)(2,1)} %get-tuple-element.120.block, bf16[80,640]{1,0:T(8,128)(2,1)} %copy-done.36, bf16[64,640]{1,0:T(8,128)(2,1)} %copy-done.42, ...), custom_call_target="tpu_custom_call" | custom-call | flops 943718400 | bytes 4000000 | tf_op jit(solution)/shard_map/pallas_call | solution.py:381
  181.4 7.9 %collective-permute-done.54.block.rest_0_ = bf16[144,640]{1,0:T(8,128)(2,1)S(1)} collective-permute-done((bf16[144,640]{1,0:T(8,128)(2,1)}, bf16[144,640]{1,0:T(8,128)(2,1)S(1)}, u32[]{:S(2)}, u32[]{:S(2)}) %collective-permute-start.54) | collective-permute-done | bytes 184352 | tf_op jit(solution)/shard_map/ppermute | solution.py:577
  189.4 1.4 collective-permute-start.55
  193.2 2.3 collective-permute-done.55.outer
  196.4 1.2 collective-permute-done.59.sb
  198.2 7.2 %shard_map.36 = (bf16[144,640]{1,0:T(8,128)(2,1)}, bf16[80,640]{1,0:T(8,128)(2,1)}, bf16[64,640]{1,0:T(8,128)(2,1)}, f32[8,640]{1,0:T(8,128)}) custom-call(s32[5]{0:T(128)} %stack.31.flags, bf16[144,640]{1,0:T(8,128)(2,1)} %copy-done.18, bf16[80,640]{1,0:T(8,128)(2,1)} %copy-done.38, bf16[64,640]{1,0:T(8,128)(2,1)} %copy-done.44, f32[8,640]{1,0:T(8,128)} %copy-done.49, ...), custom_call_target="tpu_custom_call" | custom-call | flops 943718400 | bytes 4000000 | tf_op jit(solution)/shard_map/pallas_call | solution.py:381
  206.1 1.1 collective-permute-start.63
  207.2 1.3 collective-permute-start.62
  209.2 2.3 collective-permute-done.60.outer
  213.1 1.2 collective-permute-done.64.sb
  214.8 7.3 %shard_map.37 = (bf16[144,640]{1,0:T(8,128)(2,1)}, bf16[80,640]{1,0:T(8,128)(2,1)}, bf16[64,640]{1,0:T(8,128)(2,1)}, f32[8,640]{1,0:T(8,128)}) custom-call(s32[5]{0:T(128)} %stack.31.flags, bf16[144,640]{1,0:T(8,128)(2,1)} %get-tuple-element.133.block, bf16[80,640]{1,0:T(8,128)(2,1)} %copy-done.39, bf16[64,640]{1,0:T(8,128)(2,1)} %copy-done.43, ...), custom_call_target="tpu_custom_call" | custom-call | flops 943718400 | bytes 4000000 | tf_op jit(solution)/shard_map/pallas_call | solution.py:381
  222.5 8.7 %collective-permute-done.65.block = bf16[144,640]{1,0:T(8,128)(2,1)S(1)} collective-permute-done((bf16[144,640]{1,0:T(8,128)(2,1)}, bf16[144,640]{1,0:T(8,128)(2,1)S(1)}, u32[]{:S(2)}, u32[]{:S(2)}) %collective-permute-start.65) | collective-permute-done | bytes 184352 | tf_op jit(solution)/shard_map/ppermute | solution.py:577
  232.9 3.4 %collective-permute-done.66.outer = bf16[80,640]{1,0:T(8,128)(2,1)S(1)} collective-permute-done((bf16[80,640]{1,0:T(8,128)(2,1)S(1)}, bf16[80,640]{1,0:T(8,128)(2,1)S(1)}, u32[]{:S(2)}, u32[]{:S(2)}) %collective-permute-start.66) | collective-permute-done | bytes 102432 | tf_op jit(solution)/shard_map/ppermute | solution.py:581
  236.9 9.1 %shard_map.38 = (bf16[528,320]{1,0:T(8,128)(2,1)}, bf16[144,320]{1,0:T(8,128)(2,1)}, bf16[128,320]{1,0:T(8,128)(2,1)}, f32[8,320]{1,0:T(8,128)}) custom-call(s32[5]{0:T(128)} %stack.31.flags, bf16[144,640]{1,0:T(8,128)(2,1)} %copy-done.35, bf16[80,640]{1,0:T(8,128)(2,1)} %copy-done.63, bf16[64,640]{1,0:T(8,128)(2,1)} %copy-done.67, ...), custom_call_target="tpu_custom_call" | custom-call | flops 1887436800 | bytes 4000000 | tf_op jit(solution)/shard_map/pallas_call | solution.py:420
  246.1 1.1 collective-permute-start.68
  248.0 1.8 collective-permute-start.69
  249.7 1.7 collective-permute-done.68.outer
  251.5 1.2 collective-permute-done.70
  253.5 1.1 collective-permute-done.72.sb
  255.2 9.8 %shard_map.39 = (bf16[528,320]{1,0:T(8,128)(2,1)}, bf16[144,320]{1,0:T(8,128)(2,1)}, bf16[128,320]{1,0:T(8,128)(2,1)}, f32[8,320]{1,0:T(8,128)}) custom-call(s32[5]{0:T(128)} %stack.31.flags, bf16[528,320]{1,0:T(8,128)(2,1)} %get-tuple-element.139.block.u_ref, bf16[144,320]{1,0:T(8,128)(2,1)} %copy-done.60, bf16[128,320]{1,0:T(8,128)(2,1)} %copy-done.66, ...), custom_call_target="tpu_custom_call" | custom-call | flops 1887436800 | bytes 4000000 | tf_op jit(solution)/shard_map/pallas_call | solution.py:461
  266.5 1.6 collective-permute-start.75
  268.8 2.6 collective-permute-done.73.outer
  272.7 1.1 collective-permute-done.77.sb
  274.4 7.9 %shard_map.40 = (bf16[8,16,320]{2,1,0:T(8,128)(2,1)}, bf16[8,16,320]{2,1,0:T(8,128)(2,1)}, bf16[8,16,320]{2,1,0:T(8,128)(2,1)}, bf16[8,16,320]{2,1,0:T(8,128)(2,1)}) custom-call(s32[5]{0:T(128)} %stack.31.flags, bf16[528,320]{1,0:T(8,128)(2,1)} %get-tuple-element.143.block, bf16[144,320]{1,0:T(8,128)(2,1)} %copy-done.40, bf16[128,320]{1,0:T(8,128)(2,1)} %copy-done.41, ...), custom_call_target="tpu_custom_call" | custom-call | flops 1153433600 | bytes 4000000 | tf_op jit(solution)/shard_map/pallas_call | solution.py:534
  283.7 1.3 collective-permute-start.80
  285.0 7.4 %collective-permute-done.80 = bf16[8,16,320]{2,1,0:T(8,128)(2,1)S(1)} collective-permute-done((bf16[8,16,320]{2,1,0:T(8,128)(2,1)}, bf16[8,16,320]{2,1,0:T(8,128)(2,1)S(1)}, u32[]{:S(2)}, u32[]{:S(2)}) %collective-permute-start.80) | collective-permute-done | bytes 81952 | tf_op jit(solution)/shard_map/ppermute | solution.py:722
  (304 shorter events, 51.3 us)
Async XLA Ops:
  4.7 9.3 %collective-permute-start = (bf16[144,320]{1,0:T(8,128)(2,1)}, bf16[144,320]{1,0:T(8,128)(2,1)S(1)}, u32[]{:S(2)}, u32[]{:S(2)}) collective-permute-start(bf16[144,320]{1,0:T(8,128)(2,1)} %get-tuple-element.85), channel_id=1, source_target_pairs={{0,7},{1,2},{2,1},{3,4},{4,3},{5,6},{6,5},{7,0},{8,15},{9,10},{10,... | collective-permute-start | bytes 276488 | tf_op jit(solution)/shard_map/ppermute | solution.py:581
  8.2 7.0 %collective-permute-start.3 = (f32[8,320]{1,0:T(8,128)}, f32[8,320]{1,0:T(8,128)S(1)}, u32[]{:S(2)}, u32[]{:S(2)}) collective-permute-start(f32[8,320]{1,0:T(8,128)} %get-tuple-element.79), channel_id=1, source_target_pairs={{0,4},{1,5},{2,6},{3,7},{4,0},{5,1},{6,2},{7,3},{8,12},{9,13},{10,... | collective-permute-start | bytes 30728 | tf_op jit(solution)/shard_map/ppermute | solution.py:581
  8.7 6.5 %collective-permute-start.2 = (f32[8,320]{1,0:T(8,128)}, f32[8,320]{1,0:T(8,128)S(1)}, u32[]{:S(2)}, u32[]{:S(2)}) collective-permute-start(f32[8,320]{1,0:T(8,128)} %get-tuple-element.79), channel_id=1, source_target_pairs={{0,2},{1,7},{2,4},{3,1},{4,6},{5,3},{6,0},{7,5},{8,10},{9,15},{10,... | collective-permute-start | bytes 30728 | tf_op jit(solution)/shard_map/ppermute | solution.py:581
  11.1 9.4 %collective-permute-start.5 = (bf16[80,1536]{1,0:T(8,128)(2,1)}, bf16[80,1536]{1,0:T(8,128)(2,1)S(1)}, u32[]{:S(2)}, u32[]{:S(2)}) collective-permute-start(bf16[80,1536]{1,0:T(8,128)(2,1)} %shard_map.29.rest_0_), channel_id=1, source_target_pairs={{0,2},{1,3},{2,0},{3,1},{4,6},{5,7},{6,4},{7,5},{8,10},{9,11},{10,... | collective-permute-start | bytes 737288 | tf_op jit(solution)/shard_map/ppermute | solution.py:581
  13.5 12.3 %collective-permute-start.6 = (bf16[80,1536]{1,0:T(8,128)(2,1)}, bf16[80,1536]{1,0:T(8,128)(2,1)S(1)}, u32[]{:S(2)}, u32[]{:S(2)}) collective-permute-start(bf16[80,1536]{1,0:T(8,128)(2,1)} %shard_map.29.rest_0_), channel_id=1, source_target_pairs={{0,4},{1,5},{2,6},{3,7},{4,0},{5,1},{6,2},{7,3},{8,12},{9,13},{10,... | collective-permute-start | bytes 737288 | tf_op jit(solution)/shard_map/ppermute | solution.py:581
  14.1 11.7 %collective-permute-start.7 = (bf16[80,1536]{1,0:T(8,128)(2,1)}, bf16[80,1536]{1,0:T(8,128)(2,1)S(1)}, u32[]{:S(2)}, u32[]{:S(2)}) collective-permute-start(bf16[80,1536]{1,0:T(8,128)(2,1)} %shard_map.29.rest_0_), channel_id=1, source_target_pairs={{0,6},{1,7},{2,4},{3,5},{4,2},{5,3},{6,0},{7,1},{8,14},{9,15},{10,... | collective-permute-start | bytes 737288 | tf_op jit(solution)/shard_map/ppermute | solution.py:581
  25.8 6.3 %collective-permute-start.8 = (bf16[80,1536]{1,0:T(8,128)(2,1)}, bf16[80,1536]{1,0:T(8,128)(2,1)S(1)}, u32[]{:S(2)}, u32[]{:S(2)}) collective-permute-start(bf16[80,1536]{1,0:T(8,128)(2,1)} %shard_map.29.rest_0_), channel_id=1, source_target_pairs={{0,1},{1,0},{2,3},{3,2},{4,5},{5,4},{6,7},{7,6},{8,9},{9,8},{10,11... | collective-permute-start | bytes 737288 | tf_op jit(solution)/shard_map/ppermute | solution.py:581
  25.9 6.2 %collective-permute-start.9 = (bf16[80,1536]{1,0:T(8,128)(2,1)S(1)}, bf16[80,1536]{1,0:T(8,128)(2,1)S(1)}, u32[]{:S(2)}, u32[]{:S(2)}) collective-permute-start(bf16[80,1536]{1,0:T(8,128)(2,1)S(1)} %collective-permute-done.5.rest_2_), channel_id=1, source_target_pairs={{0,1},{1,0},{2,3},{3,2},{4,5},{5,4},{6,7},{7,6},{8,9},{9,8},{10,11... | collective-permute-start | bytes 737288 | tf_op jit(solution)/shard_map/ppermute | solution.py:581
  26.4 5.8 %collective-permute-start.10 = (bf16[80,1536]{1,0:T(8,128)(2,1)S(1)}, bf16[80,1536]{1,0:T(8,128)(2,1)S(1)}, u32[]{:S(2)}, u32[]{:S(2)}) collective-permute-start(bf16[80,1536]{1,0:T(8,128)(2,1)S(1)} %collective-permute-done.6.rest_4_), channel_id=1, source_target_pairs={{0,1},{1,0},{2,3},{3,2},{4,5},{5,4},{6,7},{7,6},{8,9},{9,8},{10,11... | collective-permute-start | bytes 737288 | tf_op jit(solution)/shard_map/ppermute | solution.py:581
  26.4 5.7 %collective-permute-start.11 = (bf16[80,1536]{1,0:T(8,128)(2,1)S(1)}, bf16[80,1536]{1,0:T(8,128)(2,1)S(1)}, u32[]{:S(2)}, u32[]{:S(2)}) collective-permute-start(bf16[80,1536]{1,0:T(8,128)(2,1)S(1)} %collective-permute-done.7.rest_6_), channel_id=1, source_target_pairs={{0,1},{1,0},{2,3},{3,2},{4,5},{5,4},{6,7},{7,6},{8,9},{9,8},{10,11... | collective-permute-start | bytes 737288 | tf_op jit(solution)/shard_map/ppermute | solution.py:581
  28.8 3.3 %collective-permute-start.4 = (f32[8,320]{1,0:T(8,128)S(1)}, f32[8,320]{1,0:T(8,128)S(1)}, u32[]{:S(2)}, u32[]{:S(2)}) collective-permute-start(f32[8,320]{1,0:T(8,128)S(1)} %fusion.9.sa), channel_id=1, source_target_pairs={{0,1},{1,0},{2,3},{3,2},{4,5},{5,4},{6,7},{7,6},{8,9},{9,8},{10,11... | collective-permute-start | bytes 30728 | tf_op jit(solution)/shard_map/ppermute | solution.py:581
  40.6 8.5 %collective-permute-start.12 = (bf16[272,320]{1,0:T(8,128)(2,1)}, bf16[272,320]{1,0:T(8,128)(2,1)S(1)}, u32[]{:S(2)}, u32[]{:S(2)}) collective-permute-start(bf16[272,320]{1,0:T(8,128)(2,1)} %get-tuple-element.94), channel_id=1, source_target_pairs={{0,7},{1,2},{2,1},{3,4},{4,3},{5,6},{6,5},{7,0},{8,15},{9,10},{10,... | collective-permute-start | bytes 522248 | tf_op jit(solution)/shard_map/ppermute | solution.py:581
  41.8 25.5 %collective-permute-start.17 = (bf16[80,1536]{1,0:T(8,128)(2,1)S(1)}, bf16[80,1536]{1,0:T(8,128)(2,1)S(1)}, u32[]{:S(2)}, u32[]{:S(2)}) collective-permute-start(bf16[80,1536]{1,0:T(8,128)(2,1)S(1)} %copy-done.26), channel_id=1, source_target_pairs={{0,2},{1,3},{2,0},{3,1},{4,6},{5,7},{6,4},{7,5},{8,10},{9,11},{10,... | collective-permute-start | bytes 737288 | tf_op jit(solution)/shard_map/ppermute | solution.py:581
  42.7 24.6 %collective-permute-start.18 = (bf16[80,1536]{1,0:T(8,128)(2,1)S(1)}, bf16[80,1536]{1,0:T(8,128)(2,1)S(1)}, u32[]{:S(2)}, u32[]{:S(2)}) collective-permute-start(bf16[80,1536]{1,0:T(8,128)(2,1)S(1)} %copy-done.26), channel_id=1, source_target_pairs={{0,4},{1,5},{2,6},{3,7},{4,0},{5,1},{6,2},{7,3},{8,12},{9,13},{10,... | collective-permute-start | bytes 737288 | tf_op jit(solution)/shard_map/ppermute | solution.py:581
  43.8 27.4 %collective-permute-start.24 = (bf16[80,3072]{1,0:T(8,128)(2,1)S(1)}, bf16[80,3072]{1,0:T(8,128)(2,1)S(1)}, u32[]{:S(2)}, u32[]{:S(2)}) collective-permute-start(bf16[80,3072]{1,0:T(8,128)(2,1)S(1)} %copy-done.8), channel_id=1, source_target_pairs={{0,2},{1,3},{2,0},{3,1},{4,6},{5,7},{6,4},{7,5},{8,10},{9,11},{10,... | collective-permute-start | bytes 1474568 | tf_op jit(solution)/shard_map/ppermute | solution.py:581
  45.6 7.3 %collective-permute-start.14 = (f32[8,320]{1,0:T(8,128)}, f32[8,320]{1,0:T(8,128)S(1)}, u32[]{:S(2)}, u32[]{:S(2)}) collective-permute-start(f32[8,320]{1,0:T(8,128)} %get-tuple-element.93), channel_id=1, source_target_pairs={{0,4},{1,5},{2,6},{3,7},{4,0},{5,1},{6,2},{7,3},{8,12},{9,13},{10,... | collective-permute-start | bytes 30728 | tf_op jit(solution)/shard_map/ppermute | solution.py:581
  49.1 16.4 %collective-permute-start.13 = (f32[8,320]{1,0:T(8,128)}, f32[8,320]{1,0:T(8,128)S(1)}, u32[]{:S(2)}, u32[]{:S(2)}) collective-permute-start(f32[8,320]{1,0:T(8,128)} %get-tuple-element.93), channel_id=1, source_target_pairs={{0,2},{1,7},{2,4},{3,1},{4,6},{5,3},{6,0},{7,5},{8,10},{9,15},{10,... | collective-permute-start | bytes 30728 | tf_op jit(solution)/shard_map/ppermute | solution.py:581
  52.9 17.8 %collective-permute-start.19 = (bf16[80,1536]{1,0:T(8,128)(2,1)S(1)}, bf16[80,1536]{1,0:T(8,128)(2,1)S(1)}, u32[]{:S(2)}, u32[]{:S(2)}) collective-permute-start(bf16[80,1536]{1,0:T(8,128)(2,1)S(1)} %copy-done.26), channel_id=1, source_target_pairs={{0,6},{1,7},{2,4},{3,5},{4,2},{5,3},{6,0},{7,1},{8,14},{9,15},{10,... | collective-permute-start | bytes 737288 | tf_op jit(solution)/shard_map/ppermute | solution.py:581
  65.5 15.6 %collective-permute-start.25 = (bf16[80,3072]{1,0:T(8,128)(2,1)S(1)}, bf16[80,3072]{1,0:T(8,128)(2,1)S(1)}, u32[]{:S(2)}, u32[]{:S(2)}) collective-permute-start(bf16[80,3072]{1,0:T(8,128)(2,1)S(1)} %copy-done.8), channel_id=1, source_target_pairs={{0,4},{1,5},{2,6},{3,7},{4,0},{5,1},{6,2},{7,3},{8,12},{9,13},{10,... | collective-permute-start | bytes 1474568 | tf_op jit(solution)/shard_map/ppermute | solution.py:581
  70.7 14.8 %collective-permute-start.20 = (bf16[80,1536]{1,0:T(8,128)(2,1)S(1)}, bf16[80,1536]{1,0:T(8,128)(2,1)S(1)}, u32[]{:S(2)}, u32[]{:S(2)}) collective-permute-start(bf16[80,1536]{1,0:T(8,128)(2,1)S(1)} %copy-done.26), channel_id=1, source_target_pairs={{0,1},{1,0},{2,3},{3,2},{4,5},{5,4},{6,7},{7,6},{8,9},{9,8},{10,11... | collective-permute-start | bytes 737288 | tf_op jit(solution)/shard_map/ppermute | solution.py:581
  70.7 15.7 %collective-permute-start.21 = (bf16[80,1536]{1,0:T(8,128)(2,1)S(1)}, bf16[80,1536]{1,0:T(8,128)(2,1)S(1)}, u32[]{:S(2)}, u32[]{:S(2)}) collective-permute-start(bf16[80,1536]{1,0:T(8,128)(2,1)S(1)} %collective-permute-done.17.rest_5_.rest_10_), channel_id=1, source_target_pairs={{0,1},{1,0},{2,3},{3,2},{4,5},{5,4},{6,7},{7,6},{8,9},{9,8},{10,11... | collective-permute-start | bytes 737288 | tf_op jit(solution)/shard_map/ppermute | solution.py:581
  71.2 15.2 %collective-permute-start.22 = (bf16[80,1536]{1,0:T(8,128)(2,1)S(1)}, bf16[80,1536]{1,0:T(8,128)(2,1)S(1)}, u32[]{:S(2)}, u32[]{:S(2)}) collective-permute-start(bf16[80,1536]{1,0:T(8,128)(2,1)S(1)} %collective-permute-done.18.rest_7_.rest_12_), channel_id=1, source_target_pairs={{0,1},{1,0},{2,3},{3,2},{4,5},{5,4},{6,7},{7,6},{8,9},{9,8},{10,11... | collective-permute-start | bytes 737288 | tf_op jit(solution)/shard_map/ppermute | solution.py:581
  71.2 15.7 %collective-permute-start.23 = (bf16[80,1536]{1,0:T(8,128)(2,1)S(1)}, bf16[80,1536]{1,0:T(8,128)(2,1)S(1)}, u32[]{:S(2)}, u32[]{:S(2)}) collective-permute-start(bf16[80,1536]{1,0:T(8,128)(2,1)S(1)} %collective-permute-done.19.rest_9_.rest_14_), channel_id=1, source_target_pairs={{0,1},{1,0},{2,3},{3,2},{4,5},{5,4},{6,7},{7,6},{8,9},{9,8},{10,11... | collective-permute-start | bytes 737288 | tf_op jit(solution)/shard_map/ppermute | solution.py:581
  84.3 11.6 %collective-permute-start.29 = (bf16[80,1536]{1,0:T(8,128)(2,1)}, bf16[80,1536]{1,0:T(8,128)(2,1)}, u32[]{:S(2)}, u32[]{:S(2)}) collective-permute-start(bf16[80,1536]{1,0:T(8,128)(2,1)} %slice.275), channel_id=1, source_target_pairs={{0,4},{1,5},{2,6},{3,7},{4,0},{5,1},{6,2},{7,3},{8,12},{9,13},{10,... | collective-permute-start | bytes 737288 | tf_op jit(solution)/shard_map/ppermute | solution.py:581
  85.4 10.5 %collective-permute-start.30 = (bf16[80,1536]{1,0:T(8,128)(2,1)}, bf16[80,1536]{1,0:T(8,128)(2,1)}, u32[]{:S(2)}, u32[]{:S(2)}) collective-permute-start(bf16[80,1536]{1,0:T(8,128)(2,1)} %slice.276), channel_id=1, source_target_pairs={{0,2},{1,3},{2,0},{3,1},{4,6},{5,7},{6,4},{7,5},{8,10},{9,11},{10,... | collective-permute-start | bytes 737288 | tf_op jit(solution)/shard_map/ppermute | solution.py:581
  86.4 11.7 %collective-permute-start.27 = (bf16[80,3072]{1,0:T(8,128)(2,1)S(1)}, bf16[80,3072]{1,0:T(8,128)(2,1)S(1)}, u32[]{:S(2)}, u32[]{:S(2)}) collective-permute-start(bf16[80,3072]{1,0:T(8,128)(2,1)S(1)} %collective-permute-done.24.rest_2_.rest_18_), channel_id=1, source_target_pairs={{0,1},{1,0},{2,3},{3,2},{4,5},{5,4},{6,7},{7,6},{8,9},{9,8},{10,11... | collective-permute-start | bytes 1474568 | tf_op jit(solution)/shard_map/ppermute | solution.py:581
  86.5 11.6 %collective-permute-start.26 = (bf16[80,3072]{1,0:T(8,128)(2,1)S(1)}, bf16[80,3072]{1,0:T(8,128)(2,1)S(1)}, u32[]{:S(2)}, u32[]{:S(2)}) collective-permute-start(bf16[80,3072]{1,0:T(8,128)(2,1)S(1)} %copy-done.8), channel_id=1, source_target_pairs={{0,1},{1,0},{2,3},{3,2},{4,5},{5,4},{6,7},{7,6},{8,9},{9,8},{10,11... | collective-permute-start | bytes 1474568 | tf_op jit(solution)/shard_map/ppermute | solution.py:581
  87.0 11.8 %collective-permute-start.28 = (bf16[80,3072]{1,0:T(8,128)(2,1)S(1)}, bf16[80,3072]{1,0:T(8,128)(2,1)S(1)}, u32[]{:S(2)}, u32[]{:S(2)}) collective-permute-start(bf16[80,3072]{1,0:T(8,128)(2,1)S(1)} %collective-permute-done.25.rest_4_.rest_20_), channel_id=1, source_target_pairs={{0,1},{1,0},{2,3},{3,2},{4,5},{5,4},{6,7},{7,6},{8,9},{9,8},{10,11... | collective-permute-start | bytes 1474568 | tf_op jit(solution)/shard_map/ppermute | solution.py:581
  105.5 8.8 %collective-permute-start.33 = (bf16[144,640]{1,0:T(8,128)(2,1)}, bf16[144,640]{1,0:T(8,128)(2,1)S(1)}, u32[]{:S(2)}, u32[]{:S(2)}) collective-permute-start(bf16[144,640]{1,0:T(8,128)(2,1)} %get-tuple-element.109), channel_id=1, source_target_pairs={{0,8},{1,9},{2,10},{3,11},{4,12},{5,13},{6,14},{7,15},{8,16},{9,17... | collective-permute-start | bytes 552968 | tf_op jit(solution)/shard_map/ppermute | solution.py:577
  107.2 26.2 %collective-permute-start.45 = (bf16[80,6144]{1,0:T(8,128)(2,1)S(1)}, bf16[80,6144]{1,0:T(8,128)(2,1)S(1)}, u32[]{:S(2)}, u32[]{:S(2)}) collective-permute-start(bf16[80,6144]{1,0:T(8,128)(2,1)S(1)} %copy-done.2), channel_id=1, source_target_pairs={{0,2},{1,3},{2,0},{3,1},{4,6},{5,7},{6,4},{7,5},{8,10},{9,11},{10,... | collective-permute-start | bytes 2949128 | tf_op jit(solution)/shard_map/ppermute | solution.py:581
  108.3 26.0 %collective-permute-start.46 = (bf16[80,6144]{1,0:T(8,128)(2,1)S(1)}, bf16[80,6144]{1,0:T(8,128)(2,1)S(1)}, u32[]{:S(2)}, u32[]{:S(2)}) collective-permute-start(bf16[80,6144]{1,0:T(8,128)(2,1)S(1)} %copy-done.2), channel_id=1, source_target_pairs={{0,4},{1,5},{2,6},{3,7},{4,0},{5,1},{6,2},{7,3},{8,12},{9,13},{10,... | collective-permute-start | bytes 2949128 | tf_op jit(solution)/shard_map/ppermute | solution.py:581
  114.4 17.3 %collective-permute-start.34 = (bf16[80,640]{1,0:T(8,128)(2,1)S(1)}, bf16[80,640]{1,0:T(8,128)(2,1)S(1)}, u32[]{:S(2)}, u32[]{:S(2)}) collective-permute-start(bf16[80,640]{1,0:T(8,128)(2,1)S(1)} %pad_maximum_fusion), channel_id=1, source_target_pairs={{0,7},{1,2},{2,1},{3,4},{4,3},{5,6},{6,5},{7,0},{8,15},{9,10},{10,... | collective-permute-start | bytes 307208 | tf_op jit(solution)/shard_map/ppermute | solution.py:581
  115.1 18.1 %collective-permute-start.37 = (f32[8,640]{1,0:T(8,128)S(1)}, f32[8,640]{1,0:T(8,128)S(1)}, u32[]{:S(2)}, u32[]{:S(2)}) collective-permute-start(f32[8,640]{1,0:T(8,128)S(1)} %maximum_maximum_fusion), channel_id=1, source_target_pairs={{0,4},{1,5},{2,6},{3,7},{4,0},{5,1},{6,2},{7,3},{8,12},{9,13},{10,... | collective-permute-start | bytes 61448 | tf_op jit(solution)/shard_map/ppermute | solution.py:581
  116.1 17.2 %collective-permute-start.36 = (f32[8,640]{1,0:T(8,128)S(1)}, f32[8,640]{1,0:T(8,128)S(1)}, u32[]{:S(2)}, u32[]{:S(2)}) collective-permute-start(f32[8,640]{1,0:T(8,128)S(1)} %maximum_maximum_fusion), channel_id=1, source_target_pairs={{0,2},{1,7},{2,4},{3,1},{4,6},{5,3},{6,0},{7,5},{8,10},{9,15},{10,... | collective-permute-start | bytes 61448 | tf_op jit(solution)/shard_map/ppermute | solution.py:581
  135.2 19.5 %collective-permute-start.50 = (bf16[80,3072]{1,0:T(8,128)(2,1)}, bf16[80,3072]{1,0:T(8,128)(2,1)S(1)}, u32[]{:S(2)}, u32[]{:S(2)}) collective-permute-start(bf16[80,3072]{1,0:T(8,128)(2,1)} %slice.385), channel_id=1, source_target_pairs={{0,4},{1,5},{2,6},{3,7},{4,0},{5,1},{6,2},{7,3},{8,12},{9,13},{10,... | collective-permute-start | bytes 1474568 | tf_op jit(solution)/shard_map/ppermute | solution.py:581
  146.5 8.1 %collective-permute-start.39 = (bf16[80,640]{1,0:T(8,128)(2,1)}, bf16[80,640]{1,0:T(8,128)(2,1)S(1)}, u32[]{:S(2)}, u32[]{:S(2)}) collective-permute-start(bf16[80,640]{1,0:T(8,128)(2,1)} %get-tuple-element.116), channel_id=1, source_target_pairs={{0,7},{1,2},{2,1},{3,4},{4,3},{5,6},{6,5},{7,0},{8,15},{9,10},{10,... | collective-permute-start | bytes 307208 | tf_op jit(solution)/shard_map/ppermute | solution.py:581
  147.4 6.6 %collective-permute-start.40 = (bf16[64,640]{1,0:T(8,128)(2,1)}, bf16[64,640]{1,0:T(8,128)(2,1)S(1)}, u32[]{:S(2)}, u32[]{:S(2)}) collective-permute-start(bf16[64,640]{1,0:T(8,128)(2,1)} %get-tuple-element.117), channel_id=1, source_target_pairs={{0,1},{1,0},{2,3},{3,2},{4,5},{5,4},{6,7},{7,6},{8,9},{9,8},{10,11... | collective-permute-start | bytes 245768 | tf_op jit(solution)/shard_map/ppermute | solution.py:581
  147.4 4.2 %collective-permute-start.42 = (f32[8,640]{1,0:T(8,128)}, f32[8,640]{1,0:T(8,128)S(1)}, u32[]{:S(2)}, u32[]{:S(2)}) collective-permute-start(f32[8,640]{1,0:T(8,128)} %get-tuple-element.118), channel_id=1, source_target_pairs={{0,4},{1,5},{2,6},{3,7},{4,0},{5,1},{6,2},{7,3},{8,12},{9,13},{10,... | collective-permute-start | bytes 61448 | tf_op jit(solution)/shard_map/ppermute | solution.py:581
  148.3 5.7 %collective-permute-start.41 = (f32[8,640]{1,0:T(8,128)}, f32[8,640]{1,0:T(8,128)S(1)}, u32[]{:S(2)}, u32[]{:S(2)}) collective-permute-start(f32[8,640]{1,0:T(8,128)} %get-tuple-element.118), channel_id=1, source_target_pairs={{0,2},{1,7},{2,4},{3,1},{4,6},{5,3},{6,0},{7,5},{8,10},{9,15},{10,... | collective-permute-start | bytes 61448 | tf_op jit(solution)/shard_map/ppermute | solution.py:581
  151.6 18.4 %collective-permute-start.44 = (bf16[768,384]{1,0:T(8,128)(2,1)}, bf16[768,384]{1,0:T(8,128)(2,1)S(1)}, u32[]{:S(2)}, u32[]{:S(2)}) collective-permute-start(bf16[768,384]{1,0:T(8,128)(2,1)} %shard_map.32.skip_ref), channel_id=1, source_target_pairs={{0,24},{1,25},{2,26},{3,27},{4,28},{5,29},{6,30},{7,31},{8,0},{9,1... | collective-permute-start | bytes 1769480 | tf_op jit(solution)/shard_map/ppermute | solution.py:577
  154.0 16.3 %collective-permute-start.47 = (bf16[80,6144]{1,0:T(8,128)(2,1)S(1)}, bf16[80,6144]{1,0:T(8,128)(2,1)S(1)}, u32[]{:S(2)}, u32[]{:S(2)}) collective-permute-start(bf16[80,6144]{1,0:T(8,128)(2,1)S(1)} %copy-done.2), channel_id=1, source_target_pairs={{0,1},{1,0},{2,3},{3,2},{4,5},{5,4},{6,7},{7,6},{8,9},{9,8},{10,11... | collective-permute-start | bytes 2949128 | tf_op jit(solution)/shard_map/ppermute | solution.py:581
  154.0 16.3 %collective-permute-start.48 = (bf16[80,6144]{1,0:T(8,128)(2,1)S(1)}, bf16[80,6144]{1,0:T(8,128)(2,1)S(1)}, u32[]{:S(2)}, u32[]{:S(2)}) collective-permute-start(bf16[80,6144]{1,0:T(8,128)(2,1)S(1)} %collective-permute-done.45.rest_3_.rest_2_), channel_id=1, source_target_pairs={{0,1},{1,0},{2,3},{3,2},{4,5},{5,4},{6,7},{7,6},{8,9},{9,8},{10,11... | collective-permute-start | bytes 2949128 | tf_op jit(solution)/shard_map/ppermute | solution.py:581
  154.6 15.8 %collective-permute-start.49 = (bf16[80,6144]{1,0:T(8,128)(2,1)S(1)}, bf16[80,6144]{1,0:T(8,128)(2,1)S(1)}, u32[]{:S(2)}, u32[]{:S(2)}) collective-permute-start(bf16[80,6144]{1,0:T(8,128)(2,1)S(1)} %collective-permute-done.46.rest_5_.rest_4_), channel_id=1, source_target_pairs={{0,1},{1,0},{2,3},{3,2},{4,5},{5,4},{6,7},{7,6},{8,9},{9,8},{10,11... | collective-permute-start | bytes 2949128 | tf_op jit(solution)/shard_map/ppermute | solution.py:581
  154.7 13.8 %collective-permute-start.51 = (bf16[80,3072]{1,0:T(8,128)(2,1)}, bf16[80,3072]{1,0:T(8,128)(2,1)S(1)}, u32[]{:S(2)}, u32[]{:S(2)}) collective-permute-start(bf16[80,3072]{1,0:T(8,128)(2,1)} %slice.386), channel_id=1, source_target_pairs={{0,2},{1,3},{2,0},{3,1},{4,6},{5,7},{6,4},{7,5},{8,10},{9,11},{10,... | collective-permute-start | bytes 1474568 | tf_op jit(solution)/shard_map/ppermute | solution.py:581
  180.5 8.8 %collective-permute-start.54 = (bf16[144,640]{1,0:T(8,128)(2,1)}, bf16[144,640]{1,0:T(8,128)(2,1)S(1)}, u32[]{:S(2)}, u32[]{:S(2)}) collective-permute-start(bf16[144,640]{1,0:T(8,128)(2,1)} %get-tuple-element.132), channel_id=1, source_target_pairs={{0,8},{1,9},{2,10},{3,11},{4,12},{5,13},{6,14},{7,15},{8,16},{9,17... | collective-permute-start | bytes 552968 | tf_op jit(solution)/shard_map/ppermute | solution.py:577
  189.4 6.1 %collective-permute-start.55 = (bf16[80,640]{1,0:T(8,128)(2,1)S(1)}, bf16[80,640]{1,0:T(8,128)(2,1)S(1)}, u32[]{:S(2)}, u32[]{:S(2)}) collective-permute-start(bf16[80,640]{1,0:T(8,128)(2,1)S(1)} %pad_maximum_fusion.1), channel_id=1, source_target_pairs={{0,7},{1,2},{2,1},{3,4},{4,3},{5,6},{6,5},{7,0},{8,15},{9,10},{10,... | collective-permute-start | bytes 307208 | tf_op jit(solution)/shard_map/ppermute | solution.py:581
  190.8 4.7 %collective-permute-start.58 = (f32[8,640]{1,0:T(8,128)S(1)}, f32[8,640]{1,0:T(8,128)S(1)}, u32[]{:S(2)}, u32[]{:S(2)}) collective-permute-start(f32[8,640]{1,0:T(8,128)S(1)} %maximum_maximum_fusion.1), channel_id=1, source_target_pairs={{0,4},{1,5},{2,6},{3,7},{4,0},{5,1},{6,2},{7,3},{8,12},{9,13},{10,... | collective-permute-start | bytes 61448 | tf_op jit(solution)/shard_map/ppermute | solution.py:581
  191.6 4.7 %collective-permute-start.57 = (f32[8,640]{1,0:T(8,128)S(1)}, f32[8,640]{1,0:T(8,128)S(1)}, u32[]{:S(2)}, u32[]{:S(2)}) collective-permute-start(f32[8,640]{1,0:T(8,128)S(1)} %maximum_maximum_fusion.1), channel_id=1, source_target_pairs={{0,2},{1,7},{2,4},{3,1},{4,6},{5,3},{6,0},{7,5},{8,10},{9,15},{10,... | collective-permute-start | bytes 61448 | tf_op jit(solution)/shard_map/ppermute | solution.py:581
  192.5 3.9 %collective-permute-start.56 = (bf16[64,640]{1,0:T(8,128)(2,1)S(1)}, bf16[64,640]{1,0:T(8,128)(2,1)S(1)}, u32[]{:S(2)}, u32[]{:S(2)}) collective-permute-start(bf16[64,640]{1,0:T(8,128)(2,1)S(1)} %get-tuple-element.155), channel_id=1, source_target_pairs={{0,1},{1,0},{2,3},{3,2},{4,5},{5,4},{6,7},{7,6},{8,9},{9,8},{10,11... | collective-permute-start | bytes 245768 | tf_op jit(solution)/shard_map/ppermute | solution.py:581
  205.4 6.2 %collective-permute-start.60 = (bf16[80,640]{1,0:T(8,128)(2,1)}, bf16[80,640]{1,0:T(8,128)(2,1)S(1)}, u32[]{:S(2)}, u32[]{:S(2)}) collective-permute-start(bf16[80,640]{1,0:T(8,128)(2,1)} %get-tuple-element.134), channel_id=1, source_target_pairs={{0,7},{1,2},{2,1},{3,4},{4,3},{5,6},{6,5},{7,0},{8,15},{9,10},{10,... | collective-permute-start | bytes 307208 | tf_op jit(solution)/shard_map/ppermute | solution.py:581
  206.1 5.6 %collective-permute-start.63 = (f32[8,640]{1,0:T(8,128)}, f32[8,640]{1,0:T(8,128)S(1)}, u32[]{:S(2)}, u32[]{:S(2)}) collective-permute-start(f32[8,640]{1,0:T(8,128)} %get-tuple-element.136), channel_id=1, source_target_pairs={{0,4},{1,5},{2,6},{3,7},{4,0},{5,1},{6,2},{7,3},{8,12},{9,13},{10,... | collective-permute-start | bytes 61448 | tf_op jit(solution)/shard_map/ppermute | solution.py:581
  207.2 5.0 %collective-permute-start.62 = (f32[8,640]{1,0:T(8,128)}, f32[8,640]{1,0:T(8,128)S(1)}, u32[]{:S(2)}, u32[]{:S(2)}) collective-permute-start(f32[8,640]{1,0:T(8,128)} %get-tuple-element.136), channel_id=1, source_target_pairs={{0,2},{1,7},{2,4},{3,1},{4,6},{5,3},{6,0},{7,5},{8,10},{9,15},{10,... | collective-permute-start | bytes 61448 | tf_op jit(solution)/shard_map/ppermute | solution.py:581
  208.5 4.5 %collective-permute-start.61 = (bf16[64,640]{1,0:T(8,128)(2,1)}, bf16[64,640]{1,0:T(8,128)(2,1)S(1)}, u32[]{:S(2)}, u32[]{:S(2)}) collective-permute-start(bf16[64,640]{1,0:T(8,128)(2,1)} %get-tuple-element.135), channel_id=1, source_target_pairs={{0,1},{1,0},{2,3},{3,2},{4,5},{5,4},{6,7},{7,6},{8,9},{9,8},{10,11... | collective-permute-start | bytes 245768 | tf_op jit(solution)/shard_map/ppermute | solution.py:581
  222.2 9.0 %collective-permute-start.65 = (bf16[144,640]{1,0:T(8,128)(2,1)}, bf16[144,640]{1,0:T(8,128)(2,1)S(1)}, u32[]{:S(2)}, u32[]{:S(2)}) collective-permute-start(bf16[144,640]{1,0:T(8,128)(2,1)} %get-tuple-element.137), channel_id=1, source_target_pairs={{0,8},{1,9},{2,10},{3,11},{4,12},{5,13},{6,14},{7,15},{8,16},{9,17... | collective-permute-start | bytes 552968 | tf_op jit(solution)/shard_map/ppermute | solution.py:577
  231.2 5.1 %collective-permute-start.66 = (bf16[80,640]{1,0:T(8,128)(2,1)S(1)}, bf16[80,640]{1,0:T(8,128)(2,1)S(1)}, u32[]{:S(2)}, u32[]{:S(2)}) collective-permute-start(bf16[80,640]{1,0:T(8,128)(2,1)S(1)} %pad_maximum_fusion.2), channel_id=1, source_target_pairs={{0,7},{1,2},{2,1},{3,4},{4,3},{5,6},{6,5},{7,0},{8,15},{9,10},{10,... | collective-permute-start | bytes 307208 | tf_op jit(solution)/shard_map/ppermute | solution.py:581
  246.1 5.4 %collective-permute-start.68 = (bf16[144,320]{1,0:T(8,128)(2,1)}, bf16[144,320]{1,0:T(8,128)(2,1)S(1)}, u32[]{:S(2)}, u32[]{:S(2)}) collective-permute-start(bf16[144,320]{1,0:T(8,128)(2,1)} %get-tuple-element.140), channel_id=1, source_target_pairs={{0,7},{1,2},{2,1},{3,4},{4,3},{5,6},{6,5},{7,0},{8,15},{9,10},{10,... | collective-permute-start | bytes 276488 | tf_op jit(solution)/shard_map/ppermute | solution.py:581
  247.2 4.4 %collective-permute-start.71 = (f32[8,320]{1,0:T(8,128)}, f32[8,320]{1,0:T(8,128)S(1)}, u32[]{:S(2)}, u32[]{:S(2)}) collective-permute-start(f32[8,320]{1,0:T(8,128)} %get-tuple-element.142), channel_id=1, source_target_pairs={{0,4},{1,5},{2,6},{3,7},{4,0},{5,1},{6,2},{7,3},{8,12},{9,13},{10,... | collective-permute-start | bytes 30728 | tf_op jit(solution)/shard_map/ppermute | solution.py:581
  248.0 4.8 %collective-permute-start.70 = (f32[8,320]{1,0:T(8,128)}, f32[8,320]{1,0:T(8,128)S(1)}, u32[]{:S(2)}, u32[]{:S(2)}) collective-permute-start(f32[8,320]{1,0:T(8,128)} %get-tuple-element.142), channel_id=1, source_target_pairs={{0,2},{1,7},{2,4},{3,1},{4,6},{5,3},{6,0},{7,5},{8,10},{9,15},{10,... | collective-permute-start | bytes 30728 | tf_op jit(solution)/shard_map/ppermute | solution.py:581
  248.0 5.5 %collective-permute-start.69 = (bf16[128,320]{1,0:T(8,128)(2,1)}, bf16[128,320]{1,0:T(8,128)(2,1)S(1)}, u32[]{:S(2)}, u32[]{:S(2)}) collective-permute-start(bf16[128,320]{1,0:T(8,128)(2,1)} %get-tuple-element.141), channel_id=1, source_target_pairs={{0,1},{1,0},{2,3},{3,2},{4,5},{5,4},{6,7},{7,6},{8,9},{9,8},{10,11... | collective-permute-start | bytes 245768 | tf_op jit(solution)/shard_map/ppermute | solution.py:581
  265.0 6.4 %collective-permute-start.73 = (bf16[144,320]{1,0:T(8,128)(2,1)}, bf16[144,320]{1,0:T(8,128)(2,1)S(1)}, u32[]{:S(2)}, u32[]{:S(2)}) collective-permute-start(bf16[144,320]{1,0:T(8,128)(2,1)} %get-tuple-element.144), channel_id=1, source_target_pairs={{0,7},{1,2},{2,1},{3,4},{4,3},{5,6},{6,5},{7,0},{8,15},{9,10},{10,... | collective-permute-start | bytes 276488 | tf_op jit(solution)/shard_map/ppermute | solution.py:581
  265.6 5.8 %collective-permute-start.76 = (f32[8,320]{1,0:T(8,128)}, f32[8,320]{1,0:T(8,128)S(1)}, u32[]{:S(2)}, u32[]{:S(2)}) collective-permute-start(f32[8,320]{1,0:T(8,128)} %get-tuple-element.146), channel_id=1, source_target_pairs={{0,4},{1,5},{2,6},{3,7},{4,0},{5,1},{6,2},{7,3},{8,12},{9,13},{10,... | collective-permute-start | bytes 30728 | tf_op jit(solution)/shard_map/ppermute | solution.py:581
  266.5 5.3 %collective-permute-start.75 = (f32[8,320]{1,0:T(8,128)}, f32[8,320]{1,0:T(8,128)S(1)}, u32[]{:S(2)}, u32[]{:S(2)}) collective-permute-start(f32[8,320]{1,0:T(8,128)} %get-tuple-element.146), channel_id=1, source_target_pairs={{0,2},{1,7},{2,4},{3,1},{4,6},{5,3},{6,0},{7,5},{8,10},{9,15},{10,... | collective-permute-start | bytes 30728 | tf_op jit(solution)/shard_map/ppermute | solution.py:581
  268.1 4.5 %collective-permute-start.74 = (bf16[128,320]{1,0:T(8,128)(2,1)}, bf16[128,320]{1,0:T(8,128)(2,1)S(1)}, u32[]{:S(2)}, u32[]{:S(2)}) collective-permute-start(bf16[128,320]{1,0:T(8,128)(2,1)} %get-tuple-element.145), channel_id=1, source_target_pairs={{0,1},{1,0},{2,3},{3,2},{4,5},{5,4},{6,7},{7,6},{8,9},{9,8},{10,11... | collective-permute-start | bytes 245768 | tf_op jit(solution)/shard_map/ppermute | solution.py:581
  283.7 8.8 %collective-permute-start.80 = (bf16[8,16,320]{2,1,0:T(8,128)(2,1)}, bf16[8,16,320]{2,1,0:T(8,128)(2,1)S(1)}, u32[]{:S(2)}, u32[]{:S(2)}) collective-permute-start(bf16[8,16,320]{2,1,0:T(8,128)(2,1)} %get-tuple-element.149), channel_id=1, source_target_pairs={{24,0},{25,1},{26,2},{27,3},{28,4},{29,5},{30,6},{31,7}} | collective-permute-start | bytes 245768 | tf_op jit(solution)/shard_map/ppermute | solution.py:722
  (88 other events, 502.6 us)

commit v4 on v3

--- a/solution.py
+++ b/solution.py
@@ -221,7 +221,7 @@
     ] + list(extra)
 
 
-def call(body, n_smem, n_vmem, n_any, outs, scratch, flops, limit=60 * 1024 * 1024):
+def call(body, n_smem, n_vmem, n_any, outs, scratch, flops, limit=53 * 1024 * 1024):
     specs = (
         [pl.BlockSpec(memory_space=pltpu.SMEM)] * n_smem
         + [pl.BlockSpec(memory_space=pltpu.VMEM)] * n_vmem
@@ -674,8 +674,8 @@
 
     narrow, wide = shape.narrow, shape.wide
     x = features[0].reshape(shape.rows, shape.half, 2, narrow).transpose(0, 2, 1, 3).reshape(-1, narrow)
-    ready = prepare(shape, flags, x, 1)
-    sent = send(0, ready[3])
+    sent = send(0)
+    ready = prepare(shape, flags, after(x, sent[0]), 1)
     if n == 8:
         packed += pack_blocks(shape, after(pack.T, sent[0]), bounds[1:])
     third = send(1)
@@ -700,13 +700,14 @@
             opposite = relay(sent, got[3])
             skip, got = lax.optimization_barrier((skip, got))
             skip = permute(skip, 0, n_section - 1, lambda i: i)
+        else:
+            skip, got = lax.optimization_barrier((skip, got))
         hidden = coarse_conv(shape, flags, *weights(0, wide, wide), got, 1)
         if section == 1:
             share(3, after(sent, hidden[3]))
         then = exchange(hidden, section, section)
         if section == 1:
             share(3, after(opposite, then[3]), 3)
-            then, skip = lax.optimization_barrier((then, skip))
         coarse = coarse_conv(shape, flags, *weights(36 * q_rows, wide, wide), then, 1, residual=got[0])
     got = exchange(coarse, 2, 3, with_stats=False)
     up = up_conv(shape, flags, *weights(0, wide, narrow), got, skip, 1)

time: 294 us -> 288 us (0.980)
  waiting for transfers between devices: 128 us -> 145 us
  local copies, waits for them, and re-layouts: 17.9 us -> 7.15 us
  Pallas kernels: 83 us -> 72.7 us
  other arithmetic: 4.57 us -> 1 us
    ppermute x74, waiting for transfers between devices: 99.2 us -> 108 us  [within(): return lax.ppermute(value, ('section', 'space'), pairs)]
    ppermute x3, waiting for transfers between devices: 7.44 us -> 14.5 us  [shards(): lax.ppermute(outs[target], ('section', 'space'), pairs)]
    unnamed x143 -> x85, local copies, waits for them, and re-layouts: 12.3 us -> 6 us
    add x8, other arithmetic: 4.11 us -> 0.54 us  [exchange(): mine = own + sums_of(outer[-TAIL:], count) + b + c]
    slice x4, local copies, waits for them, and re-layouts: 3.23 us -> 0.1 us  [relay(): first, second = after((got[1][:, :half], got[2][:, half:]), *deps)]
  transfers between devices with their start and end apart: 81 -> 81, of which waited for: 39 -> 38; matrix products, arithmetic and copies ran while one was open for 2% -> 0% of each run, Pallas kernels for 7% -> 6%
where the time goes in v4:
time: 288 us; the launch traced here: 287 us
  waiting for transfers between devices  145 us (50%)
  Pallas kernels  72.7 us (25%)
  starting transfers between devices  60.6 us (21%)
  local copies, waits for them, and re-layouts  7.15 us (2%)
    ppermute x74, waiting for transfers between devices, within(): return lax.ppermute(value, ('section', 'space'), pairs)  108 us
    ppermute x74, starting transfers between devices, within(): return lax.ppermute(value, ('section', 'space'), pairs)  50.6 us
    pallas_call x4, Pallas kernels, coarse_conv(): call(body, 1, 5 + extra, len(pieces), outs, scratch_of(weights, rows + 2,...  26.4 us
    ppermute x4, waiting for transfers between devices, permute(): return lax.ppermute(value, ('section', 'space'), pairs)  22.2 us
    ppermute x3, waiting for transfers between devices, shards(): lax.ppermute(outs[target], ('section', 'space'), pairs)  14.5 us
    pallas_call x2, Pallas kernels, fine_conv(): call(body, 1, 5 + extra, n_pieces, outs, scratch_of(weights, image_rows,...  12.6 us
    pallas_call x1, Pallas kernels, join_conv(): call(body, 1, 6, len(pieces), outs, scratch, flops)  8.48 us
    pallas_call x1, Pallas kernels, up_conv(): call(body, 1, 4, len(pieces), outs, scratch, flops)  7.73 us
  transfers between devices with their start and end apart: 81, of which 38 were waited for; matrix products, arithmetic and copies ran while one was open for 0% of the time, Pallas kernels for 6%

profile of v4, /device:TPU:0, one launch (start us, length us, event | category | flops | bytes accessed | tf_op | source)
XLA Modules:
  0.0 287.1 jit_solution(15574219431431202333)
XLA Ops:
  0.0 1.2 copy.5
  2.5 1.5 shard_map.29
  4.0 3.4 %collective-permute-start = (bf16[144,320]{1,0:T(8,128)(2,1)S(1)}, bf16[144,320]{1,0:T(8,128)(2,1)S(1)}, u32[]{:S(2)}, u32[]{:S(2)}) collective-permute-start(bf16[144,320]{1,0:T(8,128)(2,1)S(1)} %get-tuple-element.84), channel_id=1, source_target_pairs={{0,7},{1,2},{2,1},{3,4},{4,3},{5,6},{6,5},{7,0},{8,15},{9,10},{10,... | collective-permute-start | bytes 276488 | tf_op jit(solution)/shard_map/ppermute | solution.py:581
  8.5 2.4 collective-permute-start.5
  11.4 1.8 collective-permute-start.7
  13.4 4.5 %collective-permute-done.5.rest_2_ = bf16[80,1536]{1,0:T(8,128)(2,1)S(1)} collective-permute-done((bf16[80,1536]{1,0:T(8,128)(2,1)S(1)}, bf16[80,1536]{1,0:T(8,128)(2,1)S(1)}, u32[]{:S(2)}, u32[]{:S(2)}) %collective-permute-start.5) | collective-permute-done | bytes 245792 | tf_op jit(solution)/shard_map/ppermute | solution.py:581
  17.9 5.1 %collective-permute-done.6.rest_4_ = bf16[80,1536]{1,0:T(8,128)(2,1)S(1)} collective-permute-done((bf16[80,1536]{1,0:T(8,128)(2,1)S(1)}, bf16[80,1536]{1,0:T(8,128)(2,1)S(1)}, u32[]{:S(2)}, u32[]{:S(2)}) %collective-permute-start.6) | collective-permute-done | bytes 245792 | tf_op jit(solution)/shard_map/ppermute | solution.py:581
  24.2 1.6 collective-permute-done.1.inner.rest_2_
  26.0 2.9 %shard_map.30 = (bf16[80,1536]{1,0:T(8,128)(2,1)S(1)}, bf16[80,3072]{1,0:T(8,128)(2,1)S(1)}, bf16[80,6144]{1,0:T(8,128)(2,1)}) custom-call(bf16[80,11520]{1,0:T(8,128)(2,1)} %bitcast.17), custom_call_target="tpu_custom_call" | custom-call | flops 1000 | bytes 4000000 | tf_op jit(solution)/shard_map/pallas_call | solution.py:556
  30.5 5.6 %shard_map.31 = (bf16[528,320]{1,0:T(8,128)(2,1)}, bf16[272,320]{1,0:T(8,128)(2,1)S(1)}, bf16[256,320]{1,0:T(8,128)(2,1)S(1)}, f32[8,320]{1,0:T(8,128)S(1)}) custom-call(s32[5]{0:T(128)S(1)} %stack.31.flags, bf16[528,320]{1,0:T(8,128)(2,1)} %get-tuple-element.83.block.rest_0_, bf16[144,320]{1,0:T(8,128)(2,1)S(1)} %collective-permute-done.outer.rest_1_, ...), custom_call_target="tpu_custom_call" | custom-call | flops 943718400 | bytes 4000000 | tf_op jit(solution)/shard_map/pallas_call | solution.py:308
  38.3 1.1 collective-permute-start.18
  39.4 1.7 collective-permute-start.24
  41.3 3.2 %collective-permute-done.12.outer = bf16[272,320]{1,0:T(8,128)(2,1)S(1)} collective-permute-done((bf16[272,320]{1,0:T(8,128)(2,1)S(1)}, bf16[272,320]{1,0:T(8,128)(2,1)S(1)}, u32[]{:S(2)}, u32[]{:S(2)}) %collective-permute-start.12) | collective-permute-done | bytes 174112 | tf_op jit(solution)/shard_map/ppermute | solution.py:581
  44.9 3.5 %collective-permute-done.14 = f32[8,320]{1,0:T(8,128)S(1)} collective-permute-done((f32[8,320]{1,0:T(8,128)S(1)}, f32[8,320]{1,0:T(8,128)S(1)}, u32[]{:S(2)}, u32[]{:S(2)}) %collective-permute-start.14) | collective-permute-done | bytes 10272 | tf_op jit(solution)/shard_map/ppermute | solution.py:581
  48.4 1.2 collective-permute-start.19
  49.6 11.3 %collective-permute-done.13 = f32[8,320]{1,0:T(8,128)S(1)} collective-permute-done((f32[8,320]{1,0:T(8,128)S(1)}, f32[8,320]{1,0:T(8,128)S(1)}, u32[]{:S(2)}, u32[]{:S(2)}) %collective-permute-start.13) | collective-permute-done | bytes 10272 | tf_op jit(solution)/shard_map/ppermute | solution.py:581
  61.9 4.2 %collective-permute-done.19.rest_9_.rest_14_ = bf16[80,1536]{1,0:T(8,128)(2,1)S(1)} collective-permute-done((bf16[80,1536]{1,0:T(8,128)(2,1)S(1)}, bf16[80,1536]{1,0:T(8,128)(2,1)S(1)}, u32[]{:S(2)}, u32[]{:S(2)}) %collective-permute-start.19) | collective-permute-done | bytes 245792 | tf_op jit(solution)/shard_map/ppermute | solution.py:581
  67.1 9.4 %collective-permute-done.25.rest_4_.rest_20_ = bf16[80,3072]{1,0:T(8,128)(2,1)S(1)} collective-permute-done((bf16[80,3072]{1,0:T(8,128)(2,1)S(1)}, bf16[80,3072]{1,0:T(8,128)(2,1)S(1)}, u32[]{:S(2)}, u32[]{:S(2)}) %collective-permute-start.25) | collective-permute-done | bytes 491552 | tf_op jit(solution)/shard_map/ppermute | solution.py:581
  76.5 1.4 collective-permute-done.15.inner
  79.1 1.1 collective-permute-start.29
  82.3 7.0 %shard_map.32.skip_ref = bf16[768,384]{1,0:T(8,128)(2,1)} custom-call(s32[5]{0:T(128)S(1)} %stack.31.flags, bf16[528,320]{1,0:T(8,128)(2,1)} %get-tuple-element.96.block, bf16[272,320]{1,0:T(8,128)(2,1)S(1)} %collective-permute-done.12.outer, bf16[256,320]{1,0:T(8,128)(2,1)S(1)} %collective-permute-done.15.inner, f32[8,320]{1,0:T(8,128)S(1)} %fusion.11.sa, ...), custom_call_target="tpu_custom_call" | custom-call | flops 1415577600 | bytes 4000000 | tf_op jit(solution)/shard_map/pallas_call | solution.py:308
  93.1 4.9 %shard_map.33 = (bf16[144,640]{1,0:T(8,128)(2,1)S(1)}, bf16[80,640]{1,0:T(8,128)(2,1)}, bf16[64,640]{1,0:T(8,128)(2,1)}, f32[8,640]{1,0:T(8,128)}) custom-call(s32[5]{0:T(128)S(1)} %stack.31.flags, bf16[768,384]{1,0:T(8,128)(2,1)} %shard_map.32.skip_ref, bf16[80,3072]{1,0:T(8,128)(2,1)} %copy-done, bf16[80,3072]{1,0:T(8,128)(2,1)} %copy-done.18, ...), custom_call_target="tpu_custom_call" | custom-call | flops 471859200 | bytes 4000000 | tf_op jit(solution)/shard_map/pallas_call | solution.py:345
  98.0 1.6 collective-permute-start.33
  99.6 1.2 collective-permute-start.45
  101.8 4.8 %collective-permute-done.33.block.rest_0_ = bf16[144,640]{1,0:T(8,128)(2,1)S(1)} collective-permute-done((bf16[144,640]{1,0:T(8,128)(2,1)S(1)}, bf16[144,640]{1,0:T(8,128)(2,1)S(1)}, u32[]{:S(2)}, u32[]{:S(2)}) %collective-permute-start.33) | collective-permute-done | bytes 184352 | tf_op jit(solution)/shard_map/ppermute | solution.py:577
  107.4 1.1 collective-permute-start.37
  109.0 15.5 %collective-permute-done.34.outer = bf16[80,640]{1,0:T(8,128)(2,1)S(1)} collective-permute-done((bf16[80,640]{1,0:T(8,128)(2,1)S(1)}, bf16[80,640]{1,0:T(8,128)(2,1)S(1)}, u32[]{:S(2)}, u32[]{:S(2)}) %collective-permute-start.34) | collective-permute-done | bytes 102432 | tf_op jit(solution)/shard_map/ppermute | solution.py:581
  124.6 1.4 collective-permute-start.35
  127.4 6.0 %shard_map.34 = (bf16[144,640]{1,0:T(8,128)(2,1)S(1)}, bf16[80,640]{1,0:T(8,128)(2,1)S(1)}, bf16[64,640]{1,0:T(8,128)(2,1)S(1)}, f32[8,640]{1,0:T(8,128)S(1)}) custom-call(s32[5]{0:T(128)S(1)} %stack.31.flags, bf16[144,640]{1,0:T(8,128)(2,1)S(1)} %collective-permute-done.33.block.rest_0_, bf16[80,640]{1,0:T(8,128)(2,1)S(1)} %collective-permute-done.34.outer, ...), custom_call_target="tpu_custom_call" | custom-call | flops 943718400 | bytes 4000000 | tf_op jit(solution)/shard_map/pallas_call | solution.py:381
  133.4 1.5 collective-permute-start.40
  136.1 1.1 collective-permute-start.43
  137.9 11.8 %collective-permute-done.43 = f32[8,640]{1,0:T(8,128)S(1)} collective-permute-done((f32[8,640]{1,0:T(8,128)S(1)}, f32[8,640]{1,0:T(8,128)S(1)}, u32[]{:S(2)}, u32[]{:S(2)}) %collective-permute-start.43) | collective-permute-done | bytes 20512 | tf_op jit(solution)/shard_map/ppermute | solution.py:581
  150.2 1.5 collective-permute-start.51
  151.9 11.5 %collective-permute-done.51.rest_9_ = bf16[80,3072]{1,0:T(8,128)(2,1)S(1)} collective-permute-done((bf16[80,3072]{1,0:T(8,128)(2,1)S(1)}, bf16[80,3072]{1,0:T(8,128)(2,1)S(1)}, u32[]{:S(2)}, u32[]{:S(2)}) %collective-permute-start.51) | collective-permute-done | bytes 491552 | tf_op jit(solution)/shard_map/ppermute | solution.py:581
  167.3 7.2 %shard_map.35 = (bf16[144,640]{1,0:T(8,128)(2,1)S(1)}, bf16[80,640]{1,0:T(8,128)(2,1)}, bf16[64,640]{1,0:T(8,128)(2,1)}, f32[8,640]{1,0:T(8,128)}) custom-call(s32[5]{0:T(128)S(1)} %stack.31.flags, bf16[144,640]{1,0:T(8,128)(2,1)S(1)} %get-tuple-element.116.block, bf16[80,640]{1,0:T(8,128)(2,1)S(1)} %collective-permute-done.40.outer, ...), custom_call_target="tpu_custom_call" | custom-call | flops 943718400 | bytes 4000000 | tf_op jit(solution)/shard_map/pallas_call | solution.py:381
  174.4 1.6 collective-permute-start.54
  176.1 2.3 collective-permute-start.39
  178.3 5.5 %collective-permute-done.54.block.rest_0_ = bf16[144,640]{1,0:T(8,128)(2,1)S(1)} collective-permute-done((bf16[144,640]{1,0:T(8,128)(2,1)S(1)}, bf16[144,640]{1,0:T(8,128)(2,1)S(1)}, u32[]{:S(2)}, u32[]{:S(2)}) %collective-permute-start.54) | collective-permute-done | bytes 184352 | tf_op jit(solution)/shard_map/ppermute | solution.py:577
  184.1 1.3 collective-permute-start.58
  185.4 1.2 collective-permute-start.57
  186.6 1.2 collective-permute-start.56
  187.8 1.8 collective-permute-done.55.outer
  190.2 5.0 %collective-permute-done.39.skip_ref = bf16[768,384]{1,0:T(8,128)(2,1)S(1)} collective-permute-done((bf16[768,384]{1,0:T(8,128)(2,1)S(1)}, bf16[768,384]{1,0:T(8,128)(2,1)S(1)}, u32[]{:S(2)}, u32[]{:S(2)}) %collective-permute-start.39) | collective-permute-done | bytes 589856 | tf_op jit(solution)/shard_map/ppermute | solution.py:577
  195.1 6.1 %shard_map.36 = (bf16[144,640]{1,0:T(8,128)(2,1)S(1)}, bf16[80,640]{1,0:T(8,128)(2,1)S(1)}, bf16[64,640]{1,0:T(8,128)(2,1)S(1)}, f32[8,640]{1,0:T(8,128)S(1)}) custom-call(s32[5]{0:T(128)S(1)} %stack.31.flags, bf16[144,640]{1,0:T(8,128)(2,1)S(1)} %collective-permute-done.54.block.rest_0_, bf16[80,640]{1,0:T(8,128)(2,1)S(1)} %collective-permute-done.55.outer, ...), custom_call_target="tpu_custom_call" | custom-call | flops 943718400 | bytes 4000000 | tf_op jit(solution)/shard_map/pallas_call | solution.py:381
  203.9 1.2 collective-permute-start.61
  205.1 1.9 collective-permute-done.60.outer
  207.0 1.1 collective-permute-done.62
  208.2 1.2 collective-permute-done.64.sb
  209.4 7.1 %shard_map.37 = (bf16[144,640]{1,0:T(8,128)(2,1)S(1)}, bf16[80,640]{1,0:T(8,128)(2,1)}, bf16[64,640]{1,0:T(8,128)(2,1)}, f32[8,640]{1,0:T(8,128)}) custom-call(s32[5]{0:T(128)S(1)} %stack.31.flags, bf16[144,640]{1,0:T(8,128)(2,1)S(1)} %get-tuple-element.133.block, bf16[80,640]{1,0:T(8,128)(2,1)S(1)} %collective-permute-done.60.outer, ...), custom_call_target="tpu_custom_call" | custom-call | flops 943718400 | bytes 4000000 | tf_op jit(solution)/shard_map/pallas_call | solution.py:381
  216.5 1.9 collective-permute-start.65
  218.4 6.9 %collective-permute-done.65.block = bf16[144,640]{1,0:T(8,128)(2,1)S(1)} collective-permute-done((bf16[144,640]{1,0:T(8,128)(2,1)S(1)}, bf16[144,640]{1,0:T(8,128)(2,1)S(1)}, u32[]{:S(2)}, u32[]{:S(2)}) %collective-permute-start.65) | collective-permute-done | bytes 184352 | tf_op jit(solution)/shard_map/ppermute | solution.py:577
  226.8 3.6 %collective-permute-done.66.outer = bf16[80,640]{1,0:T(8,128)(2,1)S(1)} collective-permute-done((bf16[80,640]{1,0:T(8,128)(2,1)S(1)}, bf16[80,640]{1,0:T(8,128)(2,1)S(1)}, u32[]{:S(2)}, u32[]{:S(2)}) %collective-permute-start.66) | collective-permute-done | bytes 102432 | tf_op jit(solution)/shard_map/ppermute | solution.py:581
  230.5 7.7 %shard_map.38 = (bf16[528,320]{1,0:T(8,128)(2,1)}, bf16[144,320]{1,0:T(8,128)(2,1)S(1)}, bf16[128,320]{1,0:T(8,128)(2,1)S(1)}, f32[8,320]{1,0:T(8,128)S(1)}) custom-call(s32[5]{0:T(128)S(1)} %stack.31.flags, bf16[144,640]{1,0:T(8,128)(2,1)S(1)} %collective-permute-done.65.block, bf16[80,640]{1,0:T(8,128)(2,1)S(1)} %collective-permute-done.66.outer, ...), custom_call_target="tpu_custom_call" | custom-call | flops 1887436800 | bytes 4000000 | tf_op jit(solution)/shard_map/pallas_call | solution.py:420
  240.2 1.7 collective-permute-start.69
  241.8 1.6 collective-permute-done.68.outer
  243.5 1.2 collective-permute-done.70
  244.8 1.2 collective-permute-done.72.sb
  245.9 8.5 %shard_map.39 = (bf16[528,320]{1,0:T(8,128)(2,1)}, bf16[144,320]{1,0:T(8,128)(2,1)S(1)}, bf16[128,320]{1,0:T(8,128)(2,1)S(1)}, f32[8,320]{1,0:T(8,128)S(1)}) custom-call(s32[5]{0:T(128)S(1)} %stack.31.flags, bf16[528,320]{1,0:T(8,128)(2,1)} %get-tuple-element.139.block.u_ref, bf16[144,320]{1,0:T(8,128)(2,1)S(1)} %collective-permute-done.68.outer, ...), custom_call_target="tpu_custom_call" | custom-call | flops 1887436800 | bytes 4000000 | tf_op jit(solution)/shard_map/pallas_call | solution.py:461
  255.9 1.4 collective-permute-start.75
  257.9 2.8 collective-permute-done.73.outer
  260.9 1.2 collective-permute-done.77.sb
  262.0 7.1 %shard_map.40 = (bf16[8,16,320]{2,1,0:T(8,128)(2,1)S(1)}, bf16[8,16,320]{2,1,0:T(8,128)(2,1)S(1)}, bf16[8,16,320]{2,1,0:T(8,128)(2,1)S(1)}, bf16[8,16,320]{2,1,0:T(8,128)(2,1)S(1)}) custom-call(s32[5]{0:T(128)S(1)} %stack.31.flags, bf16[528,320]{1,0:T(8,128)(2,1)} %get-tuple-element.143.block, bf16[144,320]{1,0:T(8,128)(2,1)S(1)} %collective-permute-done.73.outer, ...), custom_call_target="tpu_custom_call" | custom-call | flops 1153433600 | bytes 4000000 | tf_op jit(solution)/shard_map/pallas_call | solution.py:534
  270.5 1.3 collective-permute-start.80
  271.8 14.5 %collective-permute-done.80 = bf16[8,16,320]{2,1,0:T(8,128)(2,1)S(1)} collective-permute-done((bf16[8,16,320]{2,1,0:T(8,128)(2,1)S(1)}, bf16[8,16,320]{2,1,0:T(8,128)(2,1)S(1)}, u32[]{:S(2)}, u32[]{:S(2)}) %collective-permute-start.80) | collective-permute-done | bytes 81952 | tf_op jit(solution)/shard_map/ppermute | solution.py:723
  (246 shorter events, 39.0 us)
Async XLA Ops:
  4.0 7.4 %collective-permute-start = (bf16[144,320]{1,0:T(8,128)(2,1)S(1)}, bf16[144,320]{1,0:T(8,128)(2,1)S(1)}, u32[]{:S(2)}, u32[]{:S(2)}) collective-permute-start(bf16[144,320]{1,0:T(8,128)(2,1)S(1)} %get-tuple-element.84), channel_id=1, source_target_pairs={{0,7},{1,2},{2,1},{3,4},{4,3},{5,6},{6,5},{7,0},{8,15},{9,10},{10,... | collective-permute-start | bytes 276488 | tf_op jit(solution)/shard_map/ppermute | solution.py:581
  7.4 5.9 %collective-permute-start.3 = (f32[8,320]{1,0:T(8,128)S(1)}, f32[8,320]{1,0:T(8,128)S(1)}, u32[]{:S(2)}, u32[]{:S(2)}) collective-permute-start(f32[8,320]{1,0:T(8,128)S(1)} %get-tuple-element.86), channel_id=1, source_target_pairs={{0,4},{1,5},{2,6},{3,7},{4,0},{5,1},{6,2},{7,3},{8,12},{9,13},{10,... | collective-permute-start | bytes 30728 | tf_op jit(solution)/shard_map/ppermute | solution.py:581
  7.9 5.4 %collective-permute-start.2 = (f32[8,320]{1,0:T(8,128)S(1)}, f32[8,320]{1,0:T(8,128)S(1)}, u32[]{:S(2)}, u32[]{:S(2)}) collective-permute-start(f32[8,320]{1,0:T(8,128)S(1)} %get-tuple-element.86), channel_id=1, source_target_pairs={{0,2},{1,7},{2,4},{3,1},{4,6},{5,3},{6,0},{7,5},{8,10},{9,15},{10,... | collective-permute-start | bytes 30728 | tf_op jit(solution)/shard_map/ppermute | solution.py:581
  8.5 9.4 %collective-permute-start.5 = (bf16[80,1536]{1,0:T(8,128)(2,1)S(1)}, bf16[80,1536]{1,0:T(8,128)(2,1)S(1)}, u32[]{:S(2)}, u32[]{:S(2)}) collective-permute-start(bf16[80,1536]{1,0:T(8,128)(2,1)S(1)} %shard_map.28.rest_0_), channel_id=1, source_target_pairs={{0,2},{1,3},{2,0},{3,1},{4,6},{5,7},{6,4},{7,5},{8,10},{9,11},{10,... | collective-permute-start | bytes 737288 | tf_op jit(solution)/shard_map/ppermute | solution.py:581
  10.9 12.2 %collective-permute-start.6 = (bf16[80,1536]{1,0:T(8,128)(2,1)S(1)}, bf16[80,1536]{1,0:T(8,128)(2,1)S(1)}, u32[]{:S(2)}, u32[]{:S(2)}) collective-permute-start(bf16[80,1536]{1,0:T(8,128)(2,1)S(1)} %shard_map.28.rest_0_), channel_id=1, source_target_pairs={{0,4},{1,5},{2,6},{3,7},{4,0},{5,1},{6,2},{7,3},{8,12},{9,13},{10,... | collective-permute-start | bytes 737288 | tf_op jit(solution)/shard_map/ppermute | solution.py:581
  11.4 11.6 %collective-permute-start.7 = (bf16[80,1536]{1,0:T(8,128)(2,1)S(1)}, bf16[80,1536]{1,0:T(8,128)(2,1)S(1)}, u32[]{:S(2)}, u32[]{:S(2)}) collective-permute-start(bf16[80,1536]{1,0:T(8,128)(2,1)S(1)} %shard_map.28.rest_0_), channel_id=1, source_target_pairs={{0,6},{1,7},{2,4},{3,5},{4,2},{5,3},{6,0},{7,1},{8,14},{9,15},{10,... | collective-permute-start | bytes 737288 | tf_op jit(solution)/shard_map/ppermute | solution.py:581
  23.0 5.9 %collective-permute-start.8 = (bf16[80,1536]{1,0:T(8,128)(2,1)S(1)}, bf16[80,1536]{1,0:T(8,128)(2,1)S(1)}, u32[]{:S(2)}, u32[]{:S(2)}) collective-permute-start(bf16[80,1536]{1,0:T(8,128)(2,1)S(1)} %shard_map.28.rest_0_), channel_id=1, source_target_pairs={{0,1},{1,0},{2,3},{3,2},{4,5},{5,4},{6,7},{7,6},{8,9},{9,8},{10,11... | collective-permute-start | bytes 737288 | tf_op jit(solution)/shard_map/ppermute | solution.py:581
  23.1 5.8 %collective-permute-start.9 = (bf16[80,1536]{1,0:T(8,128)(2,1)S(1)}, bf16[80,1536]{1,0:T(8,128)(2,1)S(1)}, u32[]{:S(2)}, u32[]{:S(2)}) collective-permute-start(bf16[80,1536]{1,0:T(8,128)(2,1)S(1)} %collective-permute-done.5.rest_2_), channel_id=1, source_target_pairs={{0,1},{1,0},{2,3},{3,2},{4,5},{5,4},{6,7},{7,6},{8,9},{9,8},{10,11... | collective-permute-start | bytes 737288 | tf_op jit(solution)/shard_map/ppermute | solution.py:581
  23.6 5.3 %collective-permute-start.10 = (bf16[80,1536]{1,0:T(8,128)(2,1)S(1)}, bf16[80,1536]{1,0:T(8,128)(2,1)S(1)}, u32[]{:S(2)}, u32[]{:S(2)}) collective-permute-start(bf16[80,1536]{1,0:T(8,128)(2,1)S(1)} %collective-permute-done.6.rest_4_), channel_id=1, source_target_pairs={{0,1},{1,0},{2,3},{3,2},{4,5},{5,4},{6,7},{7,6},{8,9},{9,8},{10,11... | collective-permute-start | bytes 737288 | tf_op jit(solution)/shard_map/ppermute | solution.py:581
  23.7 5.3 %collective-permute-start.11 = (bf16[80,1536]{1,0:T(8,128)(2,1)S(1)}, bf16[80,1536]{1,0:T(8,128)(2,1)S(1)}, u32[]{:S(2)}, u32[]{:S(2)}) collective-permute-start(bf16[80,1536]{1,0:T(8,128)(2,1)S(1)} %collective-permute-done.7.rest_6_), channel_id=1, source_target_pairs={{0,1},{1,0},{2,3},{3,2},{4,5},{5,4},{6,7},{7,6},{8,9},{9,8},{10,11... | collective-permute-start | bytes 737288 | tf_op jit(solution)/shard_map/ppermute | solution.py:581
  36.2 8.3 %collective-permute-start.12 = (bf16[272,320]{1,0:T(8,128)(2,1)S(1)}, bf16[272,320]{1,0:T(8,128)(2,1)S(1)}, u32[]{:S(2)}, u32[]{:S(2)}) collective-permute-start(bf16[272,320]{1,0:T(8,128)(2,1)S(1)} %get-tuple-element.94), channel_id=1, source_target_pairs={{0,7},{1,2},{2,1},{3,4},{4,3},{5,6},{6,5},{7,0},{8,15},{9,10},{10,... | collective-permute-start | bytes 522248 | tf_op jit(solution)/shard_map/ppermute | solution.py:581
  37.2 24.6 %collective-permute-start.17 = (bf16[80,1536]{1,0:T(8,128)(2,1)S(1)}, bf16[80,1536]{1,0:T(8,128)(2,1)S(1)}, u32[]{:S(2)}, u32[]{:S(2)}) collective-permute-start(bf16[80,1536]{1,0:T(8,128)(2,1)S(1)} %get-tuple-element.98.rest_3_.rest_8_), channel_id=1, source_target_pairs={{0,2},{1,3},{2,0},{3,1},{4,6},{5,7},{6,4},{7,5},{8,10},{9,11},{10,... | collective-permute-start | bytes 737288 | tf_op jit(solution)/shard_map/ppermute | solution.py:581
  38.3 23.6 %collective-permute-start.18 = (bf16[80,1536]{1,0:T(8,128)(2,1)S(1)}, bf16[80,1536]{1,0:T(8,128)(2,1)S(1)}, u32[]{:S(2)}, u32[]{:S(2)}) collective-permute-start(bf16[80,1536]{1,0:T(8,128)(2,1)S(1)} %get-tuple-element.98.rest_3_.rest_8_), channel_id=1, source_target_pairs={{0,4},{1,5},{2,6},{3,7},{4,0},{5,1},{6,2},{7,3},{8,12},{9,13},{10,... | collective-permute-start | bytes 737288 | tf_op jit(solution)/shard_map/ppermute | solution.py:581
  39.4 27.2 %collective-permute-start.24 = (bf16[80,3072]{1,0:T(8,128)(2,1)S(1)}, bf16[80,3072]{1,0:T(8,128)(2,1)S(1)}, u32[]{:S(2)}, u32[]{:S(2)}) collective-permute-start(bf16[80,3072]{1,0:T(8,128)(2,1)S(1)} %get-tuple-element.102.rest_0_.rest_16_), channel_id=1, source_target_pairs={{0,2},{1,3},{2,0},{3,1},{4,6},{5,7},{6,4},{7,5},{8,10},{9,11},{10,... | collective-permute-start | bytes 1474568 | tf_op jit(solution)/shard_map/ppermute | solution.py:581
  41.1 7.3 %collective-permute-start.14 = (f32[8,320]{1,0:T(8,128)S(1)}, f32[8,320]{1,0:T(8,128)S(1)}, u32[]{:S(2)}, u32[]{:S(2)}) collective-permute-start(f32[8,320]{1,0:T(8,128)S(1)} %get-tuple-element.93), channel_id=1, source_target_pairs={{0,4},{1,5},{2,6},{3,7},{4,0},{5,1},{6,2},{7,3},{8,12},{9,13},{10,... | collective-permute-start | bytes 30728 | tf_op jit(solution)/shard_map/ppermute | solution.py:581
  44.5 16.4 %collective-permute-start.13 = (f32[8,320]{1,0:T(8,128)S(1)}, f32[8,320]{1,0:T(8,128)S(1)}, u32[]{:S(2)}, u32[]{:S(2)}) collective-permute-start(f32[8,320]{1,0:T(8,128)S(1)} %get-tuple-element.93), channel_id=1, source_target_pairs={{0,2},{1,7},{2,4},{3,1},{4,6},{5,3},{6,0},{7,5},{8,10},{9,15},{10,... | collective-permute-start | bytes 30728 | tf_op jit(solution)/shard_map/ppermute | solution.py:581
  48.4 17.7 %collective-permute-start.19 = (bf16[80,1536]{1,0:T(8,128)(2,1)S(1)}, bf16[80,1536]{1,0:T(8,128)(2,1)S(1)}, u32[]{:S(2)}, u32[]{:S(2)}) collective-permute-start(bf16[80,1536]{1,0:T(8,128)(2,1)S(1)} %get-tuple-element.98.rest_3_.rest_8_), channel_id=1, source_target_pairs={{0,6},{1,7},{2,4},{3,5},{4,2},{5,3},{6,0},{7,1},{8,14},{9,15},{10,... | collective-permute-start | bytes 737288 | tf_op jit(solution)/shard_map/ppermute | solution.py:581
  60.9 15.6 %collective-permute-start.25 = (bf16[80,3072]{1,0:T(8,128)(2,1)S(1)}, bf16[80,3072]{1,0:T(8,128)(2,1)S(1)}, u32[]{:S(2)}, u32[]{:S(2)}) collective-permute-start(bf16[80,3072]{1,0:T(8,128)(2,1)S(1)} %get-tuple-element.102.rest_0_.rest_16_), channel_id=1, source_target_pairs={{0,4},{1,5},{2,6},{3,7},{4,0},{5,1},{6,2},{7,3},{8,12},{9,13},{10,... | collective-permute-start | bytes 1474568 | tf_op jit(solution)/shard_map/ppermute | solution.py:581
  66.1 14.2 %collective-permute-start.20 = (bf16[80,1536]{1,0:T(8,128)(2,1)S(1)}, bf16[80,1536]{1,0:T(8,128)(2,1)S(1)}, u32[]{:S(2)}, u32[]{:S(2)}) collective-permute-start(bf16[80,1536]{1,0:T(8,128)(2,1)S(1)} %get-tuple-element.98.rest_3_.rest_8_), channel_id=1, source_target_pairs={{0,1},{1,0},{2,3},{3,2},{4,5},{5,4},{6,7},{7,6},{8,9},{9,8},{10,11... | collective-permute-start | bytes 737288 | tf_op jit(solution)/shard_map/ppermute | solution.py:581
  66.1 15.0 %collective-permute-start.21 = (bf16[80,1536]{1,0:T(8,128)(2,1)S(1)}, bf16[80,1536]{1,0:T(8,128)(2,1)S(1)}, u32[]{:S(2)}, u32[]{:S(2)}) collective-permute-start(bf16[80,1536]{1,0:T(8,128)(2,1)S(1)} %collective-permute-done.17.rest_5_.rest_10_), channel_id=1, source_target_pairs={{0,1},{1,0},{2,3},{3,2},{4,5},{5,4},{6,7},{7,6},{8,9},{9,8},{10,11... | collective-permute-start | bytes 737288 | tf_op jit(solution)/shard_map/ppermute | solution.py:581
  66.6 14.5 %collective-permute-start.22 = (bf16[80,1536]{1,0:T(8,128)(2,1)S(1)}, bf16[80,1536]{1,0:T(8,128)(2,1)S(1)}, u32[]{:S(2)}, u32[]{:S(2)}) collective-permute-start(bf16[80,1536]{1,0:T(8,128)(2,1)S(1)} %collective-permute-done.18.rest_7_.rest_12_), channel_id=1, source_target_pairs={{0,1},{1,0},{2,3},{3,2},{4,5},{5,4},{6,7},{7,6},{8,9},{9,8},{10,11... | collective-permute-start | bytes 737288 | tf_op jit(solution)/shard_map/ppermute | solution.py:581
  66.6 15.0 %collective-permute-start.23 = (bf16[80,1536]{1,0:T(8,128)(2,1)S(1)}, bf16[80,1536]{1,0:T(8,128)(2,1)S(1)}, u32[]{:S(2)}, u32[]{:S(2)}) collective-permute-start(bf16[80,1536]{1,0:T(8,128)(2,1)S(1)} %collective-permute-done.19.rest_9_.rest_14_), channel_id=1, source_target_pairs={{0,1},{1,0},{2,3},{3,2},{4,5},{5,4},{6,7},{7,6},{8,9},{9,8},{10,11... | collective-permute-start | bytes 737288 | tf_op jit(solution)/shard_map/ppermute | solution.py:581
  79.1 10.2 %collective-permute-start.29 = (bf16[80,1536]{1,0:T(8,128)(2,1)S(1)}, bf16[80,1536]{1,0:T(8,128)(2,1)S(1)}, u32[]{:S(2)}, u32[]{:S(2)}) collective-permute-start(bf16[80,1536]{1,0:T(8,128)(2,1)S(1)} %slice.275), channel_id=1, source_target_pairs={{0,4},{1,5},{2,6},{3,7},{4,0},{5,1},{6,2},{7,3},{8,12},{9,13},{10,... | collective-permute-start | bytes 737288 | tf_op jit(solution)/shard_map/ppermute | solution.py:581
  80.2 9.1 %collective-permute-start.30 = (bf16[80,1536]{1,0:T(8,128)(2,1)S(1)}, bf16[80,1536]{1,0:T(8,128)(2,1)S(1)}, u32[]{:S(2)}, u32[]{:S(2)}) collective-permute-start(bf16[80,1536]{1,0:T(8,128)(2,1)S(1)} %slice.276), channel_id=1, source_target_pairs={{0,2},{1,3},{2,0},{3,1},{4,6},{5,7},{6,4},{7,5},{8,10},{9,11},{10,... | collective-permute-start | bytes 737288 | tf_op jit(solution)/shard_map/ppermute | solution.py:581
  81.0 10.2 %collective-permute-start.27 = (bf16[80,3072]{1,0:T(8,128)(2,1)S(1)}, bf16[80,3072]{1,0:T(8,128)(2,1)S(1)}, u32[]{:S(2)}, u32[]{:S(2)}) collective-permute-start(bf16[80,3072]{1,0:T(8,128)(2,1)S(1)} %collective-permute-done.24.rest_2_.rest_18_), channel_id=1, source_target_pairs={{0,1},{1,0},{2,3},{3,2},{4,5},{5,4},{6,7},{7,6},{8,9},{9,8},{10,11... | collective-permute-start | bytes 1474568 | tf_op jit(solution)/shard_map/ppermute | solution.py:581
  81.1 10.2 %collective-permute-start.26 = (bf16[80,3072]{1,0:T(8,128)(2,1)S(1)}, bf16[80,3072]{1,0:T(8,128)(2,1)S(1)}, u32[]{:S(2)}, u32[]{:S(2)}) collective-permute-start(bf16[80,3072]{1,0:T(8,128)(2,1)S(1)} %get-tuple-element.102.rest_0_.rest_16_), channel_id=1, source_target_pairs={{0,1},{1,0},{2,3},{3,2},{4,5},{5,4},{6,7},{7,6},{8,9},{9,8},{10,11... | collective-permute-start | bytes 1474568 | tf_op jit(solution)/shard_map/ppermute | solution.py:581
  81.6 9.7 %collective-permute-start.28 = (bf16[80,3072]{1,0:T(8,128)(2,1)S(1)}, bf16[80,3072]{1,0:T(8,128)(2,1)S(1)}, u32[]{:S(2)}, u32[]{:S(2)}) collective-permute-start(bf16[80,3072]{1,0:T(8,128)(2,1)S(1)} %collective-permute-done.25.rest_4_.rest_20_), channel_id=1, source_target_pairs={{0,1},{1,0},{2,3},{3,2},{4,5},{5,4},{6,7},{7,6},{8,9},{9,8},{10,11... | collective-permute-start | bytes 1474568 | tf_op jit(solution)/shard_map/ppermute | solution.py:581
  98.0 8.6 %collective-permute-start.33 = (bf16[144,640]{1,0:T(8,128)(2,1)S(1)}, bf16[144,640]{1,0:T(8,128)(2,1)S(1)}, u32[]{:S(2)}, u32[]{:S(2)}) collective-permute-start(bf16[144,640]{1,0:T(8,128)(2,1)S(1)} %get-tuple-element.109), channel_id=1, source_target_pairs={{0,8},{1,9},{2,10},{3,11},{4,12},{5,13},{6,14},{7,15},{8,16},{9,17... | collective-permute-start | bytes 552968 | tf_op jit(solution)/shard_map/ppermute | solution.py:577
  99.6 35.3 %collective-permute-start.45 = (bf16[80,6144]{1,0:T(8,128)(2,1)}, bf16[80,6144]{1,0:T(8,128)(2,1)S(1)}, u32[]{:S(2)}, u32[]{:S(2)}) collective-permute-start(bf16[80,6144]{1,0:T(8,128)(2,1)} %get-tuple-element.120.rest_1_.rest_0_), channel_id=1, source_target_pairs={{0,2},{1,3},{2,0},{3,1},{4,6},{5,7},{6,4},{7,5},{8,10},{9,11},{10,... | collective-permute-start | bytes 2949128 | tf_op jit(solution)/shard_map/ppermute | solution.py:581
  100.9 34.2 %collective-permute-start.46 = (bf16[80,6144]{1,0:T(8,128)(2,1)}, bf16[80,6144]{1,0:T(8,128)(2,1)S(1)}, u32[]{:S(2)}, u32[]{:S(2)}) collective-permute-start(bf16[80,6144]{1,0:T(8,128)(2,1)} %get-tuple-element.120.rest_1_.rest_0_), channel_id=1, source_target_pairs={{0,4},{1,5},{2,6},{3,7},{4,0},{5,1},{6,2},{7,3},{8,12},{9,13},{10,... | collective-permute-start | bytes 2949128 | tf_op jit(solution)/shard_map/ppermute | solution.py:581
  106.7 17.9 %collective-permute-start.34 = (bf16[80,640]{1,0:T(8,128)(2,1)S(1)}, bf16[80,640]{1,0:T(8,128)(2,1)S(1)}, u32[]{:S(2)}, u32[]{:S(2)}) collective-permute-start(bf16[80,640]{1,0:T(8,128)(2,1)S(1)} %pad_maximum_fusion), channel_id=1, source_target_pairs={{0,7},{1,2},{2,1},{3,4},{4,3},{5,6},{6,5},{7,0},{8,15},{9,10},{10,... | collective-permute-start | bytes 307208 | tf_op jit(solution)/shard_map/ppermute | solution.py:581
  107.4 18.7 %collective-permute-start.37 = (f32[8,640]{1,0:T(8,128)S(1)}, f32[8,640]{1,0:T(8,128)S(1)}, u32[]{:S(2)}, u32[]{:S(2)}) collective-permute-start(f32[8,640]{1,0:T(8,128)S(1)} %maximum_maximum_fusion), channel_id=1, source_target_pairs={{0,4},{1,5},{2,6},{3,7},{4,0},{5,1},{6,2},{7,3},{8,12},{9,13},{10,... | collective-permute-start | bytes 61448 | tf_op jit(solution)/shard_map/ppermute | solution.py:581
  108.5 17.6 %collective-permute-start.36 = (f32[8,640]{1,0:T(8,128)S(1)}, f32[8,640]{1,0:T(8,128)S(1)}, u32[]{:S(2)}, u32[]{:S(2)}) collective-permute-start(f32[8,640]{1,0:T(8,128)S(1)} %maximum_maximum_fusion), channel_id=1, source_target_pairs={{0,2},{1,7},{2,4},{3,1},{4,6},{5,3},{6,0},{7,5},{8,10},{9,15},{10,... | collective-permute-start | bytes 61448 | tf_op jit(solution)/shard_map/ppermute | solution.py:581
  133.4 16.8 %collective-permute-start.40 = (bf16[80,640]{1,0:T(8,128)(2,1)S(1)}, bf16[80,640]{1,0:T(8,128)(2,1)S(1)}, u32[]{:S(2)}, u32[]{:S(2)}) collective-permute-start(bf16[80,640]{1,0:T(8,128)(2,1)S(1)} %get-tuple-element.117), channel_id=1, source_target_pairs={{0,7},{1,2},{2,1},{3,4},{4,3},{5,6},{6,5},{7,0},{8,15},{9,10},{10,... | collective-permute-start | bytes 307208 | tf_op jit(solution)/shard_map/ppermute | solution.py:581
  135.1 16.6 %collective-permute-start.50 = (bf16[80,3072]{1,0:T(8,128)(2,1)S(1)}, bf16[80,3072]{1,0:T(8,128)(2,1)S(1)}, u32[]{:S(2)}, u32[]{:S(2)}) collective-permute-start(bf16[80,3072]{1,0:T(8,128)(2,1)S(1)} %slice.385), channel_id=1, source_target_pairs={{0,4},{1,5},{2,6},{3,7},{4,0},{5,1},{6,2},{7,3},{8,12},{9,13},{10,... | collective-permute-start | bytes 1474568 | tf_op jit(solution)/shard_map/ppermute | solution.py:581
  136.1 13.6 %collective-permute-start.43 = (f32[8,640]{1,0:T(8,128)S(1)}, f32[8,640]{1,0:T(8,128)S(1)}, u32[]{:S(2)}, u32[]{:S(2)}) collective-permute-start(f32[8,640]{1,0:T(8,128)S(1)} %get-tuple-element.119), channel_id=1, source_target_pairs={{0,4},{1,5},{2,6},{3,7},{4,0},{5,1},{6,2},{7,3},{8,12},{9,13},{10,... | collective-permute-start | bytes 61448 | tf_op jit(solution)/shard_map/ppermute | solution.py:581
  137.2 12.5 %collective-permute-start.42 = (f32[8,640]{1,0:T(8,128)S(1)}, f32[8,640]{1,0:T(8,128)S(1)}, u32[]{:S(2)}, u32[]{:S(2)}) collective-permute-start(f32[8,640]{1,0:T(8,128)S(1)} %get-tuple-element.119), channel_id=1, source_target_pairs={{0,2},{1,7},{2,4},{3,1},{4,6},{5,3},{6,0},{7,5},{8,10},{9,15},{10,... | collective-permute-start | bytes 61448 | tf_op jit(solution)/shard_map/ppermute | solution.py:581
  137.5 27.3 %collective-permute-start.47 = (bf16[80,6144]{1,0:T(8,128)(2,1)}, bf16[80,6144]{1,0:T(8,128)(2,1)S(1)}, u32[]{:S(2)}, u32[]{:S(2)}) collective-permute-start(bf16[80,6144]{1,0:T(8,128)(2,1)} %get-tuple-element.120.rest_1_.rest_0_), channel_id=1, source_target_pairs={{0,1},{1,0},{2,3},{3,2},{4,5},{5,4},{6,7},{7,6},{8,9},{9,8},{10,11... | collective-permute-start | bytes 2949128 | tf_op jit(solution)/shard_map/ppermute | solution.py:581
  149.7 15.1 %collective-permute-start.48 = (bf16[80,6144]{1,0:T(8,128)(2,1)S(1)}, bf16[80,6144]{1,0:T(8,128)(2,1)S(1)}, u32[]{:S(2)}, u32[]{:S(2)}) collective-permute-start(bf16[80,6144]{1,0:T(8,128)(2,1)S(1)} %collective-permute-done.45.rest_3_.rest_2_), channel_id=1, source_target_pairs={{0,1},{1,0},{2,3},{3,2},{4,5},{5,4},{6,7},{7,6},{8,9},{9,8},{10,11... | collective-permute-start | bytes 2949128 | tf_op jit(solution)/shard_map/ppermute | solution.py:581
  149.7 15.1 %collective-permute-start.49 = (bf16[80,6144]{1,0:T(8,128)(2,1)S(1)}, bf16[80,6144]{1,0:T(8,128)(2,1)S(1)}, u32[]{:S(2)}, u32[]{:S(2)}) collective-permute-start(bf16[80,6144]{1,0:T(8,128)(2,1)S(1)} %collective-permute-done.46.rest_5_.rest_4_), channel_id=1, source_target_pairs={{0,1},{1,0},{2,3},{3,2},{4,5},{5,4},{6,7},{7,6},{8,9},{9,8},{10,11... | collective-permute-start | bytes 2949128 | tf_op jit(solution)/shard_map/ppermute | solution.py:581
  150.2 13.2 %collective-permute-start.51 = (bf16[80,3072]{1,0:T(8,128)(2,1)S(1)}, bf16[80,3072]{1,0:T(8,128)(2,1)S(1)}, u32[]{:S(2)}, u32[]{:S(2)}) collective-permute-start(bf16[80,3072]{1,0:T(8,128)(2,1)S(1)} %slice.386), channel_id=1, source_target_pairs={{0,2},{1,3},{2,0},{3,1},{4,6},{5,7},{6,4},{7,5},{8,10},{9,11},{10,... | collective-permute-start | bytes 1474568 | tf_op jit(solution)/shard_map/ppermute | solution.py:581
  151.7 11.7 %collective-permute-start.41 = (bf16[64,640]{1,0:T(8,128)(2,1)S(1)}, bf16[64,640]{1,0:T(8,128)(2,1)S(1)}, u32[]{:S(2)}, u32[]{:S(2)}) collective-permute-start(bf16[64,640]{1,0:T(8,128)(2,1)S(1)} %get-tuple-element.118), channel_id=1, source_target_pairs={{0,1},{1,0},{2,3},{3,2},{4,5},{5,4},{6,7},{7,6},{8,9},{9,8},{10,11... | collective-permute-start | bytes 245768 | tf_op jit(solution)/shard_map/ppermute | solution.py:581
  174.4 9.4 %collective-permute-start.54 = (bf16[144,640]{1,0:T(8,128)(2,1)S(1)}, bf16[144,640]{1,0:T(8,128)(2,1)S(1)}, u32[]{:S(2)}, u32[]{:S(2)}) collective-permute-start(bf16[144,640]{1,0:T(8,128)(2,1)S(1)} %get-tuple-element.127), channel_id=1, source_target_pairs={{0,8},{1,9},{2,10},{3,11},{4,12},{5,13},{6,14},{7,15},{8,16},{9,17... | collective-permute-start | bytes 552968 | tf_op jit(solution)/shard_map/ppermute | solution.py:577
  176.1 19.1 %collective-permute-start.39 = (bf16[768,384]{1,0:T(8,128)(2,1)S(1)}, bf16[768,384]{1,0:T(8,128)(2,1)S(1)}, u32[]{:S(2)}, u32[]{:S(2)}) collective-permute-start(bf16[768,384]{1,0:T(8,128)(2,1)S(1)} %copy-done.41), channel_id=1, source_target_pairs={{0,24},{1,25},{2,26},{3,27},{4,28},{5,29},{6,30},{7,31},{8,0},{9,1... | collective-permute-start | bytes 1769480 | tf_op jit(solution)/shard_map/ppermute | solution.py:577
  183.9 5.7 %collective-permute-start.55 = (bf16[80,640]{1,0:T(8,128)(2,1)S(1)}, bf16[80,640]{1,0:T(8,128)(2,1)S(1)}, u32[]{:S(2)}, u32[]{:S(2)}) collective-permute-start(bf16[80,640]{1,0:T(8,128)(2,1)S(1)} %pad_maximum_fusion.1), channel_id=1, source_target_pairs={{0,7},{1,2},{2,1},{3,4},{4,3},{5,6},{6,5},{7,0},{8,15},{9,10},{10,... | collective-permute-start | bytes 307208 | tf_op jit(solution)/shard_map/ppermute | solution.py:581
  184.1 5.6 %collective-permute-start.58 = (f32[8,640]{1,0:T(8,128)S(1)}, f32[8,640]{1,0:T(8,128)S(1)}, u32[]{:S(2)}, u32[]{:S(2)}) collective-permute-start(f32[8,640]{1,0:T(8,128)S(1)} %maximum_maximum_fusion.1), channel_id=1, source_target_pairs={{0,4},{1,5},{2,6},{3,7},{4,0},{5,1},{6,2},{7,3},{8,12},{9,13},{10,... | collective-permute-start | bytes 61448 | tf_op jit(solution)/shard_map/ppermute | solution.py:581
  185.4 4.7 %collective-permute-start.57 = (f32[8,640]{1,0:T(8,128)S(1)}, f32[8,640]{1,0:T(8,128)S(1)}, u32[]{:S(2)}, u32[]{:S(2)}) collective-permute-start(f32[8,640]{1,0:T(8,128)S(1)} %maximum_maximum_fusion.1), channel_id=1, source_target_pairs={{0,2},{1,7},{2,4},{3,1},{4,6},{5,3},{6,0},{7,5},{8,10},{9,15},{10,... | collective-permute-start | bytes 61448 | tf_op jit(solution)/shard_map/ppermute | solution.py:581
  186.6 8.6 %collective-permute-start.56 = (bf16[64,640]{1,0:T(8,128)(2,1)S(1)}, bf16[64,640]{1,0:T(8,128)(2,1)S(1)}, u32[]{:S(2)}, u32[]{:S(2)}) collective-permute-start(bf16[64,640]{1,0:T(8,128)(2,1)S(1)} %get-tuple-element.155), channel_id=1, source_target_pairs={{0,1},{1,0},{2,3},{3,2},{4,5},{5,4},{6,7},{7,6},{8,9},{9,8},{10,11... | collective-permute-start | bytes 245768 | tf_op jit(solution)/shard_map/ppermute | solution.py:581
  190.1 5.0 %collective-permute-start.59 = (f32[8,640]{1,0:T(8,128)S(1)}, f32[8,640]{1,0:T(8,128)S(1)}, u32[]{:S(2)}, u32[]{:S(2)}) collective-permute-start(f32[8,640]{1,0:T(8,128)S(1)} %fusion.5.sa), channel_id=1, source_target_pairs={{0,1},{1,0},{2,3},{3,2},{4,5},{5,4},{6,7},{7,6},{8,9},{9,8},{10,11... | collective-permute-start | bytes 61448 | tf_op jit(solution)/shard_map/ppermute | solution.py:581
  201.2 5.7 %collective-permute-start.60 = (bf16[80,640]{1,0:T(8,128)(2,1)S(1)}, bf16[80,640]{1,0:T(8,128)(2,1)S(1)}, u32[]{:S(2)}, u32[]{:S(2)}) collective-permute-start(bf16[80,640]{1,0:T(8,128)(2,1)S(1)} %get-tuple-element.134), channel_id=1, source_target_pairs={{0,7},{1,2},{2,1},{3,4},{4,3},{5,6},{6,5},{7,0},{8,15},{9,10},{10,... | collective-permute-start | bytes 307208 | tf_op jit(solution)/shard_map/ppermute | solution.py:581
  202.3 4.7 %collective-permute-start.63 = (f32[8,640]{1,0:T(8,128)S(1)}, f32[8,640]{1,0:T(8,128)S(1)}, u32[]{:S(2)}, u32[]{:S(2)}) collective-permute-start(f32[8,640]{1,0:T(8,128)S(1)} %get-tuple-element.136), channel_id=1, source_target_pairs={{0,4},{1,5},{2,6},{3,7},{4,0},{5,1},{6,2},{7,3},{8,12},{9,13},{10,... | collective-permute-start | bytes 61448 | tf_op jit(solution)/shard_map/ppermute | solution.py:581
  203.4 4.7 %collective-permute-start.62 = (f32[8,640]{1,0:T(8,128)S(1)}, f32[8,640]{1,0:T(8,128)S(1)}, u32[]{:S(2)}, u32[]{:S(2)}) collective-permute-start(f32[8,640]{1,0:T(8,128)S(1)} %get-tuple-element.136), channel_id=1, source_target_pairs={{0,2},{1,7},{2,4},{3,1},{4,6},{5,3},{6,0},{7,5},{8,10},{9,15},{10,... | collective-permute-start | bytes 61448 | tf_op jit(solution)/shard_map/ppermute | solution.py:581
  203.9 4.3 %collective-permute-start.61 = (bf16[64,640]{1,0:T(8,128)(2,1)S(1)}, bf16[64,640]{1,0:T(8,128)(2,1)S(1)}, u32[]{:S(2)}, u32[]{:S(2)}) collective-permute-start(bf16[64,640]{1,0:T(8,128)(2,1)S(1)} %get-tuple-element.135), channel_id=1, source_target_pairs={{0,1},{1,0},{2,3},{3,2},{4,5},{5,4},{6,7},{7,6},{8,9},{9,8},{10,11... | collective-permute-start | bytes 245768 | tf_op jit(solution)/shard_map/ppermute | solution.py:581
  216.5 8.8 %collective-permute-start.65 = (bf16[144,640]{1,0:T(8,128)(2,1)S(1)}, bf16[144,640]{1,0:T(8,128)(2,1)S(1)}, u32[]{:S(2)}, u32[]{:S(2)}) collective-permute-start(bf16[144,640]{1,0:T(8,128)(2,1)S(1)} %get-tuple-element.137), channel_id=1, source_target_pairs={{0,8},{1,9},{2,10},{3,11},{4,12},{5,13},{6,14},{7,15},{8,16},{9,17... | collective-permute-start | bytes 552968 | tf_op jit(solution)/shard_map/ppermute | solution.py:577
  225.3 5.1 %collective-permute-start.66 = (bf16[80,640]{1,0:T(8,128)(2,1)S(1)}, bf16[80,640]{1,0:T(8,128)(2,1)S(1)}, u32[]{:S(2)}, u32[]{:S(2)}) collective-permute-start(bf16[80,640]{1,0:T(8,128)(2,1)S(1)} %pad_maximum_fusion.2), channel_id=1, source_target_pairs={{0,7},{1,2},{2,1},{3,4},{4,3},{5,6},{6,5},{7,0},{8,15},{9,10},{10,... | collective-permute-start | bytes 307208 | tf_op jit(solution)/shard_map/ppermute | solution.py:581
  238.2 5.2 %collective-permute-start.68 = (bf16[144,320]{1,0:T(8,128)(2,1)S(1)}, bf16[144,320]{1,0:T(8,128)(2,1)S(1)}, u32[]{:S(2)}, u32[]{:S(2)}) collective-permute-start(bf16[144,320]{1,0:T(8,128)(2,1)S(1)} %get-tuple-element.140), channel_id=1, source_target_pairs={{0,7},{1,2},{2,1},{3,4},{4,3},{5,6},{6,5},{7,0},{8,15},{9,10},{10,... | collective-permute-start | bytes 276488 | tf_op jit(solution)/shard_map/ppermute | solution.py:581
  239.1 4.4 %collective-permute-start.71 = (f32[8,320]{1,0:T(8,128)S(1)}, f32[8,320]{1,0:T(8,128)S(1)}, u32[]{:S(2)}, u32[]{:S(2)}) collective-permute-start(f32[8,320]{1,0:T(8,128)S(1)} %get-tuple-element.142), channel_id=1, source_target_pairs={{0,4},{1,5},{2,6},{3,7},{4,0},{5,1},{6,2},{7,3},{8,12},{9,13},{10,... | collective-permute-start | bytes 30728 | tf_op jit(solution)/shard_map/ppermute | solution.py:581
  240.2 4.6 %collective-permute-start.70 = (f32[8,320]{1,0:T(8,128)S(1)}, f32[8,320]{1,0:T(8,128)S(1)}, u32[]{:S(2)}, u32[]{:S(2)}) collective-permute-start(f32[8,320]{1,0:T(8,128)S(1)} %get-tuple-element.142), channel_id=1, source_target_pairs={{0,2},{1,7},{2,4},{3,1},{4,6},{5,3},{6,0},{7,5},{8,10},{9,15},{10,... | collective-permute-start | bytes 30728 | tf_op jit(solution)/shard_map/ppermute | solution.py:581
  240.2 4.6 %collective-permute-start.69 = (bf16[128,320]{1,0:T(8,128)(2,1)S(1)}, bf16[128,320]{1,0:T(8,128)(2,1)S(1)}, u32[]{:S(2)}, u32[]{:S(2)}) collective-permute-start(bf16[128,320]{1,0:T(8,128)(2,1)S(1)} %get-tuple-element.141), channel_id=1, source_target_pairs={{0,1},{1,0},{2,3},{3,2},{4,5},{5,4},{6,7},{7,6},{8,9},{9,8},{10,11... | collective-permute-start | bytes 245768 | tf_op jit(solution)/shard_map/ppermute | solution.py:581
  254.4 6.3 %collective-permute-start.73 = (bf16[144,320]{1,0:T(8,128)(2,1)S(1)}, bf16[144,320]{1,0:T(8,128)(2,1)S(1)}, u32[]{:S(2)}, u32[]{:S(2)}) collective-permute-start(bf16[144,320]{1,0:T(8,128)(2,1)S(1)} %get-tuple-element.144), channel_id=1, source_target_pairs={{0,7},{1,2},{2,1},{3,4},{4,3},{5,6},{6,5},{7,0},{8,15},{9,10},{10,... | collective-permute-start | bytes 276488 | tf_op jit(solution)/shard_map/ppermute | solution.py:581
  254.9 5.8 %collective-permute-start.76 = (f32[8,320]{1,0:T(8,128)S(1)}, f32[8,320]{1,0:T(8,128)S(1)}, u32[]{:S(2)}, u32[]{:S(2)}) collective-permute-start(f32[8,320]{1,0:T(8,128)S(1)} %get-tuple-element.146), channel_id=1, source_target_pairs={{0,4},{1,5},{2,6},{3,7},{4,0},{5,1},{6,2},{7,3},{8,12},{9,13},{10,... | collective-permute-start | bytes 30728 | tf_op jit(solution)/shard_map/ppermute | solution.py:581
  255.9 4.9 %collective-permute-start.75 = (f32[8,320]{1,0:T(8,128)S(1)}, f32[8,320]{1,0:T(8,128)S(1)}, u32[]{:S(2)}, u32[]{:S(2)}) collective-permute-start(f32[8,320]{1,0:T(8,128)S(1)} %get-tuple-element.146), channel_id=1, source_target_pairs={{0,2},{1,7},{2,4},{3,1},{4,6},{5,3},{6,0},{7,5},{8,10},{9,15},{10,... | collective-permute-start | bytes 30728 | tf_op jit(solution)/shard_map/ppermute | solution.py:581
  257.3 3.6 %collective-permute-start.74 = (bf16[128,320]{1,0:T(8,128)(2,1)S(1)}, bf16[128,320]{1,0:T(8,128)(2,1)S(1)}, u32[]{:S(2)}, u32[]{:S(2)}) collective-permute-start(bf16[128,320]{1,0:T(8,128)(2,1)S(1)} %get-tuple-element.145), channel_id=1, source_target_pairs={{0,1},{1,0},{2,3},{3,2},{4,5},{5,4},{6,7},{7,6},{8,9},{9,8},{10,11... | collective-permute-start | bytes 245768 | tf_op jit(solution)/shard_map/ppermute | solution.py:581
  270.5 15.8 %collective-permute-start.80 = (bf16[8,16,320]{2,1,0:T(8,128)(2,1)S(1)}, bf16[8,16,320]{2,1,0:T(8,128)(2,1)S(1)}, u32[]{:S(2)}, u32[]{:S(2)}) collective-permute-start(bf16[8,16,320]{2,1,0:T(8,128)(2,1)S(1)} %get-tuple-element.149), channel_id=1, source_target_pairs={{24,0},{25,1},{26,2},{27,3},{28,4},{29,5},{30,6},{31,7}} | collective-permute-start | bytes 245768 | tf_op jit(solution)/shard_map/ppermute | solution.py:723
  (59 other events, 518.7 us)
